TPU v7x, 256 devices: a whole 4x4x8 slice. The times are simulated.
256 devices in a mesh: gx: 32 (over z_hi, x, core), gy: 8 (over z_lo, y).
Axes of the slice: x: 4, y: 4, z: 8 (z_hi: 4, z_lo: 2; z = z_hi * 2 + z_lo), core: 2. Of those that a mesh axis runs over, the one named last changes fastest.
Arguments:
- checkpoint: float32 [19, 256, 2048], P(None, 'gx', 'gy'), as said below
- cotangent: float32 [19, 256, 2048], P(None, 'gx', 'gy'), may hold values from -6 to 6
- blade_area: float32 [1536], replicated, may hold values from 0.5 to 2
- hub_tile: int32 [16], replicated, may hold values from 0 to 255
- point_side: int32 [1536], replicated, may hold values from 0 to 8
- point_local: int32 [1536], replicated, may hold values from 0 to 2047
Outputs:
- grad_checkpoint: float32 [19, 256, 2048], P(None, 'gx', 'gy')
- grad_area: float32 [1536], replicated
Inputs may be any that keep to these rules, and one draw needn't show every extreme that they name: `hub_tile`: tile ids count every tile of the slab. `point_side`: every actuator point lies in its hub tile or one of the eight tiles around it. `checkpoint`: populations are positive and near a local equilibrium with density near one and streamwise velocity near 0.08.
All inputs are finite; a program needn't handle non-finite values.
Results may differ from a plain program's by a relative error of at most 0.0003.
Values sent between devices are 32-bit elements; how exact they have to be, the bound alone decides.
No kernel may reach another device: no remote copies, remote signals or barrier semaphores. Data moves between devices by JAX's collectives and lax.ppermute only.
A program may use at most 128 MiB of HBM per device.

v0:
```python
import functools

import jax
import jax.numpy as jnp
import numpy as np
from jax import lax
from jax.experimental import pallas as pl
from jax.experimental.pallas import tpu as pltpu
from jax.sharding import PartitionSpec as P

NZ = 16
CX = 8
CY = 16
STEPS = 4
NTURB = 16
PTS = 96
MARGIN = 8
RX = CX + 2 * MARGIN
RY = CY + 2 * MARGIN
LANES = RY * NZ
OWN_ROWS = slice(MARGIN, MARGIN + CX)
OWN_LANE = MARGIN * NZ
OWN_SPAN = CY * NZ

TAU_ZERO = 0.52
SMAGORINSKY = 0.17 * 0.17
TINY = 1e-10
THRUST = 4.0
GHOST_RATES = np.array([1.05, 1.15, 1.25, 1.35, 1.45, 1.55, 1.65, 1.75, 1.85])
W_REST, W_AXIS, W_EDGE = 1.0 / 3.0, 1.0 / 18.0, 1.0 / 36.0

VECTORS = np.array(
    [(0, 0, 0), (1, 0, 0), (-1, 0, 0), (0, 1, 0), (0, -1, 0), (0, 0, 1), (0, 0, -1)]
    + [(1, 1, 0), (-1, -1, 0), (1, -1, 0), (-1, 1, 0), (1, 0, 1), (-1, 0, -1)]
    + [(1, 0, -1), (-1, 0, 1), (0, 1, 1), (0, -1, -1), (0, 1, -1), (0, -1, 1)]
)
OPPOSITE = [0] + [i + 1 if i % 2 else i - 1 for i in range(1, 19)]


def basis():
    c = VECTORS * 1.0
    weights = np.array([W_REST] + [W_AXIS] * 6 + [W_EDGE] * 12)
    x, y, z = c[:, 0], c[:, 1], c[:, 2]
    monomials = [np.ones(19), x, y, z, x * x, y * y, z * z, x * y, x * z, y * z]
    monomials += [x * y * y, x * z * z, y * x * x, y * z * z, z * x * x, z * y * y]
    monomials += [x * x * y * y, x * x * z * z, y * y * z * z]
    rows = []
    for entry in monomials:
        vector = entry * 1.0
        for sweep in range(2):
            for other in rows:
                vector = vector - np.sum(weights * vector * other) * other
        rows.append(vector / np.sqrt(np.sum(weights * vector * vector)))
    return np.stack(rows, 0)


def ghost_tables():
    rows = basis()
    odd = []
    for first, members in ((10, (1, 7, 11)), (12, (3, 7, 15)), (14, (5, 11, 15))):
        h = rows[first : first + 2][:, list(members)]
        rates = GHOST_RATES[first - 10 : first - 8]
        odd.append(np.diag([W_AXIS, W_EDGE, W_EDGE]) @ h.T @ np.diag(rates) @ h)
    even = rows[16:19][:, [0, 1, 3, 5, 7, 11, 15]]
    return odd, even, GHOST_RATES[6:9]


ODD, EVEN, EVEN_RATES = ghost_tables()
CLASS_W = [W_REST] + [W_AXIS] * 3 + [W_EDGE] * 3


def combine(coefs, values):
    total = None
    for coef, value in zip(coefs, values):
        coef = float(coef)
        if abs(coef) < 1e-12:
            continue
        term = value if coef == 1.0 else value * coef
        total = term if total is None else total + term
    return total


def split_parity(s):
    e = [s[i] + s[i + 1] for i in range(1, 19, 2)]
    o = [s[i] - s[i + 1] for i in range(1, 19, 2)]
    even = [s[0], e[0], e[1], e[2], e[3] + e[4], e[5] + e[6], e[7] + e[8]]
    cross = [e[3] - e[4], e[5] - e[6], e[7] - e[8]]
    odd_x = [o[0], o[3] + o[4], o[5] + o[6]]
    odd_y = [o[1], o[3] - o[4], o[7] + o[8]]
    odd_z = [o[2], o[5] - o[6], o[7] - o[8]]
    return even, cross, odd_x, odd_y, odd_z


def merge_parity(s, even, cross, odd_x, odd_y, odd_z):
    out = [s[0] + even[0]]
    for axis, odd in enumerate((odd_x, odd_y, odd_z)):
        out += [s[1 + 2 * axis] + (even[1 + axis] + odd[0])]
        out += [s[2 + 2 * axis] + (even[1 + axis] - odd[0])]
    pairs = ((odd_x[1], odd_y[1]), (odd_x[2], odd_z[1]), (odd_y[2], odd_z[2]))
    for family in range(3):
        first, second = pairs[family]
        base = 7 + 4 * family
        for sign, offset in ((1, 0), (-1, 2)):
            level = even[4 + family] + cross[family] if sign > 0 else even[4 + family] - cross[family]
            swing = first + second if sign > 0 else first - second
            out += [s[base + offset] + (level + swing), s[base + offset + 1] + (level - swing)]
    return out


def ghost_even(even, transpose):
    if transpose:
        even = [value * w for value, w in zip(even, CLASS_W)]
    m = [combine(EVEN[k], even) * float(EVEN_RATES[k]) for k in range(3)]
    out = [combine(EVEN[:, j], m) for j in range(7)]
    if not transpose:
        out = [value * w for value, w in zip(out, CLASS_W)]
    return out


def ghost_odd(index, odd, transpose):
    matrix = ODD[index].T if transpose else ODD[index]
    return [combine(matrix[j], odd) for j in range(3)]


def local_state(even, cross, odds):
    rho = ((even[0] + even[1]) + (even[2] + even[3])) + ((even[4] + even[5]) + even[6])
    inverse = 1.0 / rho
    mom = [(odd[0] + odd[1]) + odd[2] for odd in odds]
    u = [m * inverse for m in mom]
    third = rho * (1.0 / 3.0)
    edges = ((even[4], even[5]), (even[4], even[6]), (even[5], even[6]))
    stress = [
        ((even[1 + a] + edges[a][0]) + edges[a][1]) - third - mom[a] * u[a] for a in range(3)
    ]
    stress += [cross[0] - mom[0] * u[1], cross[1] - mom[0] * u[2], cross[2] - mom[1] * u[2]]
    square = stress[0] * stress[0] + stress[1] * stress[1] + stress[2] * stress[2]
    square = square + 2.0 * (
        stress[3] * stress[3] + stress[4] * stress[4] + stress[5] * stress[5]
    )
    norm = jnp.sqrt(square + TINY)
    root = jnp.sqrt(TAU_ZERO * TAU_ZERO + (18.0 * SMAGORINSKY) * norm * inverse)
    tau = 0.5 * (TAU_ZERO + root)
    return inverse, u, stress, norm, root, tau


def collide(s, force):
    even, cross, odd_x, odd_y, odd_z = split_parity(s)
    inverse, u, stress, norm, root, tau = local_state(even, cross, (odd_x, odd_y, odd_z))
    scale = 4.5 / tau
    k = [value * scale for value in stress]
    trace = (k[0] + k[1] + k[2]) * (1.0 / 3.0)
    relax = [-trace, k[0] - trace, k[1] - trace, k[2] - trace]
    relax += [k[0] + relax[2], k[0] + relax[3], k[1] + relax[3]]
    ghost = ghost_even(even, False)
    even_out = [-(relax[j] * CLASS_W[j] + ghost[j]) for j in range(7)]
    cross_out = [k[3 + j] * (-2.0 * W_EDGE) for j in range(3)]
    gx = ghost_odd(0, odd_x, False)
    ox = [force * (1.0 / 6.0) - gx[0], force * (1.0 / 12.0) - gx[1], force * (1.0 / 12.0) - gx[2]]
    oy = [-value for value in ghost_odd(1, odd_y, False)]
    oz = [-value for value in ghost_odd(2, odd_z, False)]
    return merge_parity(s, even_out, cross_out, ox, oy, oz)


def collide_adjoint(s, a, speed_bar):
    even, cross, odd_x, odd_y, odd_z = split_parity(s)
    inverse, u, stress, norm, root, tau = local_state(even, cross, (odd_x, odd_y, odd_z))
    ev, cr, ax, ay, az = split_parity(a)
    weighted = [value * w for value, w in zip(ev, CLASS_W)]
    total = ((weighted[0] + weighted[1]) + (weighted[2] + weighted[3])) + (
        (weighted[4] + weighted[5]) + weighted[6]
    )
    third = total * (1.0 / 3.0)
    edges = ((4, 5), (4, 6), (5, 6))
    beta = [
        (weighted[1 + i] + weighted[edges[i][0]] + weighted[edges[i][1]] - third) * -4.5
        for i in range(3)
    ]
    beta += [value * (-9.0 * W_EDGE) for value in cr]
    inv_tau = 1.0 / tau
    dot = (beta[0] * stress[0] + beta[1] * stress[1] + beta[2] * stress[2]) + (
        beta[3] * stress[3] + beta[4] * stress[4] + beta[5] * stress[5]
    )
    tau_bar = -dot * inv_tau * inv_tau
    common = tau_bar * (4.5 * SMAGORINSKY) * inverse / root
    factor = common / norm
    p_bar = [beta[i] * inv_tau + stress[i] * factor for i in range(3)]
    twice = factor + factor
    p_bar += [beta[i] * inv_tau + stress[i] * twice for i in range(3, 6)]
    sp = speed_bar * inverse
    px, py, pz, pxy, pxz, pyz = p_bar
    tx = pxy * u[1] + pxz * u[2]
    ty = pyz * u[2]
    mx = sp - (2.0 * px * u[0] + tx)
    my = -(2.0 * py * u[1] + pxy * u[0] + ty)
    mz = -(2.0 * pz * u[2] + pxz * u[0] + pyz * u[1])
    rho_bar = -common * norm * inverse - (px + py + pz) * (1.0 / 3.0)
    rho_bar = rho_bar + (px * u[0] + tx) * u[0] + (py * u[1] + ty) * u[1] + pz * u[2] * u[2]
    rho_bar = rho_bar - sp * u[0]
    ghost = ghost_even(ev, True)
    level = [rho_bar, rho_bar + px, rho_bar + py, rho_bar + pz]
    level += [level[1] + py, level[1] + pz, level[2] + pz]
    even_out = [level[j] - ghost[j] for j in range(7)]
    gx, gy, gz = (ghost_odd(i, odd, True) for i, odd in enumerate((ax, ay, az)))
    ox = [mx - value for value in gx]
    oy = [my - value for value in gy]
    oz = [mz - value for value in gz]
    return merge_parity(a, even_out, p_bar[3:], ox, oy, oz)


def chunks(body):
    def step(index, carry):
        lane = pl.multiple_of(index * 128, 128)
        for row in range(0, RX, 8):
            body(pl.ds(row, 8), pl.ds(lane, 128))
        return carry

    lax.fori_loop(0, LANES // 128, step, 0)


def shifted(value, cx, cy, cz):
    lane = (NZ * cy + cz) % LANES
    if lane:
        value = pltpu.roll(value, lane, 1)
    if cx % RX:
        value = pltpu.roll(value, cx % RX, 0)
    return value


def height():
    return lax.broadcasted_iota(jnp.int32, (RX, LANES), 1) & (NZ - 1)


def stream(field, out):
    z = height()
    for i in range(19):
        cx, cy, cz = (int(v) for v in VECTORS[i])
        value = shifted(field[i], cx, cy, cz)
        if cz:
            value = jnp.where(z == (0 if cz > 0 else NZ - 1), field[OPPOSITE[i]], value)
        out[i] = value


def stream_adjoint(field, out):
    z = height()
    for i in range(19):
        cx, cy, cz = (int(v) for v in VECTORS[i])
        value = field[i]
        if cz:
            value = jnp.where(z == (0 if cz > 0 else NZ - 1), 0.0, value)
        value = shifted(value, -cx, -cy, -cz)
        if cz:
            value = value + jnp.where(z == (NZ - 1 if cz > 0 else 0), field[OPPOSITE[i]], 0.0)
        out[i] = value


def speeds(s_ref, v_ref):
    def one(rows, lanes):
        s = [s_ref[i, rows, lanes] for i in range(19)]
        even, cross, odd_x, odd_y, odd_z = split_parity(s)
        rho = ((even[0] + even[1]) + (even[2] + even[3])) + ((even[4] + even[5]) + even[6])
        v_ref[rows, lanes] = ((odd_x[0] + odd_x[1]) + odd_x[2]) / rho

    chunks(one)


def push_back(a):
    odd = (a[7] - a[8]) + (a[9] - a[10]) + (a[11] - a[12]) + (a[13] - a[14])
    return (a[1] - a[2]) * (1.0 / 6.0) + odd * (1.0 / 12.0)


def turbine_sums(area_ref, field_ref, sums_ref, out_ref, base):
    parts = [field_ref[OWN_ROWS, OWN_LANE + j : OWN_LANE + j + 128] for j in range(0, OWN_SPAN, 128)]
    for t in range(NTURB):
        total = None
        for j, part in enumerate(parts):
            lane = OWN_LANE + 128 * j
            term = area_ref[t, OWN_ROWS, lane : lane + 128] * part
            total = term if total is None else total + term
        sums_ref[t : t + 1, :] = jnp.sum(total, axis=0, keepdims=True)
    row = jnp.sum(sums_ref[...], axis=1, keepdims=True)
    out_ref[base : base + NTURB, :] = jnp.broadcast_to(row, (NTURB, 128))


def weighted_area(area_ref, weight_ref, rows, lanes):
    total = None
    for t in range(NTURB):
        term = area_ref[t, rows, lanes] * weight_ref[t : t + 1, :]
        total = term if total is None else total + term
    return total


def split_three(value):
    high = value.astype(jnp.bfloat16)
    rest = value - high.astype(jnp.float32)
    middle = rest.astype(jnp.bfloat16)
    return high, middle, (rest - middle.astype(jnp.float32)).astype(jnp.bfloat16)


def area_kernel(x_ref, yz_ref, area_ref, out_ref):
    rows = lax.broadcasted_iota(jnp.int32, (RX, PTS), 0)
    columns = lax.broadcasted_iota(jnp.int32, (LANES, PTS), 0)

    def one(t, carry):
        point = pl.ds(t, 1)
        spots = jnp.where(rows == x_ref[point, :], area_ref[point, :], 0.0)
        left = jnp.concatenate(split_three(spots), axis=0)
        hot = jnp.where(columns == yz_ref[point, :], 1.0, 0.0).astype(jnp.bfloat16)
        product = lax.dot_general(
            left, hot, (((1,), (1,)), ((), ())), preferred_element_type=jnp.float32
        )
        out_ref[t] = product[:RX] + product[RX : 2 * RX] + product[2 * RX :]
        return carry

    lax.fori_loop(0, NTURB, one, 0)


class Joined:
    def __init__(self, *parts):
        self.parts = parts

    def __getitem__(self, index):
        return jnp.concatenate([part[index] for part in self.parts], axis=0)


def first_kernel(before_ref, own_ref, after_ref, area_ref, s_ref, v_ref, cot_ref, sum_ref, sums):
    both = Joined(before_ref, own_ref, after_ref)
    stream(both, s_ref)
    speeds(s_ref, v_ref)
    turbine_sums(area_ref, v_ref, sums, sum_ref, 0)
    for i in range(19):
        cot_ref[i] = both[19 + i]


def forward_kernel(last, s_ref, v_ref, area_ref, rotor_ref, *rest):
    if last:
        cot_ref, next_ref, vn_ref, sum_ref, field, drag, sums = rest
    else:
        next_ref, vn_ref, sum_ref, field, sums = rest

    def one(rows, lanes):
        s = [s_ref[i, rows, lanes] for i in range(19)]
        force = weighted_area(area_ref, rotor_ref, rows, lanes) * v_ref[rows, lanes] * -THRUST
        for i, value in enumerate(collide(s, force)):
            field[i, rows, lanes] = value

    chunks(one)
    stream(field, next_ref)
    speeds(next_ref, vn_ref)
    turbine_sums(area_ref, vn_ref, sums, sum_ref, 0)
    if last:

        def other(rows, lanes):
            a = [cot_ref[i, rows, lanes] for i in range(19)]
            drag[rows, lanes] = push_back(a) * vn_ref[rows, lanes] * -THRUST

        chunks(other)
        turbine_sums(area_ref, drag, sums, sum_ref, NTURB)


def adjoint_field(s_ref, a_ref, area_ref, rotor_ref, bar_ref, field):
    def one(rows, lanes):
        s = [s_ref[i, rows, lanes] for i in range(19)]
        a = [a_ref[i, rows, lanes] for i in range(19)]
        speed_bar = weighted_area(area_ref, rotor_ref, rows, lanes) * push_back(a) * -THRUST
        speed_bar = speed_bar + weighted_area(area_ref, bar_ref, rows, lanes)
        for i, value in enumerate(collide_adjoint(s, a, speed_bar)):
            field[i, rows, lanes] = value

    chunks(one)


def backward_kernel(s_ref, a_ref, area_ref, rotor_ref, bar_ref, v_ref, out_ref, drag_ref, sum_ref, field, sums):
    adjoint_field(s_ref, a_ref, area_ref, rotor_ref, bar_ref, field)
    stream_adjoint(field, out_ref)

    def other(rows, lanes):
        a = [out_ref[i, rows, lanes] for i in range(19)]
        drag_ref[rows, lanes] = push_back(a) * v_ref[rows, lanes] * -THRUST

    chunks(other)
    turbine_sums(area_ref, drag_ref, sums, sum_ref, 0)


def last_kernel(s_ref, a_ref, area_ref, rotor_ref, bar_ref, out_ref, field, result):
    adjoint_field(s_ref, a_ref, area_ref, rotor_ref, bar_ref, field)
    stream_adjoint(field, result)
    for i in range(19):
        out_ref[i] = result[i, OWN_ROWS, OWN_LANE : OWN_LANE + OWN_SPAN]


def gather_kernel(x_ref, yz_ref, cot_ref, q1, q2, q3, v1, v2, v3, v4, u1, u2, u3, u4, n2, n3, n4, inv, out_ref):
    own = (OWN_ROWS, slice(OWN_LANE, OWN_LANE + OWN_SPAN))
    v = [ref[own] for ref in (v1, v2, v3, v4)]
    q = [ref[own] for ref in (q1, q2, q3)]
    a = [cot_ref[(i,) + own] for i in range(19)]
    q.append(push_back(a) * v[3] * -THRUST)
    rows = lax.broadcasted_iota(jnp.int32, (CX, PTS), 0) + MARGIN
    columns = lax.broadcasted_iota(jnp.int32, (OWN_SPAN, PTS), 0) + OWN_LANE

    def wide(ref, t):
        return jnp.concatenate([ref[pl.ds(t, 1), :]] * (OWN_SPAN // 128), axis=1)

    out_ref[...] = jnp.zeros_like(out_ref)

    def one(t, carry):
        u = [wide(ref, t) for ref in (u1, u2, u3, u4)]
        n = [None] + [wide(ref, t) for ref in (n2, n3, n4)]
        known = u[0] * q[0]
        for k in range(1, 4):
            known = known + u[k] * q[k] + n[k] * (v[k] - u[k])
        fields = [known, q[0], (v[0] - u[0]) * wide(inv, t)]
        left = jnp.concatenate(split_three(jnp.concatenate(fields, axis=0)), axis=0)
        hot = jnp.where(columns == yz_ref[pl.ds(t, 1), :], 1.0, 0.0).astype(jnp.bfloat16)
        product = jnp.dot(left, hot, preferred_element_type=jnp.float32)
        size = 3 * CX
        product = product[:size] + product[size : 2 * size] + product[2 * size :]
        mine = rows == x_ref[pl.ds(t, 1), :]
        for j in range(3):
            picked = jnp.where(mine, product[CX * j : CX * (j + 1)], 0.0)
            out_ref[pl.ds(j * NTURB + t, 1), 0:PTS] = jnp.sum(picked, axis=0, keepdims=True)
        return carry

    lax.fori_loop(0, NTURB, one, 0)


def call(kernel, outs, scratch, *args):
    vmem = pl.BlockSpec(memory_space=pltpu.VMEM)
    return pl.pallas_call(
        kernel,
        out_shape=[jax.ShapeDtypeStruct(shape, jnp.float32) for shape in outs],
        in_specs=[vmem] * len(args),
        out_specs=[vmem] * len(outs),
        scratch_shapes=[pltpu.VMEM(shape, jnp.float32) for shape in scratch],
        compiler_params=pltpu.CompilerParams(vmem_limit_bytes=32 * 1024 * 1024),
    )(*args)


def route(value, target):
    size_x, size_y = lax.axis_size("gx"), lax.axis_size("gy")
    pairs = []
    for i in range(size_x):
        for j in range(size_y):
            to = target(i, j)
            if to is not None:
                pairs.append((i * size_y + j, to[0] % size_x * size_y + to[1] % size_y))
    return lax.ppermute(value, ("gx", "gy"), pairs)


def swap(value):
    return route(value, lambda i, j: (i ^ 1, j))


def window(value):
    value = value + swap(value)
    left = route(value, lambda i, j: (i + 2, j))
    right = route(value, lambda i, j: (i - 2, j))
    far = route(value, lambda i, j: (i + (-4 if i % 2 else 4), j))
    value = (left + right) + (far + value)
    size = lax.axis_size("gy")
    copies = jnp.tile(value, (size, 1))
    copies = lax.all_to_all(copies, "gy", 0, 0, tiled=True)
    return jnp.sum(copies.reshape((size,) + value.shape), 0)


def merge(value, parts):
    for part in parts:
        value = jnp.where(value != 0.0, value, part)
    return value


def spread(value):
    size_x, size_y = lax.axis_size("gx"), lax.axis_size("gy")
    half = size_y // 2

    def across(first, second):
        def target(i, j):
            dy, dz = second if i % 2 else first
            return i, (j // half + dz) % 2 * half + (j % half + dy) % half

        return target

    def along(block, step, first, second):
        def target(i, j):
            move = second if i % 2 else first
            if move is None:
                return None
            return i // block * block + (i % block + move * step) % block, j

        return target

    value = merge(value, [swap(value)])
    turns = [((1, 0), (1, 1)), ((3, 0), (3, 1)), ((2, 0), (2, 1)), ((0, 1), (0, 1))]
    value = merge(value, [route(value, across(*turn)) for turn in turns])
    value = merge(value, [swap(value)])
    for block, step in ((8, 2), (size_x, 8)):
        turns = [(1, 2), (3, None)]
        value = merge(value, [route(value, along(block, step, *turn)) for turn in turns])
        value = merge(value, [swap(value)])
    return value


def shift(value, axis, step):
    size = lax.axis_size(axis)
    return lax.ppermute(value, axis, [(i, (i + step) % size) for i in range(size)])


def region(checkpoint, cotangent):
    edge = MARGIN * NZ
    span = checkpoint.shape[2]
    first = jnp.concatenate([checkpoint[:, :, :edge], cotangent[:, :, :edge]], axis=0)
    last = jnp.concatenate([checkpoint[:, :, span - edge :], cotangent[:, :, span - edge :]], axis=0)
    before, after = shift(last, "gy", 1), shift(first, "gy", -1)
    own = jnp.concatenate([checkpoint, cotangent], axis=0)
    own = jnp.concatenate([before, own, after], axis=2)
    return shift(own, "gx", 1), own, shift(own, "gx", -1)


def body(checkpoint, cotangent, blade_area, hub_tile, point_side, point_local):
    count_x, count_y = lax.axis_size("gx"), lax.axis_size("gy")
    index_x, index_y = lax.axis_index("gx"), lax.axis_index("gy")
    area = blade_area.reshape(NTURB, PTS)
    side = point_side.reshape(NTURB, PTS)
    local = point_local.reshape(NTURB, PTS)
    hub = hub_tile.reshape(NTURB, 1)
    cell_x = (hub // count_y + side // 3 - 1 - index_x) * CX + local // (CY * NZ) + MARGIN
    cell_y = (hub % count_y + side % 3 - 1 - index_y) * CY + local // NZ % CY + MARGIN
    cell_x = cell_x % (count_x * CX)
    cell_y = cell_y % (count_y * CY)
    inside = (cell_x < RX) & (cell_y < RY)
    cell_x = jnp.where(inside, cell_x, -1)
    cell_yz = jnp.where(inside, cell_y * NZ + local % NZ, -1)
    mine_y = (cell_y >= MARGIN) & (cell_y < MARGIN + CY)
    inverse = jnp.broadcast_to(1.0 / jnp.sum(area, 1, keepdims=True), (NTURB, 128))

    full = (19, RX, LANES)
    flat = (RX, LANES)
    row = (NTURB, 128)
    parts = region(checkpoint, cotangent)
    (spots,) = call(area_kernel, [(NTURB,) + flat], [], cell_x, cell_yz, area)

    s, v, rotor = [None] * 5, [None] * 5, [None] * 5
    s[1], v[1], cot, sums = call(first_kernel, [full, flat, full, row], [row], *parts, spots)
    for k in (1, 2, 3):
        rotor[k] = window(sums) * inverse
        last = k == 3
        outs = [full, flat, (2 * NTURB, 128) if last else row]
        s[k + 1], v[k + 1], sums = call(
            functools.partial(forward_kernel, last),
            outs,
            [full] + ([flat] if last else []) + [row],
            *([s[k], v[k], spots, rotor[k]] + ([cot] if last else [])),
        )
    sums = window(sums)
    rotor[4] = sums[:NTURB] * inverse
    sums = sums[NTURB:]
    adjoint = cot
    bar, drag = [None] * 5, [None] * 5
    for k in (4, 3, 2):
        bar[k] = (window(sums) if k < 4 else sums) * inverse
        adjoint, drag[k - 1], sums = call(
            backward_kernel,
            [full, flat, row],
            [full, row],
            *(s[k], adjoint, spots, rotor[k], bar[k], v[k - 1]),
        )
    (points,) = call(
        gather_kernel,
        [(3 * NTURB, 128)],
        [],
        *([cell_x, jnp.where(mine_y, cell_yz, -1), cot] + drag[1:4] + v[1:] + rotor[1:] + bar[2:] + [inverse]),
    )
    points = spread(points)[:, :PTS]
    known, swing, slope = points[:NTURB], points[NTURB : 2 * NTURB], points[2 * NTURB :]
    total = jnp.sum(area * swing, 1, keepdims=True)
    grad_area = (known + total * slope).reshape(-1)
    bar[1] = total * inverse
    (grad,) = call(
        last_kernel,
        [(19, CX, CY * NZ)],
        [full, full],
        *(s[1], adjoint, spots, rotor[1], bar[1]),
    )
    return grad, grad_area


def solution(mesh):
    return jax.shard_map(
        body,
        mesh=mesh,
        in_specs=(P(None, "gx", "gy"), P(None, "gx", "gy"), P(), P(), P(), P()),
        out_specs=(P(None, "gx", "gy"), P()),
        check_vma=False,
    )
```

profile of v0, /device:TPU:1, one launch (start us, length us, event | category | flops | bytes accessed | tf_op | source)
XLA Modules:
  0.0 238.3 jit_solution(5036456571749167612)
XLA Ops:
  9.4 3.5 %collective-permute-start.2 = (f32[38,8,512]{2,1,0:T(8,128)S(1)}, f32[38,8,512]{2,1,0:T(8,128)S(1)}, u32[]{:S(2)}, u32[]{:S(2)}) collective-permute-start(f32[38,8,512]{2,1,0:T(8,128)S(1)} %pad_maximum_fusion.own_ref), channel_id=1, source_target_pairs={{0,8},{8,16},{16,24},{24,32},{32,40},{40,48},{48,56},{56,64},{64,7... | collective-permute-start | bytes 1867784 | tf_op jit(solution)/shard_map/ppermute | solution.py:504
  15.9 4.2 %collective-permute-done.2.before_ref = f32[38,8,512]{2,1,0:T(8,128)S(1)} collective-permute-done((f32[38,8,512]{2,1,0:T(8,128)S(1)}, f32[38,8,512]{2,1,0:T(8,128)S(1)}, u32[]{:S(2)}, u32[]{:S(2)}) %collective-permute-start.2) | collective-permute-done | bytes 622624 | tf_op jit(solution)/shard_map/ppermute | solution.py:504
  23.4 10.1 %collective-permute-start.4 = (f32[16,128]{1,0:T(8,128)S(1)}, f32[16,128]{1,0:T(8,128)S(1)}, u32[]{:S(2)}, u32[]{:S(2)}) collective-permute-start(f32[16,128]{1,0:T(8,128)S(1)} %get-tuple-element.25), channel_id=1, source_target_pairs={{0,8},{1,9},{2,10},{3,11},{4,12},{5,13},{6,14},{7,15},{8,0},{9,1},... | collective-permute-start | bytes 24584 | tf_op jit(solution)/shard_map/ppermute | solution.py:446
  34.4 6.1 %collective-permute-start.6 = (f32[16,128]{1,0:T(8,128)S(1)}, f32[16,128]{1,0:T(8,128)S(1)}, u32[]{:S(2)}, u32[]{:S(2)}) collective-permute-start(f32[16,128]{1,0:T(8,128)S(1)} %add.157), channel_id=1, source_target_pairs={{0,240},{1,241},{2,242},{3,243},{4,244},{5,245},{6,246},{7,247},{8... | collective-permute-start | bytes 24584 | tf_op jit(solution)/shard_map/ppermute | solution.py:446
  45.2 4.8 %all-to-all-start = ((f32[8,16,128]{2,1,0:T(8,128)}), f32[8,16,128]{2,1,0:T(8,128)S(1)}, u32[]{:S(2)}, u32[]{:S(2)}) async-start(f32[8,16,128]{2,1,0:T(8,128)} %tile.12), calls=%async_computation | async-start | bytes 131072 | tf_op jit(solution)/shard_map/all_to_all | solution.py:461
  49.9 5.2 %all-to-all-done = f32[8,16,128]{2,1,0:T(8,128)S(1)} async-done(((f32[8,16,128]{2,1,0:T(8,128)}), f32[8,16,128]{2,1,0:T(8,128)S(1)}, u32[]{:S(2)}, u32[]{:S(2)}) %all-to-all-start) | async-done | bytes 65568 | tf_op jit(solution)/shard_map/all_to_all | solution.py:461
  57.4 6.5 %collective-permute-start.8 = (f32[16,128]{1,0:T(8,128)S(1)}, f32[16,128]{1,0:T(8,128)S(1)}, u32[]{:S(2)}, u32[]{:S(2)}) collective-permute-start(f32[16,128]{1,0:T(8,128)S(1)} %get-tuple-element.28), channel_id=1, source_target_pairs={{0,8},{1,9},{2,10},{3,11},{4,12},{5,13},{6,14},{7,15},{8,0},{9,1},... | collective-permute-start | bytes 24584 | tf_op jit(solution)/shard_map/ppermute | solution.py:446
  71.6 7.6 %all_to_all.36 = f32[8,16,128]{2,1,0:T(8,128)S(1)} all-to-all(f32[8,16,128]{2,1,0:T(8,128)S(1)} %tile.13), channel_id=1, replica_groups=mesh['gx'=32,'gy'=8] {'gy'}, dimensions={0} | all-to-all | bytes 131072 | tf_op jit(solution)/shard_map/all_to_all | solution.py:461
  82.6 4.1 %collective-permute-start.12 = (f32[16,128]{1,0:T(8,128)S(1)}, f32[16,128]{1,0:T(8,128)S(1)}, u32[]{:S(2)}, u32[]{:S(2)}) collective-permute-start(f32[16,128]{1,0:T(8,128)S(1)} %get-tuple-element.31), channel_id=1, source_target_pairs={{0,8},{1,9},{2,10},{3,11},{4,12},{5,13},{6,14},{7,15},{8,0},{9,1},... | collective-permute-start | bytes 24584 | tf_op jit(solution)/shard_map/ppermute | solution.py:446
  88.1 5.2 %collective-permute-start.14 = (f32[16,128]{1,0:T(8,128)S(1)}, f32[16,128]{1,0:T(8,128)S(1)}, u32[]{:S(2)}, u32[]{:S(2)}) collective-permute-start(f32[16,128]{1,0:T(8,128)S(1)} %add.165), channel_id=1, source_target_pairs={{0,240},{1,241},{2,242},{3,243},{4,244},{5,245},{6,246},{7,247},{8... | collective-permute-start | bytes 24584 | tf_op jit(solution)/shard_map/ppermute | solution.py:446
  97.3 7.6 %all_to_all.37 = f32[8,16,128]{2,1,0:T(8,128)S(1)} all-to-all(f32[8,16,128]{2,1,0:T(8,128)S(1)} %tile.14), channel_id=1, replica_groups=mesh['gx'=32,'gy'=8] {'gy'}, dimensions={0} | all-to-all | bytes 131072 | tf_op jit(solution)/shard_map/all_to_all | solution.py:461
  108.5 6.2 %collective-permute-start.16 = (f32[32,128]{1,0:T(8,128)S(1)}, f32[32,128]{1,0:T(8,128)S(1)}, u32[]{:S(2)}, u32[]{:S(2)}) collective-permute-start(f32[32,128]{1,0:T(8,128)S(1)} %get-tuple-element.34), channel_id=1, source_target_pairs={{0,8},{1,9},{2,10},{3,11},{4,12},{5,13},{6,14},{7,15},{8,0},{9,1},... | collective-permute-start | bytes 49160 | tf_op jit(solution)/shard_map/ppermute | solution.py:446
  115.6 5.7 %collective-permute-start.18 = (f32[32,128]{1,0:T(8,128)S(1)}, f32[32,128]{1,0:T(8,128)S(1)}, u32[]{:S(2)}, u32[]{:S(2)}) collective-permute-start(f32[32,128]{1,0:T(8,128)S(1)} %add.169), channel_id=1, source_target_pairs={{0,240},{1,241},{2,242},{3,243},{4,244},{5,245},{6,246},{7,247},{8... | collective-permute-start | bytes 49160 | tf_op jit(solution)/shard_map/ppermute | solution.py:446
  125.4 7.8 %all_to_all.38 = f32[8,32,128]{2,1,0:T(8,128)S(1)} all-to-all(f32[8,32,128]{2,1,0:T(8,128)S(1)} %tile.15), channel_id=1, replica_groups=mesh['gx'=32,'gy'=8] {'gy'}, dimensions={0} | all-to-all | bytes 262144 | tf_op jit(solution)/shard_map/all_to_all | solution.py:461
  137.0 6.2 %collective-permute-start.20 = (f32[16,128]{1,0:T(8,128)S(1)}, f32[16,128]{1,0:T(8,128)S(1)}, u32[]{:S(2)}, u32[]{:S(2)}) collective-permute-start(f32[16,128]{1,0:T(8,128)S(1)} %get-tuple-element.36), channel_id=1, source_target_pairs={{0,8},{1,9},{2,10},{3,11},{4,12},{5,13},{6,14},{7,15},{8,0},{9,1},... | collective-permute-start | bytes 24584 | tf_op jit(solution)/shard_map/ppermute | solution.py:446
  144.0 5.7 %collective-permute-start.22 = (f32[16,128]{1,0:T(8,128)S(1)}, f32[16,128]{1,0:T(8,128)S(1)}, u32[]{:S(2)}, u32[]{:S(2)}) collective-permute-start(f32[16,128]{1,0:T(8,128)S(1)} %add.173), channel_id=1, source_target_pairs={{0,240},{1,241},{2,242},{3,243},{4,244},{5,245},{6,246},{7,247},{8... | collective-permute-start | bytes 24584 | tf_op jit(solution)/shard_map/ppermute | solution.py:446
  153.7 7.6 %all_to_all.39 = f32[8,16,128]{2,1,0:T(8,128)S(1)} all-to-all(f32[8,16,128]{2,1,0:T(8,128)S(1)} %tile.16), channel_id=1, replica_groups=mesh['gx'=32,'gy'=8] {'gy'}, dimensions={0} | all-to-all | bytes 131072 | tf_op jit(solution)/shard_map/all_to_all | solution.py:461
  166.2 6.4 %collective-permute-start.24 = (f32[16,128]{1,0:T(8,128)S(1)}, f32[16,128]{1,0:T(8,128)S(1)}, u32[]{:S(2)}, u32[]{:S(2)}) collective-permute-start(f32[16,128]{1,0:T(8,128)S(1)} %get-tuple-element.38), channel_id=1, source_target_pairs={{0,8},{1,9},{2,10},{3,11},{4,12},{5,13},{6,14},{7,15},{8,0},{9,1},... | collective-permute-start | bytes 24584 | tf_op jit(solution)/shard_map/ppermute | solution.py:446
  173.4 5.7 %collective-permute-start.26 = (f32[16,128]{1,0:T(8,128)S(1)}, f32[16,128]{1,0:T(8,128)S(1)}, u32[]{:S(2)}, u32[]{:S(2)}) collective-permute-start(f32[16,128]{1,0:T(8,128)S(1)} %add.177), channel_id=1, source_target_pairs={{0,240},{1,241},{2,242},{3,243},{4,244},{5,245},{6,246},{7,247},{8... | collective-permute-start | bytes 24584 | tf_op jit(solution)/shard_map/ppermute | solution.py:446
  183.1 7.6 %all_to_all.40 = f32[8,16,128]{2,1,0:T(8,128)S(1)} all-to-all(f32[8,16,128]{2,1,0:T(8,128)S(1)} %tile.17), channel_id=1, replica_groups=mesh['gx'=32,'gy'=8] {'gy'}, dimensions={0} | all-to-all | bytes 131072 | tf_op jit(solution)/shard_map/all_to_all | solution.py:461
  197.8 6.3 %collective-permute-start.28 = (f32[48,128]{1,0:T(8,128)S(1)}, f32[48,128]{1,0:T(8,128)S(1)}, u32[]{:S(2)}, u32[]{:S(2)}) collective-permute-start(f32[48,128]{1,0:T(8,128)S(1)} %shard_map.85), channel_id=1, source_target_pairs={{0,8},{1,9},{2,10},{3,11},{4,12},{5,13},{6,14},{7,15},{8,0},{9,1},... | collective-permute-start | bytes 73736 | tf_op jit(solution)/shard_map/ppermute | solution.py:446
  209.9 3.8 %collective-permute-done.31 = f32[48,128]{1,0:T(8,128)S(1)} collective-permute-done((f32[48,128]{1,0:T(8,128)S(1)}, f32[48,128]{1,0:T(8,128)S(1)}, u32[]{:S(2)}, u32[]{:S(2)}) %collective-permute-start.31) | collective-permute-done | bytes 24608 | tf_op jit(solution)/shard_map/ppermute | solution.py:446
  222.7 5.6 %collective-permute-start.37 = (f32[48,128]{1,0:T(8,128)S(1)}, f32[48,128]{1,0:T(8,128)S(1)}, u32[]{:S(2)}, u32[]{:S(2)}) collective-permute-start(f32[48,128]{1,0:T(8,128)S(1)} %compare_select_fusion.3), channel_id=1, source_target_pairs={{0,64},{1,65},{2,66},{3,67},{4,68},{5,69},{6,70},{7,71},{8,136},{9... | collective-permute-start | bytes 73736 | tf_op jit(solution)/shard_map/ppermute | solution.py:446
  229.5 3.9 %collective-permute-start.39 = (f32[48,128]{1,0:T(8,128)S(1)}, f32[48,128]{1,0:T(8,128)S(1)}, u32[]{:S(2)}, u32[]{:S(2)}) collective-permute-start(f32[48,128]{1,0:T(8,128)S(1)} %compare_select_fusion.1), channel_id=1, source_target_pairs={{0,8},{1,9},{2,10},{3,11},{4,12},{5,13},{6,14},{7,15},{8,0},{9,1},... | collective-permute-start | bytes 73736 | tf_op jit(solution)/shard_map/ppermute | solution.py:446
  (172 shorter events, 94.1 us)
Async XLA Ops:
  1.7 7.6 %collective-permute-start = (f32[38,8,128]{2,1,0:T(8,128)S(1)}, f32[38,8,128]{2,1,0:T(8,128)S(1)}, u32[]{:S(2)}, u32[]{:S(2)}) collective-permute-start(f32[38,8,128]{2,1,0:T(8,128)S(1)} %pad_maximum_fusion.1), channel_id=1, source_target_pairs={{0,1},{1,2},{2,3},{3,4},{4,5},{5,6},{6,7},{7,0},{8,9},{9,10},{10,1... | collective-permute-start | bytes 466952 | tf_op jit(solution)/shard_map/ppermute | solution.py:504
  3.9 5.4 %collective-permute-start.1 = (f32[38,8,128]{2,1,0:T(8,128)S(1)}, f32[38,8,128]{2,1,0:T(8,128)S(1)}, u32[]{:S(2)}, u32[]{:S(2)}) collective-permute-start(f32[38,8,128]{2,1,0:T(8,128)S(1)} %pad_maximum_fusion.2), channel_id=1, source_target_pairs={{0,7},{1,0},{2,1},{3,2},{4,3},{5,4},{6,5},{7,6},{8,15},{9,8},{10,9... | collective-permute-start | bytes 466952 | tf_op jit(solution)/shard_map/ppermute | solution.py:504
  9.4 10.7 %collective-permute-start.2 = (f32[38,8,512]{2,1,0:T(8,128)S(1)}, f32[38,8,512]{2,1,0:T(8,128)S(1)}, u32[]{:S(2)}, u32[]{:S(2)}) collective-permute-start(f32[38,8,512]{2,1,0:T(8,128)S(1)} %pad_maximum_fusion.own_ref), channel_id=1, source_target_pairs={{0,8},{8,16},{16,24},{24,32},{32,40},{40,48},{48,56},{56,64},{64,7... | collective-permute-start | bytes 1867784 | tf_op jit(solution)/shard_map/ppermute | solution.py:504
  12.9 10.0 %collective-permute-start.3 = (f32[38,8,512]{2,1,0:T(8,128)S(1)}, f32[38,8,512]{2,1,0:T(8,128)S(1)}, u32[]{:S(2)}, u32[]{:S(2)}) collective-permute-start(f32[38,8,512]{2,1,0:T(8,128)S(1)} %pad_maximum_fusion.own_ref), channel_id=1, source_target_pairs={{0,248},{8,0},{16,8},{24,16},{32,24},{40,32},{48,40},{56,48},{64,5... | collective-permute-start | bytes 1867784 | tf_op jit(solution)/shard_map/ppermute | solution.py:504
  23.4 11.0 %collective-permute-start.4 = (f32[16,128]{1,0:T(8,128)S(1)}, f32[16,128]{1,0:T(8,128)S(1)}, u32[]{:S(2)}, u32[]{:S(2)}) collective-permute-start(f32[16,128]{1,0:T(8,128)S(1)} %get-tuple-element.25), channel_id=1, source_target_pairs={{0,8},{1,9},{2,10},{3,11},{4,12},{5,13},{6,14},{7,15},{8,0},{9,1},... | collective-permute-start | bytes 24584 | tf_op jit(solution)/shard_map/ppermute | solution.py:446
  34.4 7.4 %collective-permute-start.5 = (f32[16,128]{1,0:T(8,128)S(1)}, f32[16,128]{1,0:T(8,128)S(1)}, u32[]{:S(2)}, u32[]{:S(2)}) collective-permute-start(f32[16,128]{1,0:T(8,128)S(1)} %add.157), channel_id=1, source_target_pairs={{0,16},{1,17},{2,18},{3,19},{4,20},{5,21},{6,22},{7,23},{8,24},{9,... | collective-permute-start | bytes 24584 | tf_op jit(solution)/shard_map/ppermute | solution.py:446
  34.4 7.4 %collective-permute-start.6 = (f32[16,128]{1,0:T(8,128)S(1)}, f32[16,128]{1,0:T(8,128)S(1)}, u32[]{:S(2)}, u32[]{:S(2)}) collective-permute-start(f32[16,128]{1,0:T(8,128)S(1)} %add.157), channel_id=1, source_target_pairs={{0,240},{1,241},{2,242},{3,243},{4,244},{5,245},{6,246},{7,247},{8... | collective-permute-start | bytes 24584 | tf_op jit(solution)/shard_map/ppermute | solution.py:446
  45.2 10.0 %all-to-all-start = ((f32[8,16,128]{2,1,0:T(8,128)}), f32[8,16,128]{2,1,0:T(8,128)S(1)}, u32[]{:S(2)}, u32[]{:S(2)}) async-start(f32[8,16,128]{2,1,0:T(8,128)} %tile.12), calls=%async_computation | async-start | bytes 131072 | tf_op jit(solution)/shard_map/all_to_all | solution.py:461
  57.4 7.3 %collective-permute-start.8 = (f32[16,128]{1,0:T(8,128)S(1)}, f32[16,128]{1,0:T(8,128)S(1)}, u32[]{:S(2)}, u32[]{:S(2)}) collective-permute-start(f32[16,128]{1,0:T(8,128)S(1)} %get-tuple-element.28), channel_id=1, source_target_pairs={{0,8},{1,9},{2,10},{3,11},{4,12},{5,13},{6,14},{7,15},{8,0},{9,1},... | collective-permute-start | bytes 24584 | tf_op jit(solution)/shard_map/ppermute | solution.py:446
  64.8 6.8 %collective-permute-start.9 = (f32[16,128]{1,0:T(8,128)S(1)}, f32[16,128]{1,0:T(8,128)S(1)}, u32[]{:S(2)}, u32[]{:S(2)}) collective-permute-start(f32[16,128]{1,0:T(8,128)S(1)} %add.161), channel_id=1, source_target_pairs={{0,16},{1,17},{2,18},{3,19},{4,20},{5,21},{6,22},{7,23},{8,24},{9,... | collective-permute-start | bytes 24584 | tf_op jit(solution)/shard_map/ppermute | solution.py:446
  87.6 6.8 %collective-permute-start.13 = (f32[16,128]{1,0:T(8,128)S(1)}, f32[16,128]{1,0:T(8,128)S(1)}, u32[]{:S(2)}, u32[]{:S(2)}) collective-permute-start(f32[16,128]{1,0:T(8,128)S(1)} %add.165), channel_id=1, source_target_pairs={{0,16},{1,17},{2,18},{3,19},{4,20},{5,21},{6,22},{7,23},{8,24},{9,... | collective-permute-start | bytes 24584 | tf_op jit(solution)/shard_map/ppermute | solution.py:446
  88.1 6.3 %collective-permute-start.14 = (f32[16,128]{1,0:T(8,128)S(1)}, f32[16,128]{1,0:T(8,128)S(1)}, u32[]{:S(2)}, u32[]{:S(2)}) collective-permute-start(f32[16,128]{1,0:T(8,128)S(1)} %add.165), channel_id=1, source_target_pairs={{0,240},{1,241},{2,242},{3,243},{4,244},{5,245},{6,246},{7,247},{8... | collective-permute-start | bytes 24584 | tf_op jit(solution)/shard_map/ppermute | solution.py:446
  108.5 7.1 %collective-permute-start.16 = (f32[32,128]{1,0:T(8,128)S(1)}, f32[32,128]{1,0:T(8,128)S(1)}, u32[]{:S(2)}, u32[]{:S(2)}) collective-permute-start(f32[32,128]{1,0:T(8,128)S(1)} %get-tuple-element.34), channel_id=1, source_target_pairs={{0,8},{1,9},{2,10},{3,11},{4,12},{5,13},{6,14},{7,15},{8,0},{9,1},... | collective-permute-start | bytes 49160 | tf_op jit(solution)/shard_map/ppermute | solution.py:446
  115.6 6.9 %collective-permute-start.17 = (f32[32,128]{1,0:T(8,128)S(1)}, f32[32,128]{1,0:T(8,128)S(1)}, u32[]{:S(2)}, u32[]{:S(2)}) collective-permute-start(f32[32,128]{1,0:T(8,128)S(1)} %add.169), channel_id=1, source_target_pairs={{0,16},{1,17},{2,18},{3,19},{4,20},{5,21},{6,22},{7,23},{8,24},{9,... | collective-permute-start | bytes 49160 | tf_op jit(solution)/shard_map/ppermute | solution.py:446
  115.6 6.9 %collective-permute-start.18 = (f32[32,128]{1,0:T(8,128)S(1)}, f32[32,128]{1,0:T(8,128)S(1)}, u32[]{:S(2)}, u32[]{:S(2)}) collective-permute-start(f32[32,128]{1,0:T(8,128)S(1)} %add.169), channel_id=1, source_target_pairs={{0,240},{1,241},{2,242},{3,243},{4,244},{5,245},{6,246},{7,247},{8... | collective-permute-start | bytes 49160 | tf_op jit(solution)/shard_map/ppermute | solution.py:446
  137.0 7.1 %collective-permute-start.20 = (f32[16,128]{1,0:T(8,128)S(1)}, f32[16,128]{1,0:T(8,128)S(1)}, u32[]{:S(2)}, u32[]{:S(2)}) collective-permute-start(f32[16,128]{1,0:T(8,128)S(1)} %get-tuple-element.36), channel_id=1, source_target_pairs={{0,8},{1,9},{2,10},{3,11},{4,12},{5,13},{6,14},{7,15},{8,0},{9,1},... | collective-permute-start | bytes 24584 | tf_op jit(solution)/shard_map/ppermute | solution.py:446
  144.0 6.7 %collective-permute-start.21 = (f32[16,128]{1,0:T(8,128)S(1)}, f32[16,128]{1,0:T(8,128)S(1)}, u32[]{:S(2)}, u32[]{:S(2)}) collective-permute-start(f32[16,128]{1,0:T(8,128)S(1)} %add.173), channel_id=1, source_target_pairs={{0,16},{1,17},{2,18},{3,19},{4,20},{5,21},{6,22},{7,23},{8,24},{9,... | collective-permute-start | bytes 24584 | tf_op jit(solution)/shard_map/ppermute | solution.py:446
  144.0 6.7 %collective-permute-start.22 = (f32[16,128]{1,0:T(8,128)S(1)}, f32[16,128]{1,0:T(8,128)S(1)}, u32[]{:S(2)}, u32[]{:S(2)}) collective-permute-start(f32[16,128]{1,0:T(8,128)S(1)} %add.173), channel_id=1, source_target_pairs={{0,240},{1,241},{2,242},{3,243},{4,244},{5,245},{6,246},{7,247},{8... | collective-permute-start | bytes 24584 | tf_op jit(solution)/shard_map/ppermute | solution.py:446
  166.2 7.2 %collective-permute-start.24 = (f32[16,128]{1,0:T(8,128)S(1)}, f32[16,128]{1,0:T(8,128)S(1)}, u32[]{:S(2)}, u32[]{:S(2)}) collective-permute-start(f32[16,128]{1,0:T(8,128)S(1)} %get-tuple-element.38), channel_id=1, source_target_pairs={{0,8},{1,9},{2,10},{3,11},{4,12},{5,13},{6,14},{7,15},{8,0},{9,1},... | collective-permute-start | bytes 24584 | tf_op jit(solution)/shard_map/ppermute | solution.py:446
  173.4 6.8 %collective-permute-start.25 = (f32[16,128]{1,0:T(8,128)S(1)}, f32[16,128]{1,0:T(8,128)S(1)}, u32[]{:S(2)}, u32[]{:S(2)}) collective-permute-start(f32[16,128]{1,0:T(8,128)S(1)} %add.177), channel_id=1, source_target_pairs={{0,16},{1,17},{2,18},{3,19},{4,20},{5,21},{6,22},{7,23},{8,24},{9,... | collective-permute-start | bytes 24584 | tf_op jit(solution)/shard_map/ppermute | solution.py:446
  173.4 6.8 %collective-permute-start.26 = (f32[16,128]{1,0:T(8,128)S(1)}, f32[16,128]{1,0:T(8,128)S(1)}, u32[]{:S(2)}, u32[]{:S(2)}) collective-permute-start(f32[16,128]{1,0:T(8,128)S(1)} %add.177), channel_id=1, source_target_pairs={{0,240},{1,241},{2,242},{3,243},{4,244},{5,245},{6,246},{7,247},{8... | collective-permute-start | bytes 24584 | tf_op jit(solution)/shard_map/ppermute | solution.py:446
  197.8 7.2 %collective-permute-start.28 = (f32[48,128]{1,0:T(8,128)S(1)}, f32[48,128]{1,0:T(8,128)S(1)}, u32[]{:S(2)}, u32[]{:S(2)}) collective-permute-start(f32[48,128]{1,0:T(8,128)S(1)} %shard_map.85), channel_id=1, source_target_pairs={{0,8},{1,9},{2,10},{3,11},{4,12},{5,13},{6,14},{7,15},{8,0},{9,1},... | collective-permute-start | bytes 73736 | tf_op jit(solution)/shard_map/ppermute | solution.py:446
  208.6 5.1 %collective-permute-start.32 = (f32[48,128]{1,0:T(8,128)S(1)}, f32[48,128]{1,0:T(8,128)S(1)}, u32[]{:S(2)}, u32[]{:S(2)}) collective-permute-start(f32[48,128]{1,0:T(8,128)S(1)} %compare_select_fusion.11), channel_id=1, source_target_pairs={{0,4},{1,5},{2,6},{3,7},{4,0},{5,1},{6,2},{7,3},{8,12},{9,13},{10,... | collective-permute-start | bytes 73736 | tf_op jit(solution)/shard_map/ppermute | solution.py:446
  222.7 6.8 %collective-permute-start.37 = (f32[48,128]{1,0:T(8,128)S(1)}, f32[48,128]{1,0:T(8,128)S(1)}, u32[]{:S(2)}, u32[]{:S(2)}) collective-permute-start(f32[48,128]{1,0:T(8,128)S(1)} %compare_select_fusion.3), channel_id=1, source_target_pairs={{0,64},{1,65},{2,66},{3,67},{4,68},{5,69},{6,70},{7,71},{8,136},{9... | collective-permute-start | bytes 73736 | tf_op jit(solution)/shard_map/ppermute | solution.py:446
  (37 other events, 128.8 us)
where the time goes:
time: 240 us; the launch traced here: 238 us
  starting transfers between devices  109 us (45%)
  waiting for transfers between devices  53.9 us (22%)
  blocking collectives  38.1 us (16%)
  local copies, waits for them, and re-layouts  18.4 us (8%)
  Pallas kernels  16.7 us (7%)
    ppermute x36, starting transfers between devices, route(): return lax.ppermute(value, ('gx', 'gy'), pairs)  95.7 us
    ppermute x36, waiting for transfers between devices, route(): return lax.ppermute(value, ('gx', 'gy'), pairs)  41 us
    all_to_all x5, blocking collectives, window(): copies = lax.all_to_all(copies, 'gy', 0, 0, tiled=True)  38.1 us
    pallas_call x10, Pallas kernels, call(): pl.pallas_call(kernel, out_shape=[jax.ShapeDtypeStruct(shape, jnp.float32...  16.7 us
    unnamed x40, local copies, waits for them, and re-layouts  15.5 us
    ppermute x4, starting transfers between devices, shift(): lax.ppermute(value, axis, [(i, (i + step) % size) for i in range(size)])  8.64 us
    ppermute x4, waiting for transfers between devices, shift(): lax.ppermute(value, axis, [(i, (i + step) % size) for i in range(size)])  7.71 us
    all_to_all x1, waiting for transfers between devices, window(): copies = lax.all_to_all(copies, 'gy', 0, 0, tiled=True)  5.19 us
  transfers between devices with their start and end apart: 41, of which 30 were waited for; matrix products, arithmetic and copies ran while one was open for 0% of the time, Pallas kernels for 1%

commit v1 on v0

--- a/solution.py
+++ b/solution.py
@@ -21,6 +21,8 @@
 OWN_ROWS = slice(MARGIN, MARGIN + CX)
 OWN_LANE = MARGIN * NZ
 OWN_SPAN = CY * NZ
+
+VMEM_LIMIT = 8 * 1024 * 1024
 
 TAU_ZERO = 0.52
 SMAGORINSKY = 0.17 * 0.17
@@ -268,7 +270,7 @@
     return (a[1] - a[2]) * (1.0 / 6.0) + odd * (1.0 / 12.0)
 
 
-def turbine_sums(area_ref, field_ref, sums_ref, out_ref, base):
+def turbine_sums(area_ref, field_ref, sums_ref, base):
     parts = [field_ref[OWN_ROWS, OWN_LANE + j : OWN_LANE + j + 128] for j in range(0, OWN_SPAN, 128)]
     for t in range(NTURB):
         total = None
@@ -276,9 +278,27 @@
             lane = OWN_LANE + 128 * j
             term = area_ref[t, OWN_ROWS, lane : lane + 128] * part
             total = term if total is None else total + term
-        sums_ref[t : t + 1, :] = jnp.sum(total, axis=0, keepdims=True)
-    row = jnp.sum(sums_ref[...], axis=1, keepdims=True)
-    out_ref[base : base + NTURB, :] = jnp.broadcast_to(row, (NTURB, 128))
+        sums_ref[base + t : base + t + 1, :] = jnp.sum(total, axis=0, keepdims=True)
+
+
+def publish(sums_ref, out_ref):
+    ones = jnp.ones((8, 128), jnp.bfloat16)
+    row = None
+    for part in split_three(sums_ref[...]):
+        term = lax.dot_general(
+            ones, part, (((1,), (1,)), ((), ())), preferred_element_type=jnp.float32
+        )
+        row = term if row is None else row + term
+    for j in range(0, out_ref.shape[0], 8):
+        out_ref[j : j + 8, :] = row
+
+
+def totals(got_ref, base):
+    row = jnp.sum(got_ref[...], axis=0, keepdims=True)
+    index = lax.broadcasted_iota(jnp.int32, (NTURB, 128), 0) + base
+    lane = lax.broadcasted_iota(jnp.int32, (NTURB, 128), 1)
+    picked = jnp.where(index == lane, jnp.broadcast_to(row, (NTURB, 128)), 0.0)
+    return jnp.broadcast_to(jnp.sum(picked, axis=1, keepdims=True), (NTURB, 128))
 
 
 def weighted_area(area_ref, weight_ref, rows, lanes):
@@ -322,20 +342,23 @@
         return jnp.concatenate([part[index] for part in self.parts], axis=0)
 
 
-def first_kernel(before_ref, own_ref, after_ref, area_ref, s_ref, v_ref, cot_ref, sum_ref, sums):
+def first_kernel(before_ref, own_ref, after_ref, area_ref, s_ref, v_ref, cot_ref, out_ref, sums):
     both = Joined(before_ref, own_ref, after_ref)
     stream(both, s_ref)
     speeds(s_ref, v_ref)
-    turbine_sums(area_ref, v_ref, sums, sum_ref, 0)
+    sums[...] = jnp.zeros_like(sums)
+    turbine_sums(area_ref, v_ref, sums, 0)
+    publish(sums, out_ref)
     for i in range(19):
         cot_ref[i] = both[19 + i]
 
 
-def forward_kernel(last, s_ref, v_ref, area_ref, rotor_ref, *rest):
+def forward_kernel(last, s_ref, v_ref, area_ref, inv_ref, got_ref, *rest):
     if last:
-        cot_ref, next_ref, vn_ref, sum_ref, field, drag, sums = rest
+        cot_ref, next_ref, vn_ref, rotor_ref, out_ref, field, sums, drag = rest
     else:
-        next_ref, vn_ref, sum_ref, field, sums = rest
+        next_ref, vn_ref, rotor_ref, out_ref, field, sums = rest
+    rotor_ref[...] = totals(got_ref, 0) * inv_ref[...]
 
     def one(rows, lanes):
         s = [s_ref[i, rows, lanes] for i in range(19)]
@@ -346,7 +369,8 @@
     chunks(one)
     stream(field, next_ref)
     speeds(next_ref, vn_ref)
-    turbine_sums(area_ref, vn_ref, sums, sum_ref, 0)
+    sums[...] = jnp.zeros_like(sums)
+    turbine_sums(area_ref, vn_ref, sums, 0)
     if last:
 
         def other(rows, lanes):
@@ -354,7 +378,8 @@
             drag[rows, lanes] = push_back(a) * vn_ref[rows, lanes] * -THRUST
 
         chunks(other)
-        turbine_sums(area_ref, drag, sums, sum_ref, NTURB)
+        turbine_sums(area_ref, drag, sums, NTURB)
+    publish(sums, out_ref)
 
 
 def adjoint_field(s_ref, a_ref, area_ref, rotor_ref, bar_ref, field):
@@ -369,7 +394,13 @@
     chunks(one)
 
 
-def backward_kernel(s_ref, a_ref, area_ref, rotor_ref, bar_ref, v_ref, out_ref, drag_ref, sum_ref, field, sums):
+def backward_kernel(first, s_ref, a_ref, area_ref, inv_ref, got_ref, v_ref, *rest):
+    if first:
+        out_ref, drag_ref, bar_ref, publish_ref, rotor_ref, field, sums = rest
+        rotor_ref[...] = totals(got_ref, 0) * inv_ref[...]
+    else:
+        rotor_ref, out_ref, drag_ref, bar_ref, publish_ref, field, sums = rest
+    bar_ref[...] = totals(got_ref, NTURB if first else 0) * inv_ref[...]
     adjoint_field(s_ref, a_ref, area_ref, rotor_ref, bar_ref, field)
     stream_adjoint(field, out_ref)
 
@@ -378,7 +409,9 @@
         drag_ref[rows, lanes] = push_back(a) * v_ref[rows, lanes] * -THRUST
 
     chunks(other)
-    turbine_sums(area_ref, drag_ref, sums, sum_ref, 0)
+    sums[...] = jnp.zeros_like(sums)
+    turbine_sums(area_ref, drag_ref, sums, 0)
+    publish(sums, publish_ref)
 
 
 def last_kernel(s_ref, a_ref, area_ref, rotor_ref, bar_ref, out_ref, field, result):
@@ -431,7 +464,7 @@
         in_specs=[vmem] * len(args),
         out_specs=[vmem] * len(outs),
         scratch_shapes=[pltpu.VMEM(shape, jnp.float32) for shape in scratch],
-        compiler_params=pltpu.CompilerParams(vmem_limit_bytes=32 * 1024 * 1024),
+        compiler_params=pltpu.CompilerParams(vmem_limit_bytes=VMEM_LIMIT),
     )(*args)
 
 
@@ -450,16 +483,8 @@
     return route(value, lambda i, j: (i ^ 1, j))
 
 
-def window(value):
-    value = value + swap(value)
-    left = route(value, lambda i, j: (i + 2, j))
-    right = route(value, lambda i, j: (i - 2, j))
-    far = route(value, lambda i, j: (i + (-4 if i % 2 else 4), j))
-    value = (left + right) + (far + value)
-    size = lax.axis_size("gy")
-    copies = jnp.tile(value, (size, 1))
-    copies = lax.all_to_all(copies, "gy", 0, 0, tiled=True)
-    return jnp.sum(copies.reshape((size,) + value.shape), 0)
+def exchange(rows):
+    return lax.all_to_all(rows, ("gx", "gy"), 0, 0, tiled=True)
 
 
 def merge(value, parts):
@@ -539,30 +564,31 @@
     (spots,) = call(area_kernel, [(NTURB,) + flat], [], cell_x, cell_yz, area)
 
     s, v, rotor = [None] * 5, [None] * 5, [None] * 5
-    s[1], v[1], cot, sums = call(first_kernel, [full, flat, full, row], [row], *parts, spots)
+    table = (128, 128)
+    every = (count_x * count_y, 128)
+    s[1], v[1], cot, sums = call(first_kernel, [full, flat, full, every], [table], *parts, spots)
     for k in (1, 2, 3):
-        rotor[k] = window(sums) * inverse
         last = k == 3
-        outs = [full, flat, (2 * NTURB, 128) if last else row]
-        s[k + 1], v[k + 1], sums = call(
+        s[k + 1], v[k + 1], rotor[k], sums = call(
             functools.partial(forward_kernel, last),
-            outs,
-            [full] + ([flat] if last else []) + [row],
-            *([s[k], v[k], spots, rotor[k]] + ([cot] if last else [])),
+            [full, flat, row, every],
+            [full, table] + ([flat] if last else []),
+            *([s[k], v[k], spots, inverse, exchange(sums)] + ([cot] if last else [])),
         )
-    sums = window(sums)
-    rotor[4] = sums[:NTURB] * inverse
-    sums = sums[NTURB:]
     adjoint = cot
     bar, drag = [None] * 5, [None] * 5
     for k in (4, 3, 2):
-        bar[k] = (window(sums) if k < 4 else sums) * inverse
-        adjoint, drag[k - 1], sums = call(
-            backward_kernel,
-            [full, flat, row],
-            [full, row],
-            *(s[k], adjoint, spots, rotor[k], bar[k], v[k - 1]),
+        first = k == 4
+        args = [s[k], adjoint, spots, inverse, exchange(sums), v[k - 1]]
+        outs = call(
+            functools.partial(backward_kernel, first),
+            [full, flat, row, every] + ([row] if first else []),
+            [full, table],
+            *(args + ([] if first else [rotor[k]])),
         )
+        adjoint, drag[k - 1], bar[k], sums = outs[:4]
+        if first:
+            rotor[4] = outs[4]
     (points,) = call(
         gather_kernel,
         [(3 * NTURB, 128)],

time: 240 us -> 201 us (0.84)
  starting transfers between devices: 109 us -> 42.7 us
  blocking collectives: 38.1 us -> 93.2 us
  waiting for transfers between devices: 53.9 us -> 38.3 us
  local copies, waits for them, and re-layouts: 18.4 us -> 5.61 us
    ppermute x36 -> x12, starting transfers between devices: 95.7 us -> 12.7 us  [route(): return lax.ppermute(value, ('gx', 'gy'), pairs)]
    all_to_all x5, blocking collectives: 38.1 us -> 93.2 us  [exchange(): return lax.all_to_all(rows, ('gx', 'gy'), 0, 0, tiled=True)]
    ppermute x36 -> x12, waiting for transfers between devices: 41 us -> 16 us  [route(): return lax.ppermute(value, ('gx', 'gy'), pairs)]
    all_to_all x1, starting transfers between devices: 4.76 us -> 21.8 us  [exchange(): return lax.all_to_all(rows, ('gx', 'gy'), 0, 0, tiled=True)]
    unnamed x40 -> x16, local copies, waits for them, and re-layouts: 15.5 us -> 3.4 us
    all_to_all x1, waiting for transfers between devices: 5.19 us -> 12.6 us  [exchange(): return lax.all_to_all(rows, ('gx', 'gy'), 0, 0, tiled=True)]
  transfers between devices with their start and end apart: 41 -> 17, of which waited for: 30 -> 12; matrix products, arithmetic and copies ran while one was open for 0% -> 0% of each run, Pallas kernels for 1% -> 1%
where the time goes in v1:
time: 201 us; the launch traced here: 200 us
  blocking collectives  93.2 us (46%)
  starting transfers between devices  42.7 us (21%)
  waiting for transfers between devices  38.3 us (19%)
  Pallas kernels  18.9 us (9%)
  local copies, waits for them, and re-layouts  5.61 us (3%)
    all_to_all x5, blocking collectives, exchange(): return lax.all_to_all(rows, ('gx', 'gy'), 0, 0, tiled=True)  93.2 us
    all_to_all x1, starting transfers between devices, exchange(): return lax.all_to_all(rows, ('gx', 'gy'), 0, 0, tiled=True)  21.8 us
    pallas_call x10, Pallas kernels, call(): pl.pallas_call(kernel, out_shape=[jax.ShapeDtypeStruct(shape, jnp.float32...  18.9 us
    ppermute x12, waiting for transfers between devices, route(): return lax.ppermute(value, ('gx', 'gy'), pairs)  16 us
    ppermute x12, starting transfers between devices, route(): return lax.ppermute(value, ('gx', 'gy'), pairs)  12.7 us
    all_to_all x1, waiting for transfers between devices, exchange(): return lax.all_to_all(rows, ('gx', 'gy'), 0, 0, tiled=True)  12.6 us
    ppermute x4, waiting for transfers between devices, shift(): lax.ppermute(value, axis, [(i, (i + step) % size) for i in range(size)])  9.81 us
    ppermute x4, starting transfers between devices, shift(): lax.ppermute(value, axis, [(i, (i + step) % size) for i in range(size)])  8.21 us
  transfers between devices with their start and end apart: 17, of which 12 were waited for; matrix products, arithmetic and copies ran while one was open for 0% of the time, Pallas kernels for 1%

profile of v1, /device:TPU:1, one launch (start us, length us, event | category | flops | bytes accessed | tf_op | source)
XLA Modules:
  0.0 200.1 jit_solution(3216341041112091857)
XLA Ops:
  1.7 5.0 %collective-permute-start.1 = (f32[38,8,128]{2,1,0:T(8,128)S(1)}, f32[38,8,128]{2,1,0:T(8,128)S(1)}, u32[]{:S(2)}, u32[]{:S(2)}) collective-permute-start(f32[38,8,128]{2,1,0:T(8,128)S(1)} %pad_maximum_fusion.2), channel_id=1, source_target_pairs={{0,7},{1,0},{2,1},{3,2},{4,3},{5,4},{6,5},{7,6},{8,15},{9,8},{10,9... | collective-permute-start | bytes 466952 | tf_op jit(solution)/shard_map/ppermute | solution.py:529
  9.4 4.1 %collective-permute-done = f32[38,8,128]{2,1,0:T(8,128)S(1)} collective-permute-done((f32[38,8,128]{2,1,0:T(8,128)S(1)}, f32[38,8,128]{2,1,0:T(8,128)S(1)}, u32[]{:S(2)}, u32[]{:S(2)}) %collective-permute-start) | collective-permute-done | bytes 155680 | tf_op jit(solution)/shard_map/ppermute | solution.py:529
  13.5 1.9 collective-permute-start.3
  16.8 2.9 %shard_map.77.area_ref = f32[16,24,512]{2,1,0:T(8,128)S(1)} custom-call(s32[16,96]{1,0:T(8,128)S(1)} %fusion.21.x_ref, s32[16,96]{1,0:T(8,128)S(1)} %get-tuple-element.59.yz_ref, f32[16,96]{1,0:T(8,128)S(1)} %reshape.66.area_ref), custom_call_target="tpu_custom_call" | custom-call | tf_op jit(solution)/shard_map/pallas_call | solution.py:461
  19.7 4.8 %collective-permute-done.3.after_ref = f32[38,8,512]{2,1,0:T(8,128)S(1)} collective-permute-done((f32[38,8,512]{2,1,0:T(8,128)S(1)}, f32[38,8,512]{2,1,0:T(8,128)S(1)}, u32[]{:S(2)}, u32[]{:S(2)}) %collective-permute-start.3) | collective-permute-done | bytes 622624 | tf_op jit(solution)/shard_map/ppermute | solution.py:529
  25.8 21.8 %all-to-all-start = ((f32[256,1,128]{2,1,0:T(1,128)}), f32[256,1,128]{2,1,0:T(1,128)S(1)}, u32[]{:S(2)}, u32[]{:S(2)}) async-start(f32[256,1,128]{2,1,0:T(1,128)} %bitcast.1), calls=%async_computation | async-start | bytes 262144 | tf_op jit(solution)/shard_map/all_to_all | solution.py:487
  47.8 12.6 %all-to-all-done = f32[256,1,128]{2,1,0:T(1,128)S(1)} async-done(((f32[256,1,128]{2,1,0:T(1,128)}), f32[256,1,128]{2,1,0:T(1,128)S(1)}, u32[]{:S(2)}, u32[]{:S(2)}) %all-to-all-start) | async-done | bytes 131104 | tf_op jit(solution)/shard_map/all_to_all | solution.py:487
  61.9 18.6 %all_to_all.66 = f32[256,1,128]{2,1,0:T(1,128)S(1)} all-to-all(f32[256,1,128]{2,1,0:T(1,128)S(1)} %bitcast.32), channel_id=1, replica_groups=mesh['gx'=32,'gy'=8] {'gx','gy'}, dimensions={0} | all-to-all | bytes 262144 | tf_op jit(solution)/shard_map/all_to_all | solution.py:487
  82.0 18.6 %all_to_all.67 = f32[256,1,128]{2,1,0:T(1,128)S(1)} all-to-all(f32[256,1,128]{2,1,0:T(1,128)S(1)} %bitcast.33), channel_id=1, replica_groups=mesh['gx'=32,'gy'=8] {'gx','gy'}, dimensions={0} | all-to-all | bytes 262144 | tf_op jit(solution)/shard_map/all_to_all | solution.py:487
  100.6 1.6 shard_map.81
  102.2 18.6 %all_to_all.68 = f32[256,1,128]{2,1,0:T(1,128)S(1)} all-to-all(f32[256,1,128]{2,1,0:T(1,128)S(1)} %bitcast.34), channel_id=1, replica_groups=mesh['gx'=32,'gy'=8] {'gx','gy'}, dimensions={0} | all-to-all | bytes 262144 | tf_op jit(solution)/shard_map/all_to_all | solution.py:487
  120.8 1.7 shard_map.82
  122.5 18.8 %all_to_all.69 = f32[256,1,128]{2,1,0:T(1,128)S(1)} all-to-all(f32[256,1,128]{2,1,0:T(1,128)S(1)} %bitcast.30), channel_id=1, replica_groups=mesh['gx'=32,'gy'=8] {'gx','gy'}, dimensions={0} | all-to-all | bytes 262144 | tf_op jit(solution)/shard_map/all_to_all | solution.py:487
  141.3 1.7 shard_map.83
  143.0 18.6 %all_to_all.70 = f32[256,1,128]{2,1,0:T(1,128)S(1)} all-to-all(f32[256,1,128]{2,1,0:T(1,128)S(1)} %bitcast.31), channel_id=1, replica_groups=mesh['gx'=32,'gy'=8] {'gx','gy'}, dimensions={0} | all-to-all | bytes 262144 | tf_op jit(solution)/shard_map/all_to_all | solution.py:487
  161.6 2.4 %shard_map.84 = (f32[19,24,512]{2,1,0:T(8,128)S(1)}, f32[24,512]{1,0:T(8,128)S(1)}, f32[16,128]{1,0:T(8,128)S(1)}, f32[256,128]{1,0:T(8,128)}) custom-call(f32[19,24,512]{2,1,0:T(8,128)S(1)} %get-tuple-element.33.s_ref, f32[19,24,512]{2,1,0:T(8,128)S(1)} %get-tuple-element.45.a_ref, f32[16,24,512]{2,1,0:T(8,128)S(1)} %shard_map.77.area_ref, ...), custom_call_target="tpu_custom_call" | custom-call | tf_op jit(solution)/shard_map/pallas_call | solution.py:461
  164.9 2.5 %shard_map.85 = f32[48,128]{1,0:T(8,128)S(1)} custom-call(s32[16,96]{1,0:T(8,128)S(1)} %fusion.21.x_ref, s32[16,96]{1,0:T(8,128)S(1)} %get-tuple-element.58.yz_ref, f32[19,24,512]{2,1,0:T(8,128)S(1)} %get-tuple-element.39.rest_0_.a_ref.cot_ref, f32[24,512]{1,0:T(8,128)S(1)} %get-tuple-element.50.q1, f32[24,512]{1,0:T(8,128)S(1)} %get-tuple-element.51.q2, ...), custom_call_target="tpu_custom_call" | custom-call | tf_op jit(solution)/shard_map/pallas_call | solution.py:461
  170.9 2.3 %collective-permute-start.6 = (f32[48,128]{1,0:T(8,128)S(1)}, f32[48,128]{1,0:T(8,128)S(1)}, u32[]{:S(2)}, u32[]{:S(2)}) collective-permute-start(f32[48,128]{1,0:T(8,128)S(1)} %compare_select_fusion.11), channel_id=1, source_target_pairs={{0,3},{1,0},{2,1},{3,2},{4,7},{5,4},{6,5},{7,6},{8,15},{9,12},{10,... | collective-permute-start | bytes 73736 | tf_op jit(solution)/shard_map/ppermute | solution.py:479
  174.7 3.2 %collective-permute-done.5 = f32[48,128]{1,0:T(8,128)S(1)} collective-permute-done((f32[48,128]{1,0:T(8,128)S(1)}, f32[48,128]{1,0:T(8,128)S(1)}, u32[]{:S(2)}, u32[]{:S(2)}) %collective-permute-start.5) | collective-permute-done | bytes 24608 | tf_op jit(solution)/shard_map/ppermute | solution.py:479
  180.3 3.2 %collective-permute-done.10 = f32[48,128]{1,0:T(8,128)S(1)} collective-permute-done((f32[48,128]{1,0:T(8,128)S(1)}, f32[48,128]{1,0:T(8,128)S(1)}, u32[]{:S(2)}, u32[]{:S(2)}) %collective-permute-start.10) | collective-permute-done | bytes 24608 | tf_op jit(solution)/shard_map/ppermute | solution.py:479
  183.5 2.7 %collective-permute-start.12 = (f32[48,128]{1,0:T(8,128)S(1)}, f32[48,128]{1,0:T(8,128)S(1)}, u32[]{:S(2)}, u32[]{:S(2)}) collective-permute-start(f32[48,128]{1,0:T(8,128)S(1)} %compare_select_fusion.4), channel_id=1, source_target_pairs={{0,8},{1,9},{2,10},{3,11},{4,12},{5,13},{6,14},{7,15},{8,0},{9,1},... | collective-permute-start | bytes 73736 | tf_op jit(solution)/shard_map/ppermute | solution.py:479
  188.4 5.4 %collective-permute-done.13 = f32[48,128]{1,0:T(8,128)S(1)} collective-permute-done((f32[48,128]{1,0:T(8,128)S(1)}, f32[48,128]{1,0:T(8,128)S(1)}, u32[]{:S(2)}, u32[]{:S(2)}) %collective-permute-start.13) | collective-permute-done | bytes 24608 | tf_op jit(solution)/shard_map/ppermute | solution.py:479
  193.8 1.6 collective-permute-start.15
  198.3 1.8 shard_map.86
  (70 shorter events, 23.0 us)
Async XLA Ops:
  1.7 7.7 %collective-permute-start.1 = (f32[38,8,128]{2,1,0:T(8,128)S(1)}, f32[38,8,128]{2,1,0:T(8,128)S(1)}, u32[]{:S(2)}, u32[]{:S(2)}) collective-permute-start(f32[38,8,128]{2,1,0:T(8,128)S(1)} %pad_maximum_fusion.2), channel_id=1, source_target_pairs={{0,7},{1,0},{2,1},{3,2},{4,3},{5,4},{6,5},{7,6},{8,15},{9,8},{10,9... | collective-permute-start | bytes 466952 | tf_op jit(solution)/shard_map/ppermute | solution.py:529
  6.7 6.8 %copy-start.2 = (f32[19,8,256]{2,1,0:T(8,128)S(1)}, f32[19,8,256]{2,1,0:T(8,128)}, u32[]{:S(2)}) copy-start(f32[19,8,256]{2,1,0:T(8,128)} %param.6) | copy-start | bytes 466948
  6.7 6.8 %copy-start.3 = (f32[19,8,256]{2,1,0:T(8,128)S(1)}, f32[19,8,256]{2,1,0:T(8,128)}, u32[]{:S(2)}) copy-start(f32[19,8,256]{2,1,0:T(8,128)} %param.7) | copy-start | bytes 466948
  6.7 0.7 copy-start.4
  6.7 6.8 %collective-permute-start = (f32[38,8,128]{2,1,0:T(8,128)S(1)}, f32[38,8,128]{2,1,0:T(8,128)S(1)}, u32[]{:S(2)}, u32[]{:S(2)}) collective-permute-start(f32[38,8,128]{2,1,0:T(8,128)S(1)} %pad_maximum_fusion.1), channel_id=1, source_target_pairs={{0,1},{1,2},{2,3},{3,4},{4,5},{5,6},{6,7},{7,0},{8,9},{9,10},{10,1... | collective-permute-start | bytes 466952 | tf_op jit(solution)/shard_map/ppermute | solution.py:529
  6.8 0.7 copy-start.5
  8.5 8.2 %copy-start.7 = (s32[16]{0:T(128)S(1)}, s32[16]{0:T(128)}, u32[]{:S(2)}) copy-start(s32[16]{0:T(128)} %param.9) | copy-start | bytes 196
  13.5 11.0 %collective-permute-start.3 = (f32[38,8,512]{2,1,0:T(8,128)S(1)}, f32[38,8,512]{2,1,0:T(8,128)S(1)}, u32[]{:S(2)}, u32[]{:S(2)}) collective-permute-start(f32[38,8,512]{2,1,0:T(8,128)S(1)} %pad_maximum_fusion.own_ref), channel_id=1, source_target_pairs={{0,248},{8,0},{16,8},{24,16},{32,24},{40,32},{48,40},{56,48},{64,5... | collective-permute-start | bytes 1867784 | tf_op jit(solution)/shard_map/ppermute | solution.py:529
  15.5 9.0 %collective-permute-start.2 = (f32[38,8,512]{2,1,0:T(8,128)S(1)}, f32[38,8,512]{2,1,0:T(8,128)S(1)}, u32[]{:S(2)}, u32[]{:S(2)}) collective-permute-start(f32[38,8,512]{2,1,0:T(8,128)S(1)} %pad_maximum_fusion.own_ref), channel_id=1, source_target_pairs={{0,8},{8,16},{16,24},{24,32},{32,40},{40,48},{48,56},{56,64},{64,7... | collective-permute-start | bytes 1867784 | tf_op jit(solution)/shard_map/ppermute | solution.py:529
  25.8 34.5 %all-to-all-start = ((f32[256,1,128]{2,1,0:T(1,128)}), f32[256,1,128]{2,1,0:T(1,128)S(1)}, u32[]{:S(2)}, u32[]{:S(2)}) async-start(f32[256,1,128]{2,1,0:T(1,128)} %bitcast.1), calls=%async_computation | async-start | bytes 262144 | tf_op jit(solution)/shard_map/all_to_all | solution.py:487
  164.0 0.9 copy-start
  167.5 2.1 %collective-permute-start.4 = (f32[48,128]{1,0:T(8,128)S(1)}, f32[48,128]{1,0:T(8,128)S(1)}, u32[]{:S(2)}, u32[]{:S(2)}) collective-permute-start(f32[48,128]{1,0:T(8,128)S(1)} %shard_map.85), channel_id=1, source_target_pairs={{0,8},{1,9},{2,10},{3,11},{4,12},{5,13},{6,14},{7,15},{8,0},{9,1},... | collective-permute-start | bytes 73736 | tf_op jit(solution)/shard_map/ppermute | solution.py:479
  169.5 5.2 %collective-permute-start.7 = (f32[48,128]{1,0:T(8,128)S(1)}, f32[48,128]{1,0:T(8,128)S(1)}, u32[]{:S(2)}, u32[]{:S(2)}) collective-permute-start(f32[48,128]{1,0:T(8,128)S(1)} %compare_select_fusion.11), channel_id=1, source_target_pairs={{0,2},{1,3},{2,0},{3,1},{4,6},{5,7},{6,4},{7,5},{8,14},{9,15},{10,... | collective-permute-start | bytes 73736 | tf_op jit(solution)/shard_map/ppermute | solution.py:479
  170.9 3.9 %collective-permute-start.6 = (f32[48,128]{1,0:T(8,128)S(1)}, f32[48,128]{1,0:T(8,128)S(1)}, u32[]{:S(2)}, u32[]{:S(2)}) collective-permute-start(f32[48,128]{1,0:T(8,128)S(1)} %compare_select_fusion.11), channel_id=1, source_target_pairs={{0,3},{1,0},{2,1},{3,2},{4,7},{5,4},{6,5},{7,6},{8,15},{9,12},{10,... | collective-permute-start | bytes 73736 | tf_op jit(solution)/shard_map/ppermute | solution.py:479
  173.2 4.8 %collective-permute-start.5 = (f32[48,128]{1,0:T(8,128)S(1)}, f32[48,128]{1,0:T(8,128)S(1)}, u32[]{:S(2)}, u32[]{:S(2)}) collective-permute-start(f32[48,128]{1,0:T(8,128)S(1)} %compare_select_fusion.11), channel_id=1, source_target_pairs={{0,1},{1,2},{2,3},{3,0},{4,5},{5,6},{6,7},{7,4},{8,13},{9,14},{10,... | collective-permute-start | bytes 73736 | tf_op jit(solution)/shard_map/ppermute | solution.py:479
  173.2 4.7 %collective-permute-start.8 = (f32[48,128]{1,0:T(8,128)S(1)}, f32[48,128]{1,0:T(8,128)S(1)}, u32[]{:S(2)}, u32[]{:S(2)}) collective-permute-start(f32[48,128]{1,0:T(8,128)S(1)} %compare_select_fusion.11), channel_id=1, source_target_pairs={{0,4},{1,5},{2,6},{3,7},{4,0},{5,1},{6,2},{7,3},{8,12},{9,13},{10,... | collective-permute-start | bytes 73736 | tf_op jit(solution)/shard_map/ppermute | solution.py:479
  178.0 1.3 collective-permute-start.9
  179.3 4.2 %collective-permute-start.10 = (f32[48,128]{1,0:T(8,128)S(1)}, f32[48,128]{1,0:T(8,128)S(1)}, u32[]{:S(2)}, u32[]{:S(2)}) collective-permute-start(f32[48,128]{1,0:T(8,128)S(1)} %compare_select_fusion.6), channel_id=1, source_target_pairs={{0,16},{1,17},{2,18},{3,19},{4,20},{5,21},{6,22},{7,23},{8,40},{9,... | collective-permute-start | bytes 73736 | tf_op jit(solution)/shard_map/ppermute | solution.py:479
  179.6 3.8 %collective-permute-start.11 = (f32[48,128]{1,0:T(8,128)S(1)}, f32[48,128]{1,0:T(8,128)S(1)}, u32[]{:S(2)}, u32[]{:S(2)}) collective-permute-start(f32[48,128]{1,0:T(8,128)S(1)} %compare_select_fusion.6), channel_id=1, source_target_pairs={{0,48},{1,49},{2,50},{3,51},{4,52},{5,53},{6,54},{7,55},{16,0},{17... | collective-permute-start | bytes 73736 | tf_op jit(solution)/shard_map/ppermute | solution.py:479
  183.5 3.6 %collective-permute-start.12 = (f32[48,128]{1,0:T(8,128)S(1)}, f32[48,128]{1,0:T(8,128)S(1)}, u32[]{:S(2)}, u32[]{:S(2)}) collective-permute-start(f32[48,128]{1,0:T(8,128)S(1)} %compare_select_fusion.4), channel_id=1, source_target_pairs={{0,8},{1,9},{2,10},{3,11},{4,12},{5,13},{6,14},{7,15},{8,0},{9,1},... | collective-permute-start | bytes 73736 | tf_op jit(solution)/shard_map/ppermute | solution.py:479
  187.0 6.8 %collective-permute-start.13 = (f32[48,128]{1,0:T(8,128)S(1)}, f32[48,128]{1,0:T(8,128)S(1)}, u32[]{:S(2)}, u32[]{:S(2)}) collective-permute-start(f32[48,128]{1,0:T(8,128)S(1)} %compare_select_fusion.3), channel_id=1, source_target_pairs={{0,64},{1,65},{2,66},{3,67},{4,68},{5,69},{6,70},{7,71},{8,136},{9... | collective-permute-start | bytes 73736 | tf_op jit(solution)/shard_map/ppermute | solution.py:479
  187.7 6.1 %collective-permute-start.14 = (f32[48,128]{1,0:T(8,128)S(1)}, f32[48,128]{1,0:T(8,128)S(1)}, u32[]{:S(2)}, u32[]{:S(2)}) collective-permute-start(f32[48,128]{1,0:T(8,128)S(1)} %compare_select_fusion.3), channel_id=1, source_target_pairs={{0,192},{1,193},{2,194},{3,195},{4,196},{5,197},{6,198},{7,199},{1... | collective-permute-start | bytes 73736 | tf_op jit(solution)/shard_map/ppermute | solution.py:479
  193.8 2.4 %collective-permute-start.15 = (f32[48,128]{1,0:T(8,128)S(1)}, f32[48,128]{1,0:T(8,128)S(1)}, u32[]{:S(2)}, u32[]{:S(2)}) collective-permute-start(f32[48,128]{1,0:T(8,128)S(1)} %compare_select_fusion.1), channel_id=1, source_target_pairs={{0,8},{1,9},{2,10},{3,11},{4,12},{5,13},{6,14},{7,15},{8,0},{9,1},... | collective-permute-start | bytes 73736 | tf_op jit(solution)/shard_map/ppermute | solution.py:479
  197.1 1.2 copy-start.1
  (1 other events, 0.7 us)

commit v2 on v1

--- a/solution.py
+++ b/solution.py
@@ -334,23 +334,64 @@
     lax.fori_loop(0, NTURB, one, 0)
 
 
+def pack_x_kernel(field_ref, cot_ref, next_ref, prev_ref):
+    half = OWN_SPAN // 2
+    top = lax.broadcasted_iota(jnp.int32, (CX, half), 0) < CX // 2
+    for i in range(19):
+        low, high = cot_ref[i, :, :half], cot_ref[i, :, half:]
+        next_ref[i, :, :OWN_SPAN] = field_ref[i]
+        prev_ref[i, :, :OWN_SPAN] = field_ref[i]
+        next_ref[i, :, OWN_SPAN:] = jnp.where(top, pltpu.roll(low, CX // 2, 0), high)
+        prev_ref[i, :, OWN_SPAN:] = jnp.where(top, low, pltpu.roll(high, CX // 2, 0))
+
+
+def pack_y_kernel(field_ref, cot_ref, before_ref, after_ref, fields_ref, cots_ref, next_ref, prev_ref):
+    half = OWN_SPAN // 2
+    top = lax.broadcasted_iota(jnp.int32, (CX, half), 0) < CX // 2
+    left = lax.broadcasted_iota(jnp.int32, (CX, half), 1) < half // 2
+    for i in range(19):
+        for j, part in enumerate((before_ref[i, :, :OWN_SPAN], field_ref[i], after_ref[i, :, :OWN_SPAN])):
+            rows = slice(CX * j, CX * (j + 1))
+            fields_ref[i, rows] = part
+            prev_ref[i, rows] = part[:, :half]
+            next_ref[i, rows] = part[:, half:]
+        before, after = before_ref[i, :, OWN_SPAN:], after_ref[i, :, OWN_SPAN:]
+        low = (pltpu.roll(before, CX // 2, 0), cot_ref[i, :, :half], after)
+        high = (before, cot_ref[i, :, half:], pltpu.roll(after, CX // 2, 0))
+        for j in range(3):
+            rows = slice(CX * j, CX * (j + 1))
+            cots_ref[i, rows, :half] = low[j]
+            cots_ref[i, rows, half:] = high[j]
+        outer = jnp.where(top, low[2], low[0])
+        prev_ref[i, RX:] = jnp.where(left, low[1], pltpu.roll(outer, half // 2, 1))
+        outer = jnp.where(top, high[2], high[0])
+        next_ref[i, RX:] = jnp.where(left, pltpu.roll(high[1], half // 2, 1), outer)
+
+
 class Joined:
-    def __init__(self, *parts):
-        self.parts = parts
+    def __init__(self, before, here, after):
+        self.parts = before, here, after
 
     def __getitem__(self, index):
-        return jnp.concatenate([part[index] for part in self.parts], axis=0)
-
-
-def first_kernel(before_ref, own_ref, after_ref, area_ref, s_ref, v_ref, cot_ref, out_ref, sums):
-    both = Joined(before_ref, own_ref, after_ref)
-    stream(both, s_ref)
+        before, here, after = self.parts
+        return jnp.concatenate([before[index, :RX], here[index], after[index, :RX]], axis=1)
+
+
+def first_kernel(before_ref, fields_ref, after_ref, cots_ref, area_ref, s_ref, v_ref, cot_ref, out_ref, sums):
+    stream(Joined(before_ref, fields_ref, after_ref), s_ref)
     speeds(s_ref, v_ref)
     sums[...] = jnp.zeros_like(sums)
     turbine_sums(area_ref, v_ref, sums, 0)
     publish(sums, out_ref)
+    half = OWN_SPAN // 2
     for i in range(19):
-        cot_ref[i] = both[19 + i]
+        before, after = before_ref[i, RX:], after_ref[i, RX:]
+        turned = pltpu.roll(before, half // 2, 1), pltpu.roll(after, half // 2, 1)
+        for j in range(3):
+            rows = slice(CX * j, CX * (j + 1))
+            cot_ref[i, rows, :OWN_LANE] = turned[0] if j == 1 else before
+            cot_ref[i, rows, OWN_LANE + OWN_SPAN :] = after if j == 1 else turned[1]
+        cot_ref[i, :, OWN_LANE : OWN_LANE + OWN_SPAN] = cots_ref[i]
 
 
 def forward_kernel(last, s_ref, v_ref, area_ref, inv_ref, got_ref, *rest):
@@ -530,14 +571,14 @@
 
 
 def region(checkpoint, cotangent):
-    edge = MARGIN * NZ
-    span = checkpoint.shape[2]
-    first = jnp.concatenate([checkpoint[:, :, :edge], cotangent[:, :, :edge]], axis=0)
-    last = jnp.concatenate([checkpoint[:, :, span - edge :], cotangent[:, :, span - edge :]], axis=0)
-    before, after = shift(last, "gy", 1), shift(first, "gy", -1)
-    own = jnp.concatenate([checkpoint, cotangent], axis=0)
-    own = jnp.concatenate([before, own, after], axis=2)
-    return shift(own, "gx", 1), own, shift(own, "gx", -1)
+    wide = (19, CX, OWN_SPAN + OWN_SPAN // 2)
+    right, left = call(pack_x_kernel, [wide] * 2, [], checkpoint, cotangent)
+    before, after = shift(right, "gx", 1), shift(left, "gx", -1)
+    stack, edge = (19, RX, OWN_SPAN), (19, RX + CX, OWN_SPAN // 2)
+    fields, cots, right, left = call(
+        pack_y_kernel, [stack, stack, edge, edge], [], checkpoint, cotangent, before, after
+    )
+    return shift(right, "gy", 1), fields, shift(left, "gy", -1), cots
 
 
 def body(checkpoint, cotangent, blade_area, hub_tile, point_side, point_local):

time: 201 us -> 197 us (0.980)
  starting transfers between devices: 42.7 us -> 37.2 us
  local copies, waits for them, and re-layouts: 5.61 us -> 10 us
  waiting for transfers between devices: 38.3 us -> 35.2 us
    unnamed x16 -> x30, local copies, waits for them, and re-layouts: 3.4 us -> 8.86 us
    all_to_all x1, starting transfers between devices: 21.8 us -> 17 us  [exchange(): return lax.all_to_all(rows, ('gx', 'gy'), 0, 0, tiled=True)]
    ppermute x4, waiting for transfers between devices: 9.81 us -> 6.85 us  [shift(): lax.ppermute(value, axis, [(i, (i + step) % size) for i in range(size)])]
    pallas_call x10 -> x12, Pallas kernels: 18.9 us -> 18.5 us  [call(): pl.pallas_call(kernel, out_shape=[jax.ShapeDtypeStruct(shape, jnp.float32...]
  transfers between devices with their start and end apart: 17 -> 17, of which waited for: 12 -> 11; matrix products, arithmetic and copies ran while one was open for 0% -> 1% of each run, Pallas kernels for 1% -> 1%
where the time goes in v2:
time: 197 us; the launch traced here: 196 us
  blocking collectives  93.2 us (47%)
  starting transfers between devices  37.2 us (19%)
  waiting for transfers between devices  35.2 us (18%)
  Pallas kernels  18.5 us (9%)
  local copies, waits for them, and re-layouts  10 us (5%)
    all_to_all x5, blocking collectives, exchange(): return lax.all_to_all(rows, ('gx', 'gy'), 0, 0, tiled=True)  93.2 us
    pallas_call x12, Pallas kernels, call(): pl.pallas_call(kernel, out_shape=[jax.ShapeDtypeStruct(shape, jnp.float32...  18.5 us
    all_to_all x1, starting transfers between devices, exchange(): return lax.all_to_all(rows, ('gx', 'gy'), 0, 0, tiled=True)  17 us
    ppermute x12, waiting for transfers between devices, route(): return lax.ppermute(value, ('gx', 'gy'), pairs)  16 us
    ppermute x12, starting transfers between devices, route(): return lax.ppermute(value, ('gx', 'gy'), pairs)  12.7 us
    all_to_all x1, waiting for transfers between devices, exchange(): return lax.all_to_all(rows, ('gx', 'gy'), 0, 0, tiled=True)  12.4 us
    unnamed x30, local copies, waits for them, and re-layouts  8.86 us
    ppermute x4, starting transfers between devices, shift(): lax.ppermute(value, axis, [(i, (i + step) % size) for i in range(size)])  7.51 us
  transfers between devices with their start and end apart: 17, of which 11 were waited for; matrix products, arithmetic and copies ran while one was open for 1% of the time, Pallas kernels for 1%

profile of v2, /device:TPU:1, one launch (start us, length us, event | category | flops | bytes accessed | tf_op | source)
XLA Modules:
  0.0 196.1 jit_solution(9137898578236404445)
XLA Ops:
  2.5 2.7 %collective-permute-start = (f32[19,8,384]{2,1,0:T(8,128)S(1)}, f32[19,8,384]{2,1,0:T(8,128)S(1)}, u32[]{:S(2)}, u32[]{:S(2)}) collective-permute-start(f32[19,8,384]{2,1,0:T(8,128)S(1)} %get-tuple-element.36), channel_id=1, source_target_pairs={{0,8},{8,16},{16,24},{24,32},{32,40},{40,48},{48,56},{56,64},{64,7... | collective-permute-start | bytes 700424 | tf_op jit(solution)/shard_map/ppermute | solution.py:570
  8.2 2.5 %collective-permute-done.1.after_ref = f32[19,8,384]{2,1,0:T(8,128)S(1)} collective-permute-done((f32[19,8,384]{2,1,0:T(8,128)S(1)}, f32[19,8,384]{2,1,0:T(8,128)S(1)}, u32[]{:S(2)}, u32[]{:S(2)}) %collective-permute-start.1) | collective-permute-done | bytes 233504 | tf_op jit(solution)/shard_map/ppermute | solution.py:570
  12.9 2.8 %collective-permute-start.3 = (f32[19,32,128]{2,1,0:T(8,128)S(1)}, f32[19,32,128]{2,1,0:T(8,128)S(1)}, u32[]{:S(2)}, u32[]{:S(2)}) collective-permute-start(f32[19,32,128]{2,1,0:T(8,128)S(1)} %get-tuple-element.40), channel_id=1, source_target_pairs={{0,7},{1,0},{2,1},{3,2},{4,3},{5,4},{6,5},{7,6},{8,15},{9,8},{10,9... | collective-permute-start | bytes 933896 | tf_op jit(solution)/shard_map/ppermute | solution.py:570
  16.5 2.9 %shard_map.79.area_ref = f32[16,24,512]{2,1,0:T(8,128)S(1)} custom-call(s32[16,96]{1,0:T(8,128)S(1)} %fusion.21.x_ref, s32[16,96]{1,0:T(8,128)S(1)} %get-tuple-element.71.yz_ref, f32[16,96]{1,0:T(8,128)S(1)} %reshape.66.area_ref), custom_call_target="tpu_custom_call" | custom-call | tf_op jit(solution)/shard_map/pallas_call | solution.py:502
  19.4 4.3 %collective-permute-done.2.before_ref = f32[19,32,128]{2,1,0:T(8,128)S(1)} collective-permute-done((f32[19,32,128]{2,1,0:T(8,128)S(1)}, f32[19,32,128]{2,1,0:T(8,128)S(1)}, u32[]{:S(2)}, u32[]{:S(2)}) %collective-permute-start.2) | collective-permute-done | bytes 311328 | tf_op jit(solution)/shard_map/ppermute | solution.py:570
  26.8 17.0 %all-to-all-start = ((f32[256,1,128]{2,1,0:T(1,128)}), f32[256,1,128]{2,1,0:T(1,128)S(1)}, u32[]{:S(2)}, u32[]{:S(2)}) async-start(f32[256,1,128]{2,1,0:T(1,128)} %bitcast.30), calls=%async_computation | async-start | bytes 262144 | tf_op jit(solution)/shard_map/all_to_all | solution.py:528
  43.9 12.4 %all-to-all-done = f32[256,1,128]{2,1,0:T(1,128)S(1)} async-done(((f32[256,1,128]{2,1,0:T(1,128)}), f32[256,1,128]{2,1,0:T(1,128)S(1)}, u32[]{:S(2)}, u32[]{:S(2)}) %all-to-all-start) | async-done | bytes 131104 | tf_op jit(solution)/shard_map/all_to_all | solution.py:528
  57.9 18.6 %all_to_all.66 = f32[256,1,128]{2,1,0:T(1,128)S(1)} all-to-all(f32[256,1,128]{2,1,0:T(1,128)S(1)} %bitcast.33), channel_id=1, replica_groups=mesh['gx'=32,'gy'=8] {'gx','gy'}, dimensions={0} | all-to-all | bytes 262144 | tf_op jit(solution)/shard_map/all_to_all | solution.py:528
  78.0 18.6 %all_to_all.67 = f32[256,1,128]{2,1,0:T(1,128)S(1)} all-to-all(f32[256,1,128]{2,1,0:T(1,128)S(1)} %bitcast.34), channel_id=1, replica_groups=mesh['gx'=32,'gy'=8] {'gx','gy'}, dimensions={0} | all-to-all | bytes 262144 | tf_op jit(solution)/shard_map/all_to_all | solution.py:528
  96.6 1.6 shard_map.83
  98.2 18.6 %all_to_all.68 = f32[256,1,128]{2,1,0:T(1,128)S(1)} all-to-all(f32[256,1,128]{2,1,0:T(1,128)S(1)} %bitcast.35), channel_id=1, replica_groups=mesh['gx'=32,'gy'=8] {'gx','gy'}, dimensions={0} | all-to-all | bytes 262144 | tf_op jit(solution)/shard_map/all_to_all | solution.py:528
  116.8 1.7 shard_map.84
  118.5 18.8 %all_to_all.69 = f32[256,1,128]{2,1,0:T(1,128)S(1)} all-to-all(f32[256,1,128]{2,1,0:T(1,128)S(1)} %bitcast.31), channel_id=1, replica_groups=mesh['gx'=32,'gy'=8] {'gx','gy'}, dimensions={0} | all-to-all | bytes 262144 | tf_op jit(solution)/shard_map/all_to_all | solution.py:528
  137.3 1.7 shard_map.85
  139.0 18.6 %all_to_all.70 = f32[256,1,128]{2,1,0:T(1,128)S(1)} all-to-all(f32[256,1,128]{2,1,0:T(1,128)S(1)} %bitcast.32), channel_id=1, replica_groups=mesh['gx'=32,'gy'=8] {'gx','gy'}, dimensions={0} | all-to-all | bytes 262144 | tf_op jit(solution)/shard_map/all_to_all | solution.py:528
  157.6 2.4 %shard_map.86 = (f32[19,24,512]{2,1,0:T(8,128)S(1)}, f32[24,512]{1,0:T(8,128)S(1)}, f32[16,128]{1,0:T(8,128)S(1)}, f32[256,128]{1,0:T(8,128)}) custom-call(f32[19,24,512]{2,1,0:T(8,128)S(1)} %get-tuple-element.45.s_ref, f32[19,24,512]{2,1,0:T(8,128)S(1)} %get-tuple-element.57.a_ref, f32[16,24,512]{2,1,0:T(8,128)S(1)} %shard_map.79.area_ref, ...), custom_call_target="tpu_custom_call" | custom-call | tf_op jit(solution)/shard_map/pallas_call | solution.py:502
  160.9 2.5 %shard_map.87 = f32[48,128]{1,0:T(8,128)S(1)} custom-call(s32[16,96]{1,0:T(8,128)S(1)} %fusion.21.x_ref, s32[16,96]{1,0:T(8,128)S(1)} %get-tuple-element.70.yz_ref, f32[19,24,512]{2,1,0:T(8,128)S(1)} %get-tuple-element.51.rest_0_.a_ref.cot_ref, f32[24,512]{1,0:T(8,128)S(1)} %get-tuple-element.62.q1, f32[24,512]{1,0:T(8,128)S(1)} %get-tuple-element.63.q2, ...), custom_call_target="tpu_custom_call" | custom-call | tf_op jit(solution)/shard_map/pallas_call | solution.py:502
  166.9 2.3 %collective-permute-start.6 = (f32[48,128]{1,0:T(8,128)S(1)}, f32[48,128]{1,0:T(8,128)S(1)}, u32[]{:S(2)}, u32[]{:S(2)}) collective-permute-start(f32[48,128]{1,0:T(8,128)S(1)} %compare_select_fusion.11), channel_id=1, source_target_pairs={{0,3},{1,0},{2,1},{3,2},{4,7},{5,4},{6,5},{7,6},{8,15},{9,12},{10,... | collective-permute-start | bytes 73736 | tf_op jit(solution)/shard_map/ppermute | solution.py:520
  170.7 3.2 %collective-permute-done.5 = f32[48,128]{1,0:T(8,128)S(1)} collective-permute-done((f32[48,128]{1,0:T(8,128)S(1)}, f32[48,128]{1,0:T(8,128)S(1)}, u32[]{:S(2)}, u32[]{:S(2)}) %collective-permute-start.5) | collective-permute-done | bytes 24608 | tf_op jit(solution)/shard_map/ppermute | solution.py:520
  176.3 3.2 %collective-permute-done.10 = f32[48,128]{1,0:T(8,128)S(1)} collective-permute-done((f32[48,128]{1,0:T(8,128)S(1)}, f32[48,128]{1,0:T(8,128)S(1)}, u32[]{:S(2)}, u32[]{:S(2)}) %collective-permute-start.10) | collective-permute-done | bytes 24608 | tf_op jit(solution)/shard_map/ppermute | solution.py:520
  179.4 2.7 %collective-permute-start.12 = (f32[48,128]{1,0:T(8,128)S(1)}, f32[48,128]{1,0:T(8,128)S(1)}, u32[]{:S(2)}, u32[]{:S(2)}) collective-permute-start(f32[48,128]{1,0:T(8,128)S(1)} %compare_select_fusion.4), channel_id=1, source_target_pairs={{0,8},{1,9},{2,10},{3,11},{4,12},{5,13},{6,14},{7,15},{8,0},{9,1},... | collective-permute-start | bytes 73736 | tf_op jit(solution)/shard_map/ppermute | solution.py:520
  184.4 5.4 %collective-permute-done.13 = f32[48,128]{1,0:T(8,128)S(1)} collective-permute-done((f32[48,128]{1,0:T(8,128)S(1)}, f32[48,128]{1,0:T(8,128)S(1)}, u32[]{:S(2)}, u32[]{:S(2)}) %collective-permute-start.13) | collective-permute-done | bytes 24608 | tf_op jit(solution)/shard_map/ppermute | solution.py:520
  189.8 1.6 collective-permute-start.15
  194.3 1.8 shard_map.88
  (82 shorter events, 27.5 us)
Async XLA Ops:
  2.5 8.2 %copy-start.3 = (f32[19,8,256]{2,1,0:T(8,128)S(1)}, f32[19,8,256]{2,1,0:T(8,128)}, u32[]{:S(2)}) copy-start(f32[19,8,256]{2,1,0:T(8,128)} %field_ref.3) | copy-start | bytes 466948
  2.5 8.2 %copy-start.5 = (f32[19,8,256]{2,1,0:T(8,128)S(1)}, f32[19,8,256]{2,1,0:T(8,128)}, u32[]{:S(2)}) copy-start(f32[19,8,256]{2,1,0:T(8,128)} %cot_ref.3) | copy-start | bytes 466948
  2.5 5.7 %collective-permute-start = (f32[19,8,384]{2,1,0:T(8,128)S(1)}, f32[19,8,384]{2,1,0:T(8,128)S(1)}, u32[]{:S(2)}, u32[]{:S(2)}) collective-permute-start(f32[19,8,384]{2,1,0:T(8,128)S(1)} %get-tuple-element.36), channel_id=1, source_target_pairs={{0,8},{8,16},{16,24},{24,32},{32,40},{40,48},{48,56},{56,64},{64,7... | collective-permute-start | bytes 700424 | tf_op jit(solution)/shard_map/ppermute | solution.py:570
  5.2 1.5 copy-start.11
  5.2 5.5 %collective-permute-start.1 = (f32[19,8,384]{2,1,0:T(8,128)S(1)}, f32[19,8,384]{2,1,0:T(8,128)S(1)}, u32[]{:S(2)}, u32[]{:S(2)}) collective-permute-start(f32[19,8,384]{2,1,0:T(8,128)S(1)} %get-tuple-element.37), channel_id=1, source_target_pairs={{0,248},{8,0},{16,8},{24,16},{32,24},{40,32},{48,40},{56,48},{64,5... | collective-permute-start | bytes 700424 | tf_op jit(solution)/shard_map/ppermute | solution.py:570
  11.6 12.1 %collective-permute-start.2 = (f32[19,32,128]{2,1,0:T(8,128)S(1)}, f32[19,32,128]{2,1,0:T(8,128)S(1)}, u32[]{:S(2)}, u32[]{:S(2)}) collective-permute-start(f32[19,32,128]{2,1,0:T(8,128)S(1)} %get-tuple-element.38), channel_id=1, source_target_pairs={{0,1},{1,2},{2,3},{3,4},{4,5},{5,6},{6,7},{7,0},{8,9},{9,10},{10,1... | collective-permute-start | bytes 933896 | tf_op jit(solution)/shard_map/ppermute | solution.py:570
  12.9 10.8 %collective-permute-start.3 = (f32[19,32,128]{2,1,0:T(8,128)S(1)}, f32[19,32,128]{2,1,0:T(8,128)S(1)}, u32[]{:S(2)}, u32[]{:S(2)}) collective-permute-start(f32[19,32,128]{2,1,0:T(8,128)S(1)} %get-tuple-element.40), channel_id=1, source_target_pairs={{0,7},{1,0},{2,1},{3,2},{4,3},{5,4},{6,5},{7,6},{8,15},{9,8},{10,9... | collective-permute-start | bytes 933896 | tf_op jit(solution)/shard_map/ppermute | solution.py:570
  16.5 8.0 %copy-start.7 = (f32[19,24,256]{2,1,0:T(8,128)S(1)}, f32[19,24,256]{2,1,0:T(8,128)}, u32[]{:S(2)}) copy-start(f32[19,24,256]{2,1,0:T(8,128)} %copy-done.6) | copy-start | bytes 1400836
  24.5 1.0 copy-start.9
  26.8 29.5 %all-to-all-start = ((f32[256,1,128]{2,1,0:T(1,128)}), f32[256,1,128]{2,1,0:T(1,128)S(1)}, u32[]{:S(2)}, u32[]{:S(2)}) async-start(f32[256,1,128]{2,1,0:T(1,128)} %bitcast.30), calls=%async_computation | async-start | bytes 262144 | tf_op jit(solution)/shard_map/all_to_all | solution.py:528
  160.0 0.9 copy-start
  163.4 2.1 %collective-permute-start.4 = (f32[48,128]{1,0:T(8,128)S(1)}, f32[48,128]{1,0:T(8,128)S(1)}, u32[]{:S(2)}, u32[]{:S(2)}) collective-permute-start(f32[48,128]{1,0:T(8,128)S(1)} %shard_map.87), channel_id=1, source_target_pairs={{0,8},{1,9},{2,10},{3,11},{4,12},{5,13},{6,14},{7,15},{8,0},{9,1},... | collective-permute-start | bytes 73736 | tf_op jit(solution)/shard_map/ppermute | solution.py:520
  165.5 5.2 %collective-permute-start.7 = (f32[48,128]{1,0:T(8,128)S(1)}, f32[48,128]{1,0:T(8,128)S(1)}, u32[]{:S(2)}, u32[]{:S(2)}) collective-permute-start(f32[48,128]{1,0:T(8,128)S(1)} %compare_select_fusion.11), channel_id=1, source_target_pairs={{0,2},{1,3},{2,0},{3,1},{4,6},{5,7},{6,4},{7,5},{8,14},{9,15},{10,... | collective-permute-start | bytes 73736 | tf_op jit(solution)/shard_map/ppermute | solution.py:520
  166.9 3.9 %collective-permute-start.6 = (f32[48,128]{1,0:T(8,128)S(1)}, f32[48,128]{1,0:T(8,128)S(1)}, u32[]{:S(2)}, u32[]{:S(2)}) collective-permute-start(f32[48,128]{1,0:T(8,128)S(1)} %compare_select_fusion.11), channel_id=1, source_target_pairs={{0,3},{1,0},{2,1},{3,2},{4,7},{5,4},{6,5},{7,6},{8,15},{9,12},{10,... | collective-permute-start | bytes 73736 | tf_op jit(solution)/shard_map/ppermute | solution.py:520
  169.2 4.8 %collective-permute-start.5 = (f32[48,128]{1,0:T(8,128)S(1)}, f32[48,128]{1,0:T(8,128)S(1)}, u32[]{:S(2)}, u32[]{:S(2)}) collective-permute-start(f32[48,128]{1,0:T(8,128)S(1)} %compare_select_fusion.11), channel_id=1, source_target_pairs={{0,1},{1,2},{2,3},{3,0},{4,5},{5,6},{6,7},{7,4},{8,13},{9,14},{10,... | collective-permute-start | bytes 73736 | tf_op jit(solution)/shard_map/ppermute | solution.py:520
  169.2 4.7 %collective-permute-start.8 = (f32[48,128]{1,0:T(8,128)S(1)}, f32[48,128]{1,0:T(8,128)S(1)}, u32[]{:S(2)}, u32[]{:S(2)}) collective-permute-start(f32[48,128]{1,0:T(8,128)S(1)} %compare_select_fusion.11), channel_id=1, source_target_pairs={{0,4},{1,5},{2,6},{3,7},{4,0},{5,1},{6,2},{7,3},{8,12},{9,13},{10,... | collective-permute-start | bytes 73736 | tf_op jit(solution)/shard_map/ppermute | solution.py:520
  174.0 1.3 collective-permute-start.9
  175.3 4.2 %collective-permute-start.10 = (f32[48,128]{1,0:T(8,128)S(1)}, f32[48,128]{1,0:T(8,128)S(1)}, u32[]{:S(2)}, u32[]{:S(2)}) collective-permute-start(f32[48,128]{1,0:T(8,128)S(1)} %compare_select_fusion.6), channel_id=1, source_target_pairs={{0,16},{1,17},{2,18},{3,19},{4,20},{5,21},{6,22},{7,23},{8,40},{9,... | collective-permute-start | bytes 73736 | tf_op jit(solution)/shard_map/ppermute | solution.py:520
  175.6 3.8 %collective-permute-start.11 = (f32[48,128]{1,0:T(8,128)S(1)}, f32[48,128]{1,0:T(8,128)S(1)}, u32[]{:S(2)}, u32[]{:S(2)}) collective-permute-start(f32[48,128]{1,0:T(8,128)S(1)} %compare_select_fusion.6), channel_id=1, source_target_pairs={{0,48},{1,49},{2,50},{3,51},{4,52},{5,53},{6,54},{7,55},{16,0},{17... | collective-permute-start | bytes 73736 | tf_op jit(solution)/shard_map/ppermute | solution.py:520
  179.4 3.6 %collective-permute-start.12 = (f32[48,128]{1,0:T(8,128)S(1)}, f32[48,128]{1,0:T(8,128)S(1)}, u32[]{:S(2)}, u32[]{:S(2)}) collective-permute-start(f32[48,128]{1,0:T(8,128)S(1)} %compare_select_fusion.4), channel_id=1, source_target_pairs={{0,8},{1,9},{2,10},{3,11},{4,12},{5,13},{6,14},{7,15},{8,0},{9,1},... | collective-permute-start | bytes 73736 | tf_op jit(solution)/shard_map/ppermute | solution.py:520
  183.0 6.8 %collective-permute-start.13 = (f32[48,128]{1,0:T(8,128)S(1)}, f32[48,128]{1,0:T(8,128)S(1)}, u32[]{:S(2)}, u32[]{:S(2)}) collective-permute-start(f32[48,128]{1,0:T(8,128)S(1)} %compare_select_fusion.3), channel_id=1, source_target_pairs={{0,64},{1,65},{2,66},{3,67},{4,68},{5,69},{6,70},{7,71},{8,136},{9... | collective-permute-start | bytes 73736 | tf_op jit(solution)/shard_map/ppermute | solution.py:520
  183.7 6.1 %collective-permute-start.14 = (f32[48,128]{1,0:T(8,128)S(1)}, f32[48,128]{1,0:T(8,128)S(1)}, u32[]{:S(2)}, u32[]{:S(2)}) collective-permute-start(f32[48,128]{1,0:T(8,128)S(1)} %compare_select_fusion.3), channel_id=1, source_target_pairs={{0,192},{1,193},{2,194},{3,195},{4,196},{5,197},{6,198},{7,199},{1... | collective-permute-start | bytes 73736 | tf_op jit(solution)/shard_map/ppermute | solution.py:520
  189.8 2.4 %collective-permute-start.15 = (f32[48,128]{1,0:T(8,128)S(1)}, f32[48,128]{1,0:T(8,128)S(1)}, u32[]{:S(2)}, u32[]{:S(2)}) collective-permute-start(f32[48,128]{1,0:T(8,128)S(1)} %compare_select_fusion.1), channel_id=1, source_target_pairs={{0,8},{1,9},{2,10},{3,11},{4,12},{5,13},{6,14},{7,15},{8,0},{9,1},... | collective-permute-start | bytes 73736 | tf_op jit(solution)/shard_map/ppermute | solution.py:520
  193.1 1.2 copy-start.1
  (8 other events, 6.0 us)

commit v3 on v2

--- a/solution.py
+++ b/solution.py
@@ -334,7 +334,13 @@
     lax.fori_loop(0, NTURB, one, 0)
 
 
-def pack_x_kernel(field_ref, cot_ref, next_ref, prev_ref):
+def pack_x_kernel(field_hbm, cot_hbm, next_ref, prev_ref, field_ref, cot_ref, sems):
+    first = pltpu.make_async_copy(field_hbm, field_ref, sems.at[0])
+    second = pltpu.make_async_copy(cot_hbm, cot_ref, sems.at[1])
+    first.start()
+    second.start()
+    first.wait()
+    second.wait()
     half = OWN_SPAN // 2
     top = lax.broadcasted_iota(jnp.int32, (CX, half), 0) < CX // 2
     for i in range(19):
@@ -435,12 +441,14 @@
     chunks(one)
 
 
-def backward_kernel(first, s_ref, a_ref, area_ref, inv_ref, got_ref, v_ref, *rest):
+def backward_kernel(first, sends, s_ref, a_ref, area_ref, inv_ref, got_ref, v_ref, *rest):
+    rest = list(rest)
+    rotor_ref = None if first else rest.pop(0)
+    out_ref, drag_ref, bar_ref = rest[:3]
+    field, sums = rest[-2:]
     if first:
-        out_ref, drag_ref, bar_ref, publish_ref, rotor_ref, field, sums = rest
+        rotor_ref = rest[-3]
         rotor_ref[...] = totals(got_ref, 0) * inv_ref[...]
-    else:
-        rotor_ref, out_ref, drag_ref, bar_ref, publish_ref, field, sums = rest
     bar_ref[...] = totals(got_ref, NTURB if first else 0) * inv_ref[...]
     adjoint_field(s_ref, a_ref, area_ref, rotor_ref, bar_ref, field)
     stream_adjoint(field, out_ref)
@@ -450,13 +458,20 @@
         drag_ref[rows, lanes] = push_back(a) * v_ref[rows, lanes] * -THRUST
 
     chunks(other)
-    sums[...] = jnp.zeros_like(sums)
-    turbine_sums(area_ref, drag_ref, sums, 0)
-    publish(sums, publish_ref)
-
-
-def last_kernel(s_ref, a_ref, area_ref, rotor_ref, bar_ref, out_ref, field, result):
-    adjoint_field(s_ref, a_ref, area_ref, rotor_ref, bar_ref, field)
+    if sends:
+        sums[...] = jnp.zeros_like(sums)
+        turbine_sums(area_ref, drag_ref, sums, 0)
+        publish(sums, rest[3])
+
+
+def last_kernel(s_ref, a_ref, area_ref, rotor_ref, point_ref, size_ref, inv_ref, out_ref, grad_ref, field, result, bar):
+    known, swing, slope = (
+        point_ref[NTURB * j : NTURB * (j + 1), :PTS] for j in range(3)
+    )
+    total = jnp.sum(size_ref[...] * swing, axis=1, keepdims=True)
+    grad_ref[...] = known + total * slope
+    bar[...] = jnp.broadcast_to(total, (NTURB, 128)) * inv_ref[...]
+    adjoint_field(s_ref, a_ref, area_ref, rotor_ref, bar, field)
     stream_adjoint(field, result)
     for i in range(19):
         out_ref[i] = result[i, OWN_ROWS, OWN_LANE : OWN_LANE + OWN_SPAN]
@@ -494,7 +509,7 @@
             out_ref[pl.ds(j * NTURB + t, 1), 0:PTS] = jnp.sum(picked, axis=0, keepdims=True)
         return carry
 
-    lax.fori_loop(0, NTURB, one, 0)
+    lax.fori_loop(0, NTURB, one, 0, unroll=4)
 
 
 def call(kernel, outs, scratch, *args):
@@ -528,9 +543,15 @@
     return lax.all_to_all(rows, ("gx", "gy"), 0, 0, tiled=True)
 
 
+def merge_kernel(*refs):
+    value = refs[0][...]
+    for ref in refs[1:-1]:
+        value = jnp.where(value != 0.0, value, ref[...])
+    refs[-1][...] = value
+
+
 def merge(value, parts):
-    for part in parts:
-        value = jnp.where(value != 0.0, value, part)
+    (value,) = call(merge_kernel, [value.shape], [], value, *parts)
     return value
 
 
@@ -570,15 +591,23 @@
     return lax.ppermute(value, axis, [(i, (i + step) % size) for i in range(size)])
 
 
-def region(checkpoint, cotangent):
+def region(checkpoint, cotangent, ready):
     wide = (19, CX, OWN_SPAN + OWN_SPAN // 2)
-    right, left = call(pack_x_kernel, [wide] * 2, [], checkpoint, cotangent)
+    right, left = pl.pallas_call(
+        pack_x_kernel,
+        out_shape=[jax.ShapeDtypeStruct(wide, jnp.float32)] * 2,
+        in_specs=[pl.BlockSpec(memory_space=pltpu.HBM)] * 2,
+        out_specs=[pl.BlockSpec(memory_space=pltpu.VMEM)] * 2,
+        scratch_shapes=[pltpu.VMEM(checkpoint.shape, jnp.float32)] * 2 + [pltpu.SemaphoreType.DMA((2,))],
+        compiler_params=pltpu.CompilerParams(vmem_limit_bytes=VMEM_LIMIT),
+    )(checkpoint, cotangent)
     before, after = shift(right, "gx", 1), shift(left, "gx", -1)
+    before, after, *ready = lax.optimization_barrier((before, after) + ready)
     stack, edge = (19, RX, OWN_SPAN), (19, RX + CX, OWN_SPAN // 2)
     fields, cots, right, left = call(
         pack_y_kernel, [stack, stack, edge, edge], [], checkpoint, cotangent, before, after
     )
-    return shift(right, "gy", 1), fields, shift(left, "gy", -1), cots
+    return (shift(right, "gy", 1), fields, shift(left, "gy", -1), cots), ready
 
 
 def body(checkpoint, cotangent, blade_area, hub_tile, point_side, point_local):
@@ -601,8 +630,10 @@
     full = (19, RX, LANES)
     flat = (RX, LANES)
     row = (NTURB, 128)
-    parts = region(checkpoint, cotangent)
     (spots,) = call(area_kernel, [(NTURB,) + flat], [], cell_x, cell_yz, area)
+    own_yz = jnp.where(mine_y, cell_yz, -1)
+    parts, ready = region(checkpoint, cotangent, (spots, cell_x, own_yz, area, inverse))
+    spots, cell_x, own_yz, area, inverse = ready
 
     s, v, rotor = [None] * 5, [None] * 5, [None] * 5
     table = (128, 128)
@@ -619,35 +650,31 @@
     adjoint = cot
     bar, drag = [None] * 5, [None] * 5
     for k in (4, 3, 2):
-        first = k == 4
+        first, sends = k == 4, k > 2
         args = [s[k], adjoint, spots, inverse, exchange(sums), v[k - 1]]
         outs = call(
-            functools.partial(backward_kernel, first),
-            [full, flat, row, every] + ([row] if first else []),
+            functools.partial(backward_kernel, first, sends),
+            [full, flat, row] + ([every] if sends else []) + ([row] if first else []),
             [full, table],
             *(args + ([] if first else [rotor[k]])),
         )
-        adjoint, drag[k - 1], bar[k], sums = outs[:4]
+        adjoint, drag[k - 1], bar[k] = outs[:3]
+        sums = outs[3] if sends else None
         if first:
             rotor[4] = outs[4]
     (points,) = call(
         gather_kernel,
         [(3 * NTURB, 128)],
         [],
-        *([cell_x, jnp.where(mine_y, cell_yz, -1), cot] + drag[1:4] + v[1:] + rotor[1:] + bar[2:] + [inverse]),
-    )
-    points = spread(points)[:, :PTS]
-    known, swing, slope = points[:NTURB], points[NTURB : 2 * NTURB], points[2 * NTURB :]
-    total = jnp.sum(area * swing, 1, keepdims=True)
-    grad_area = (known + total * slope).reshape(-1)
-    bar[1] = total * inverse
-    (grad,) = call(
+        *([cell_x, own_yz, cot] + drag[1:4] + v[1:] + rotor[1:] + bar[2:] + [inverse]),
+    )
+    grad, grad_area = call(
         last_kernel,
-        [(19, CX, CY * NZ)],
-        [full, full],
-        *(s[1], adjoint, spots, rotor[1], bar[1]),
-    )
-    return grad, grad_area
+        [(19, CX, CY * NZ), (NTURB, PTS)],
+        [full, full, row],
+        *(s[1], adjoint, spots, rotor[1], spread(points), area, inverse),
+    )
+    return grad, grad_area.reshape(-1)
 
 
 def solution(mesh):

time: 197 us -> 192 us (0.975)
  blocking collectives: 93.2 us -> 122 us
  starting transfers between devices: 37.2 us -> 20.3 us
  waiting for transfers between devices: 35.2 us -> 27.4 us
  local copies, waits for them, and re-layouts: 10 us -> 4.28 us
  Pallas kernels: 18.5 us -> 16.4 us
    all_to_all x5 -> x6, blocking collectives: 93.2 us -> 122 us  [exchange(): return lax.all_to_all(rows, ('gx', 'gy'), 0, 0, tiled=True)]
    all_to_all x1 -> x0, starting transfers between devices: 17 us -> none  [exchange(): return lax.all_to_all(rows, ('gx', 'gy'), 0, 0, tiled=True)]
    all_to_all x1 -> x0, waiting for transfers between devices: 12.4 us -> none  [exchange(): return lax.all_to_all(rows, ('gx', 'gy'), 0, 0, tiled=True)]
    unnamed x30 -> x16, local copies, waits for them, and re-layouts: 8.86 us -> 3.17 us
    ppermute x12, waiting for transfers between devices: 16 us -> 18.9 us  [route(): return lax.ppermute(value, ('gx', 'gy'), pairs)]
    pallas_call x12 -> x18, Pallas kernels: 18.5 us -> 16 us  [call(): pl.pallas_call(kernel, out_shape=[jax.ShapeDtypeStruct(shape, jnp.float32...]
  transfers between devices with their start and end apart: 17 -> 16, of which waited for: 11 -> 9; matrix products, arithmetic and copies ran while one was open for 1% -> 0% of each run, Pallas kernels for 1% -> 2%
where the time goes in v3:
time: 192 us
  blocking collectives  122 us (64%)
  waiting for transfers between devices  27.4 us (14%)
  starting transfers between devices  20.3 us (11%)
  Pallas kernels  16.4 us (9%)
  local copies, waits for them, and re-layouts  4.28 us (2%)
    all_to_all x6, blocking collectives, exchange(): return lax.all_to_all(rows, ('gx', 'gy'), 0, 0, tiled=True)  122 us
    ppermute x12, waiting for transfers between devices, route(): return lax.ppermute(value, ('gx', 'gy'), pairs)  18.9 us
    pallas_call x18, Pallas kernels, call(): pl.pallas_call(kernel, out_shape=[jax.ShapeDtypeStruct(shape, jnp.float32...  16 us
    ppermute x12, starting transfers between devices, route(): return lax.ppermute(value, ('gx', 'gy'), pairs)  12.9 us
    ppermute x4, waiting for transfers between devices, shift(): lax.ppermute(value, axis, [(i, (i + step) % size) for i in range(size)])  8.56 us
    ppermute x4, starting transfers between devices, shift(): lax.ppermute(value, axis, [(i, (i + step) % size) for i in range(size)])  7.46 us
  transfers between devices with their start and end apart: 16, of which 9 were waited for; matrix products, arithmetic and copies ran while one was open for 0% of the time, Pallas kernels for 2%

profile of v3, /device:TPU:1, one launch (start us, length us, event | category | flops | bytes accessed | tf_op | source)
XLA Modules:
  0.0 192.1 jit_solution(9850122362145088197)
XLA Ops:
  2.9 2.7 %collective-permute-start = (f32[19,8,384]{2,1,0:T(8,128)S(1)}, f32[19,8,384]{2,1,0:T(8,128)S(1)}, u32[]{:S(2)}, u32[]{:S(2)}) collective-permute-start(f32[19,8,384]{2,1,0:T(8,128)S(1)} %get-tuple-element.45), channel_id=1, source_target_pairs={{0,8},{8,16},{16,24},{24,32},{32,40},{40,48},{48,56},{56,64},{64,7... | collective-permute-start | bytes 700424 | tf_op jit(solution)/shard_map/ppermute | solution.py:591
  8.3 2.9 %shard_map.78.area_ref = f32[16,24,512]{2,1,0:T(8,128)S(1)} custom-call(s32[16,96]{1,0:T(8,128)S(1)} %fusion.19.x_ref, s32[16,96]{1,0:T(8,128)S(1)} %get-tuple-element.89.yz_ref, f32[16,96]{1,0:T(8,128)S(1)} %reshape.65.area_ref.size_ref), custom_call_target="tpu_custom_call" | custom-call | tf_op jit(solution)/shard_map/pallas_call | solution.py:517
  12.7 2.9 %collective-permute-start.3 = (f32[19,32,128]{2,1,0:T(8,128)S(1)}, f32[19,32,128]{2,1,0:T(8,128)S(1)}, u32[]{:S(2)}, u32[]{:S(2)}) collective-permute-start(f32[19,32,128]{2,1,0:T(8,128)S(1)} %get-tuple-element.51), channel_id=1, source_target_pairs={{0,7},{1,0},{2,1},{3,2},{4,3},{5,4},{6,5},{7,6},{8,15},{9,8},{10,9... | collective-permute-start | bytes 933896 | tf_op jit(solution)/shard_map/ppermute | solution.py:591
  15.6 8.6 %collective-permute-done.2.before_ref = f32[19,32,128]{2,1,0:T(8,128)S(1)} collective-permute-done((f32[19,32,128]{2,1,0:T(8,128)S(1)}, f32[19,32,128]{2,1,0:T(8,128)S(1)}, u32[]{:S(2)}, u32[]{:S(2)}) %collective-permute-start.2) | collective-permute-done | bytes 311328 | tf_op jit(solution)/shard_map/ppermute | solution.py:591
  24.8 29.3 %all_to_all.66 = f32[256,1,128]{2,1,0:T(1,128)S(1)} all-to-all(f32[256,1,128]{2,1,0:T(1,128)S(1)} %bitcast.30), channel_id=1, replica_groups=mesh['gx'=32,'gy'=8] {'gx','gy'}, dimensions={0} | all-to-all | bytes 262144 | tf_op jit(solution)/shard_map/all_to_all | solution.py:543
  54.1 1.5 shard_map.81
  55.6 18.6 %all_to_all.67 = f32[256,1,128]{2,1,0:T(1,128)S(1)} all-to-all(f32[256,1,128]{2,1,0:T(1,128)S(1)} %bitcast.33), channel_id=1, replica_groups=mesh['gx'=32,'gy'=8] {'gx','gy'}, dimensions={0} | all-to-all | bytes 262144 | tf_op jit(solution)/shard_map/all_to_all | solution.py:543
  74.2 1.5 shard_map.82
  75.7 18.6 %all_to_all.68 = f32[256,1,128]{2,1,0:T(1,128)S(1)} all-to-all(f32[256,1,128]{2,1,0:T(1,128)S(1)} %bitcast.34), channel_id=1, replica_groups=mesh['gx'=32,'gy'=8] {'gx','gy'}, dimensions={0} | all-to-all | bytes 262144 | tf_op jit(solution)/shard_map/all_to_all | solution.py:543
  94.3 1.6 shard_map.83
  95.9 18.6 %all_to_all.69 = f32[256,1,128]{2,1,0:T(1,128)S(1)} all-to-all(f32[256,1,128]{2,1,0:T(1,128)S(1)} %bitcast.35), channel_id=1, replica_groups=mesh['gx'=32,'gy'=8] {'gx','gy'}, dimensions={0} | all-to-all | bytes 262144 | tf_op jit(solution)/shard_map/all_to_all | solution.py:543
  114.5 1.7 shard_map.84
  116.2 18.8 %all_to_all.70 = f32[256,1,128]{2,1,0:T(1,128)S(1)} all-to-all(f32[256,1,128]{2,1,0:T(1,128)S(1)} %bitcast.31), channel_id=1, replica_groups=mesh['gx'=32,'gy'=8] {'gx','gy'}, dimensions={0} | all-to-all | bytes 262144 | tf_op jit(solution)/shard_map/all_to_all | solution.py:543
  135.0 1.7 shard_map.85
  136.7 18.6 %all_to_all.71 = f32[256,1,128]{2,1,0:T(1,128)S(1)} all-to-all(f32[256,1,128]{2,1,0:T(1,128)S(1)} %bitcast.32), channel_id=1, replica_groups=mesh['gx'=32,'gy'=8] {'gx','gy'}, dimensions={0} | all-to-all | bytes 262144 | tf_op jit(solution)/shard_map/all_to_all | solution.py:543
  155.3 1.5 shard_map.86
  161.7 2.6 %collective-permute-start.6 = (f32[48,128]{1,0:T(8,128)S(1)}, f32[48,128]{1,0:T(8,128)S(1)}, u32[]{:S(2)}, u32[]{:S(2)}) collective-permute-start(f32[48,128]{1,0:T(8,128)S(1)} %shard_map.88.refs_0_), channel_id=1, source_target_pairs={{0,3},{1,0},{2,1},{3,2},{4,7},{5,4},{6,5},{7,6},{8,15},{9,12},{10,... | collective-permute-start | bytes 73736 | tf_op jit(solution)/shard_map/ppermute | solution.py:535
  164.2 1.4 collective-permute-done.7.refs_3_
  165.7 3.5 %collective-permute-done.5.refs_1_ = f32[48,128]{1,0:T(8,128)S(1)} collective-permute-done((f32[48,128]{1,0:T(8,128)S(1)}, f32[48,128]{1,0:T(8,128)S(1)}, u32[]{:S(2)}, u32[]{:S(2)}) %collective-permute-start.5) | collective-permute-done | bytes 24608 | tf_op jit(solution)/shard_map/ppermute | solution.py:535
  171.5 4.2 %collective-permute-done.10.refs_1_ = f32[48,128]{1,0:T(8,128)S(1)} collective-permute-done((f32[48,128]{1,0:T(8,128)S(1)}, f32[48,128]{1,0:T(8,128)S(1)}, u32[]{:S(2)}, u32[]{:S(2)}) %collective-permute-start.10) | collective-permute-done | bytes 24608 | tf_op jit(solution)/shard_map/ppermute | solution.py:535
  175.7 3.1 %collective-permute-start.12 = (f32[48,128]{1,0:T(8,128)S(1)}, f32[48,128]{1,0:T(8,128)S(1)}, u32[]{:S(2)}, u32[]{:S(2)}) collective-permute-start(f32[48,128]{1,0:T(8,128)S(1)} %shard_map.91.refs_0_), channel_id=1, source_target_pairs={{0,8},{1,9},{2,10},{3,11},{4,12},{5,13},{6,14},{7,15},{8,0},{9,1},... | collective-permute-start | bytes 73736 | tf_op jit(solution)/shard_map/ppermute | solution.py:535
  180.9 6.4 %collective-permute-done.13.refs_1_ = f32[48,128]{1,0:T(8,128)S(1)} collective-permute-done((f32[48,128]{1,0:T(8,128)S(1)}, f32[48,128]{1,0:T(8,128)S(1)}, u32[]{:S(2)}, u32[]{:S(2)}) %collective-permute-start.13) | collective-permute-done | bytes 24608 | tf_op jit(solution)/shard_map/ppermute | solution.py:535
  187.3 1.3 collective-permute-start.15
  189.5 1.9 shard_map.95
  (63 shorter events, 17.9 us)
Async XLA Ops:
  0.6 0.9 copy-start
  1.5 0.9 copy-start.2
  2.5 3.8 %copy-start.4 = (s32[1536]{0:T(1024)S(1)}, s32[1536]{0:T(1024)}, u32[]{:S(2)}) copy-start(s32[1536]{0:T(1024)} %param.10) | copy-start | bytes 18436
  2.9 8.4 %collective-permute-start = (f32[19,8,384]{2,1,0:T(8,128)S(1)}, f32[19,8,384]{2,1,0:T(8,128)S(1)}, u32[]{:S(2)}, u32[]{:S(2)}) collective-permute-start(f32[19,8,384]{2,1,0:T(8,128)S(1)} %get-tuple-element.45), channel_id=1, source_target_pairs={{0,8},{8,16},{16,24},{24,32},{32,40},{40,48},{48,56},{56,64},{64,7... | collective-permute-start | bytes 700424 | tf_op jit(solution)/shard_map/ppermute | solution.py:591
  5.6 5.7 %collective-permute-start.1 = (f32[19,8,384]{2,1,0:T(8,128)S(1)}, f32[19,8,384]{2,1,0:T(8,128)S(1)}, u32[]{:S(2)}, u32[]{:S(2)}) collective-permute-start(f32[19,8,384]{2,1,0:T(8,128)S(1)} %get-tuple-element.46), channel_id=1, source_target_pairs={{0,248},{8,0},{16,8},{24,16},{32,24},{40,32},{48,40},{56,48},{64,5... | collective-permute-start | bytes 700424 | tf_op jit(solution)/shard_map/ppermute | solution.py:591
  6.3 0.8 copy-start.5
  6.3 0.7 copy-start.7
  7.4 0.7 copy-start.6
  8.3 3.0 %copy-start.1 = (f32[19,8,256]{2,1,0:T(8,128)S(1)}, f32[19,8,256]{2,1,0:T(8,128)}, u32[]{:S(2)}) copy-start(f32[19,8,256]{2,1,0:T(8,128)} %field_ref.1) | copy-start | bytes 466948
  8.3 3.0 %copy-start.3 = (f32[19,8,256]{2,1,0:T(8,128)S(1)}, f32[19,8,256]{2,1,0:T(8,128)}, u32[]{:S(2)}) copy-start(f32[19,8,256]{2,1,0:T(8,128)} %cot_ref.1) | copy-start | bytes 466948
  11.5 12.6 %collective-permute-start.2 = (f32[19,32,128]{2,1,0:T(8,128)S(1)}, f32[19,32,128]{2,1,0:T(8,128)S(1)}, u32[]{:S(2)}, u32[]{:S(2)}) collective-permute-start(f32[19,32,128]{2,1,0:T(8,128)S(1)} %get-tuple-element.49), channel_id=1, source_target_pairs={{0,1},{1,2},{2,3},{3,4},{4,5},{5,6},{6,7},{7,0},{8,9},{9,10},{10,1... | collective-permute-start | bytes 933896 | tf_op jit(solution)/shard_map/ppermute | solution.py:591
  12.7 11.4 %collective-permute-start.3 = (f32[19,32,128]{2,1,0:T(8,128)S(1)}, f32[19,32,128]{2,1,0:T(8,128)S(1)}, u32[]{:S(2)}, u32[]{:S(2)}) collective-permute-start(f32[19,32,128]{2,1,0:T(8,128)S(1)} %get-tuple-element.51), channel_id=1, source_target_pairs={{0,7},{1,0},{2,1},{3,2},{4,3},{5,4},{6,5},{7,6},{8,15},{9,8},{10,9... | collective-permute-start | bytes 933896 | tf_op jit(solution)/shard_map/ppermute | solution.py:591
  157.7 2.1 %collective-permute-start.4 = (f32[48,128]{1,0:T(8,128)S(1)}, f32[48,128]{1,0:T(8,128)S(1)}, u32[]{:S(2)}, u32[]{:S(2)}) collective-permute-start(f32[48,128]{1,0:T(8,128)S(1)} %shard_map.87.refs_0_), channel_id=1, source_target_pairs={{0,8},{1,9},{2,10},{3,11},{4,12},{5,13},{6,14},{7,15},{8,0},{9,1},... | collective-permute-start | bytes 73736 | tf_op jit(solution)/shard_map/ppermute | solution.py:535
  159.7 4.5 %collective-permute-start.8 = (f32[48,128]{1,0:T(8,128)S(1)}, f32[48,128]{1,0:T(8,128)S(1)}, u32[]{:S(2)}, u32[]{:S(2)}) collective-permute-start(f32[48,128]{1,0:T(8,128)S(1)} %shard_map.88.refs_0_), channel_id=1, source_target_pairs={{0,4},{1,5},{2,6},{3,7},{4,0},{5,1},{6,2},{7,3},{8,12},{9,13},{10,... | collective-permute-start | bytes 73736 | tf_op jit(solution)/shard_map/ppermute | solution.py:535
  160.6 5.1 %collective-permute-start.7 = (f32[48,128]{1,0:T(8,128)S(1)}, f32[48,128]{1,0:T(8,128)S(1)}, u32[]{:S(2)}, u32[]{:S(2)}) collective-permute-start(f32[48,128]{1,0:T(8,128)S(1)} %shard_map.88.refs_0_), channel_id=1, source_target_pairs={{0,2},{1,3},{2,0},{3,1},{4,6},{5,7},{6,4},{7,5},{8,14},{9,15},{10,... | collective-permute-start | bytes 73736 | tf_op jit(solution)/shard_map/ppermute | solution.py:535
  161.7 4.0 %collective-permute-start.6 = (f32[48,128]{1,0:T(8,128)S(1)}, f32[48,128]{1,0:T(8,128)S(1)}, u32[]{:S(2)}, u32[]{:S(2)}) collective-permute-start(f32[48,128]{1,0:T(8,128)S(1)} %shard_map.88.refs_0_), channel_id=1, source_target_pairs={{0,3},{1,0},{2,1},{3,2},{4,7},{5,4},{6,5},{7,6},{8,15},{9,12},{10,... | collective-permute-start | bytes 73736 | tf_op jit(solution)/shard_map/ppermute | solution.py:535
  164.2 4.9 %collective-permute-start.5 = (f32[48,128]{1,0:T(8,128)S(1)}, f32[48,128]{1,0:T(8,128)S(1)}, u32[]{:S(2)}, u32[]{:S(2)}) collective-permute-start(f32[48,128]{1,0:T(8,128)S(1)} %shard_map.88.refs_0_), channel_id=1, source_target_pairs={{0,1},{1,2},{2,3},{3,0},{4,5},{5,6},{6,7},{7,4},{8,13},{9,14},{10,... | collective-permute-start | bytes 73736 | tf_op jit(solution)/shard_map/ppermute | solution.py:535
  169.1 1.6 collective-permute-start.9
  170.8 0.8 collective-permute-start.11
  171.4 4.3 %collective-permute-start.10 = (f32[48,128]{1,0:T(8,128)S(1)}, f32[48,128]{1,0:T(8,128)S(1)}, u32[]{:S(2)}, u32[]{:S(2)}) collective-permute-start(f32[48,128]{1,0:T(8,128)S(1)} %shard_map.90.refs_0_), channel_id=1, source_target_pairs={{0,16},{1,17},{2,18},{3,19},{4,20},{5,21},{6,22},{7,23},{8,40},{9,... | collective-permute-start | bytes 73736 | tf_op jit(solution)/shard_map/ppermute | solution.py:535
  175.7 4.0 %collective-permute-start.12 = (f32[48,128]{1,0:T(8,128)S(1)}, f32[48,128]{1,0:T(8,128)S(1)}, u32[]{:S(2)}, u32[]{:S(2)}) collective-permute-start(f32[48,128]{1,0:T(8,128)S(1)} %shard_map.91.refs_0_), channel_id=1, source_target_pairs={{0,8},{1,9},{2,10},{3,11},{4,12},{5,13},{6,14},{7,15},{8,0},{9,1},... | collective-permute-start | bytes 73736 | tf_op jit(solution)/shard_map/ppermute | solution.py:535
  179.7 1.2 collective-permute-start.14
  180.3 7.0 %collective-permute-start.13 = (f32[48,128]{1,0:T(8,128)S(1)}, f32[48,128]{1,0:T(8,128)S(1)}, u32[]{:S(2)}, u32[]{:S(2)}) collective-permute-start(f32[48,128]{1,0:T(8,128)S(1)} %shard_map.92.refs_0_), channel_id=1, source_target_pairs={{0,64},{1,65},{2,66},{3,67},{4,68},{5,69},{6,70},{7,71},{8,136},{9... | collective-permute-start | bytes 73736 | tf_op jit(solution)/shard_map/ppermute | solution.py:535
  187.3 2.2 %collective-permute-start.15 = (f32[48,128]{1,0:T(8,128)S(1)}, f32[48,128]{1,0:T(8,128)S(1)}, u32[]{:S(2)}, u32[]{:S(2)}) collective-permute-start(f32[48,128]{1,0:T(8,128)S(1)} %shard_map.93.refs_0_), channel_id=1, source_target_pairs={{0,8},{1,9},{2,10},{3,11},{4,12},{5,13},{6,14},{7,15},{8,0},{9,1},... | collective-permute-start | bytes 73736 | tf_op jit(solution)/shard_map/ppermute | solution.py:535

commit v4 on v3

--- a/solution.py
+++ b/solution.py
@@ -216,7 +216,7 @@
             body(pl.ds(row, 8), pl.ds(lane, 128))
         return carry
 
-    lax.fori_loop(0, LANES // 128, step, 0)
+    lax.fori_loop(0, LANES // 128, step, 0, unroll=True)
 
 
 def shifted(value, cx, cy, cz):
@@ -509,7 +509,7 @@
             out_ref[pl.ds(j * NTURB + t, 1), 0:PTS] = jnp.sum(picked, axis=0, keepdims=True)
         return carry
 
-    lax.fori_loop(0, NTURB, one, 0, unroll=4)
+    lax.fori_loop(0, NTURB, one, 0, unroll=True)
 
 
 def call(kernel, outs, scratch, *args):

time: 192 us -> 189 us (0.984)
  Pallas kernels: 16.4 us -> 12.5 us
    pallas_call x18, Pallas kernels: 16 us -> 12.1 us  [call(): pl.pallas_call(kernel, out_shape=[jax.ShapeDtypeStruct(shape, jnp.float32...]
where the time goes in v4:
time: 189 us; the launch traced here: 188 us
  blocking collectives  122 us (65%)
  waiting for transfers between devices  27.4 us (14%)
  starting transfers between devices  20.6 us (11%)
  Pallas kernels  12.5 us (7%)
  local copies, waits for them, and re-layouts  4.28 us (2%)
    all_to_all x6, blocking collectives, exchange(): return lax.all_to_all(rows, ('gx', 'gy'), 0, 0, tiled=True)  122 us
    ppermute x12, waiting for transfers between devices, route(): return lax.ppermute(value, ('gx', 'gy'), pairs)  18.9 us
    ppermute x12, starting transfers between devices, route(): return lax.ppermute(value, ('gx', 'gy'), pairs)  13.1 us
    pallas_call x18, Pallas kernels, call(): pl.pallas_call(kernel, out_shape=[jax.ShapeDtypeStruct(shape, jnp.float32...  12.1 us
    ppermute x4, waiting for transfers between devices, shift(): lax.ppermute(value, axis, [(i, (i + step) % size) for i in range(size)])  8.56 us
    ppermute x4, starting transfers between devices, shift(): lax.ppermute(value, axis, [(i, (i + step) % size) for i in range(size)])  7.46 us
  transfers between devices with their start and end apart: 16, of which 9 were waited for; matrix products, arithmetic and copies ran while one was open for 0% of the time, Pallas kernels for 2%

profile of v4, /device:TPU:1, one launch (start us, length us, event | category | flops | bytes accessed | tf_op | source)
XLA Modules:
  0.0 188.4 jit_solution(15230543611414538342)
XLA Ops:
  2.9 2.7 %collective-permute-start = (f32[19,8,384]{2,1,0:T(8,128)S(1)}, f32[19,8,384]{2,1,0:T(8,128)S(1)}, u32[]{:S(2)}, u32[]{:S(2)}) collective-permute-start(f32[19,8,384]{2,1,0:T(8,128)S(1)} %get-tuple-element.45), channel_id=1, source_target_pairs={{0,8},{8,16},{16,24},{24,32},{32,40},{40,48},{48,56},{56,64},{64,7... | collective-permute-start | bytes 700424 | tf_op jit(solution)/shard_map/ppermute | solution.py:591
  8.3 2.9 %shard_map.78.area_ref = f32[16,24,512]{2,1,0:T(8,128)S(1)} custom-call(s32[16,96]{1,0:T(8,128)S(1)} %fusion.19.x_ref, s32[16,96]{1,0:T(8,128)S(1)} %get-tuple-element.89.yz_ref, f32[16,96]{1,0:T(8,128)S(1)} %reshape.65.area_ref.size_ref), custom_call_target="tpu_custom_call" | custom-call | tf_op jit(solution)/shard_map/pallas_call | solution.py:517
  11.5 1.2 collective-permute-start.2
  12.7 2.9 %collective-permute-start.3 = (f32[19,32,128]{2,1,0:T(8,128)S(1)}, f32[19,32,128]{2,1,0:T(8,128)S(1)}, u32[]{:S(2)}, u32[]{:S(2)}) collective-permute-start(f32[19,32,128]{2,1,0:T(8,128)S(1)} %get-tuple-element.51), channel_id=1, source_target_pairs={{0,7},{1,0},{2,1},{3,2},{4,3},{5,4},{6,5},{7,6},{8,15},{9,8},{10,9... | collective-permute-start | bytes 933896 | tf_op jit(solution)/shard_map/ppermute | solution.py:591
  15.6 8.6 %collective-permute-done.2.before_ref = f32[19,32,128]{2,1,0:T(8,128)S(1)} collective-permute-done((f32[19,32,128]{2,1,0:T(8,128)S(1)}, f32[19,32,128]{2,1,0:T(8,128)S(1)}, u32[]{:S(2)}, u32[]{:S(2)}) %collective-permute-start.2) | collective-permute-done | bytes 311328 | tf_op jit(solution)/shard_map/ppermute | solution.py:591
  24.6 29.3 %all_to_all.66 = f32[256,1,128]{2,1,0:T(1,128)S(1)} all-to-all(f32[256,1,128]{2,1,0:T(1,128)S(1)} %bitcast.30), channel_id=1, replica_groups=mesh['gx'=32,'gy'=8] {'gx','gy'}, dimensions={0} | all-to-all | bytes 262144 | tf_op jit(solution)/shard_map/all_to_all | solution.py:543
  54.8 18.6 %all_to_all.67 = f32[256,1,128]{2,1,0:T(1,128)S(1)} all-to-all(f32[256,1,128]{2,1,0:T(1,128)S(1)} %bitcast.33), channel_id=1, replica_groups=mesh['gx'=32,'gy'=8] {'gx','gy'}, dimensions={0} | all-to-all | bytes 262144 | tf_op jit(solution)/shard_map/all_to_all | solution.py:543
  74.3 18.6 %all_to_all.68 = f32[256,1,128]{2,1,0:T(1,128)S(1)} all-to-all(f32[256,1,128]{2,1,0:T(1,128)S(1)} %bitcast.34), channel_id=1, replica_groups=mesh['gx'=32,'gy'=8] {'gx','gy'}, dimensions={0} | all-to-all | bytes 262144 | tf_op jit(solution)/shard_map/all_to_all | solution.py:543
  93.9 18.8 %all_to_all.69 = f32[256,1,128]{2,1,0:T(1,128)S(1)} all-to-all(f32[256,1,128]{2,1,0:T(1,128)S(1)} %bitcast.35), channel_id=1, replica_groups=mesh['gx'=32,'gy'=8] {'gx','gy'}, dimensions={0} | all-to-all | bytes 262144 | tf_op jit(solution)/shard_map/all_to_all | solution.py:543
  112.7 1.2 shard_map.84
  113.9 18.6 %all_to_all.70 = f32[256,1,128]{2,1,0:T(1,128)S(1)} all-to-all(f32[256,1,128]{2,1,0:T(1,128)S(1)} %bitcast.31), channel_id=1, replica_groups=mesh['gx'=32,'gy'=8] {'gx','gy'}, dimensions={0} | all-to-all | bytes 262144 | tf_op jit(solution)/shard_map/all_to_all | solution.py:543
  132.5 1.2 shard_map.85
  133.8 18.6 %all_to_all.71 = f32[256,1,128]{2,1,0:T(1,128)S(1)} all-to-all(f32[256,1,128]{2,1,0:T(1,128)S(1)} %bitcast.32), channel_id=1, replica_groups=mesh['gx'=32,'gy'=8] {'gx','gy'}, dimensions={0} | all-to-all | bytes 262144 | tf_op jit(solution)/shard_map/all_to_all | solution.py:543
  152.4 1.2 shard_map.86
  154.1 1.2 collective-permute-start.4
  157.0 1.1 collective-permute-start.7
  158.1 2.6 %collective-permute-start.6 = (f32[48,128]{1,0:T(8,128)S(1)}, f32[48,128]{1,0:T(8,128)S(1)}, u32[]{:S(2)}, u32[]{:S(2)}) collective-permute-start(f32[48,128]{1,0:T(8,128)S(1)} %shard_map.88.refs_0_), channel_id=1, source_target_pairs={{0,3},{1,0},{2,1},{3,2},{4,7},{5,4},{6,5},{7,6},{8,15},{9,12},{10,... | collective-permute-start | bytes 73736 | tf_op jit(solution)/shard_map/ppermute | solution.py:535
  160.7 1.4 collective-permute-done.7.refs_3_
  162.1 3.5 %collective-permute-done.5.refs_1_ = f32[48,128]{1,0:T(8,128)S(1)} collective-permute-done((f32[48,128]{1,0:T(8,128)S(1)}, f32[48,128]{1,0:T(8,128)S(1)}, u32[]{:S(2)}, u32[]{:S(2)}) %collective-permute-start.5) | collective-permute-done | bytes 24608 | tf_op jit(solution)/shard_map/ppermute | solution.py:535
  168.2 4.2 %collective-permute-done.10.refs_1_ = f32[48,128]{1,0:T(8,128)S(1)} collective-permute-done((f32[48,128]{1,0:T(8,128)S(1)}, f32[48,128]{1,0:T(8,128)S(1)}, u32[]{:S(2)}, u32[]{:S(2)}) %collective-permute-start.10) | collective-permute-done | bytes 24608 | tf_op jit(solution)/shard_map/ppermute | solution.py:535
  172.3 3.1 %collective-permute-start.12 = (f32[48,128]{1,0:T(8,128)S(1)}, f32[48,128]{1,0:T(8,128)S(1)}, u32[]{:S(2)}, u32[]{:S(2)}) collective-permute-start(f32[48,128]{1,0:T(8,128)S(1)} %shard_map.91.refs_0_), channel_id=1, source_target_pairs={{0,8},{1,9},{2,10},{3,11},{4,12},{5,13},{6,14},{7,15},{8,0},{9,1},... | collective-permute-start | bytes 73736 | tf_op jit(solution)/shard_map/ppermute | solution.py:535
  177.5 6.4 %collective-permute-done.13.refs_1_ = f32[48,128]{1,0:T(8,128)S(1)} collective-permute-done((f32[48,128]{1,0:T(8,128)S(1)}, f32[48,128]{1,0:T(8,128)S(1)}, u32[]{:S(2)}, u32[]{:S(2)}) %collective-permute-start.13) | collective-permute-done | bytes 24608 | tf_op jit(solution)/shard_map/ppermute | solution.py:535
  183.9 1.3 collective-permute-start.15
  186.1 1.6 shard_map.95
  (63 shorter events, 16.9 us)
Async XLA Ops:
  0.6 0.9 copy-start
  1.5 0.9 copy-start.2
  2.5 3.8 %copy-start.4 = (s32[1536]{0:T(1024)S(1)}, s32[1536]{0:T(1024)}, u32[]{:S(2)}) copy-start(s32[1536]{0:T(1024)} %param.10) | copy-start | bytes 18436
  2.9 8.4 %collective-permute-start = (f32[19,8,384]{2,1,0:T(8,128)S(1)}, f32[19,8,384]{2,1,0:T(8,128)S(1)}, u32[]{:S(2)}, u32[]{:S(2)}) collective-permute-start(f32[19,8,384]{2,1,0:T(8,128)S(1)} %get-tuple-element.45), channel_id=1, source_target_pairs={{0,8},{8,16},{16,24},{24,32},{32,40},{40,48},{48,56},{56,64},{64,7... | collective-permute-start | bytes 700424 | tf_op jit(solution)/shard_map/ppermute | solution.py:591
  5.6 5.7 %collective-permute-start.1 = (f32[19,8,384]{2,1,0:T(8,128)S(1)}, f32[19,8,384]{2,1,0:T(8,128)S(1)}, u32[]{:S(2)}, u32[]{:S(2)}) collective-permute-start(f32[19,8,384]{2,1,0:T(8,128)S(1)} %get-tuple-element.46), channel_id=1, source_target_pairs={{0,248},{8,0},{16,8},{24,16},{32,24},{40,32},{48,40},{56,48},{64,5... | collective-permute-start | bytes 700424 | tf_op jit(solution)/shard_map/ppermute | solution.py:591
  6.3 0.8 copy-start.5
  6.3 0.7 copy-start.7
  7.4 0.7 copy-start.6
  8.3 3.0 %copy-start.1 = (f32[19,8,256]{2,1,0:T(8,128)S(1)}, f32[19,8,256]{2,1,0:T(8,128)}, u32[]{:S(2)}) copy-start(f32[19,8,256]{2,1,0:T(8,128)} %field_ref.1) | copy-start | bytes 466948
  8.3 3.0 %copy-start.3 = (f32[19,8,256]{2,1,0:T(8,128)S(1)}, f32[19,8,256]{2,1,0:T(8,128)}, u32[]{:S(2)}) copy-start(f32[19,8,256]{2,1,0:T(8,128)} %cot_ref.1) | copy-start | bytes 466948
  11.5 12.6 %collective-permute-start.2 = (f32[19,32,128]{2,1,0:T(8,128)S(1)}, f32[19,32,128]{2,1,0:T(8,128)S(1)}, u32[]{:S(2)}, u32[]{:S(2)}) collective-permute-start(f32[19,32,128]{2,1,0:T(8,128)S(1)} %get-tuple-element.49), channel_id=1, source_target_pairs={{0,1},{1,2},{2,3},{3,4},{4,5},{5,6},{6,7},{7,0},{8,9},{9,10},{10,1... | collective-permute-start | bytes 933896 | tf_op jit(solution)/shard_map/ppermute | solution.py:591
  12.7 11.4 %collective-permute-start.3 = (f32[19,32,128]{2,1,0:T(8,128)S(1)}, f32[19,32,128]{2,1,0:T(8,128)S(1)}, u32[]{:S(2)}, u32[]{:S(2)}) collective-permute-start(f32[19,32,128]{2,1,0:T(8,128)S(1)} %get-tuple-element.51), channel_id=1, source_target_pairs={{0,7},{1,0},{2,1},{3,2},{4,3},{5,4},{6,5},{7,6},{8,15},{9,8},{10,9... | collective-permute-start | bytes 933896 | tf_op jit(solution)/shard_map/ppermute | solution.py:591
  154.1 2.1 %collective-permute-start.4 = (f32[48,128]{1,0:T(8,128)S(1)}, f32[48,128]{1,0:T(8,128)S(1)}, u32[]{:S(2)}, u32[]{:S(2)}) collective-permute-start(f32[48,128]{1,0:T(8,128)S(1)} %shard_map.87.refs_0_), channel_id=1, source_target_pairs={{0,8},{1,9},{2,10},{3,11},{4,12},{5,13},{6,14},{7,15},{8,0},{9,1},... | collective-permute-start | bytes 73736 | tf_op jit(solution)/shard_map/ppermute | solution.py:535
  156.2 4.5 %collective-permute-start.8 = (f32[48,128]{1,0:T(8,128)S(1)}, f32[48,128]{1,0:T(8,128)S(1)}, u32[]{:S(2)}, u32[]{:S(2)}) collective-permute-start(f32[48,128]{1,0:T(8,128)S(1)} %shard_map.88.refs_0_), channel_id=1, source_target_pairs={{0,4},{1,5},{2,6},{3,7},{4,0},{5,1},{6,2},{7,3},{8,12},{9,13},{10,... | collective-permute-start | bytes 73736 | tf_op jit(solution)/shard_map/ppermute | solution.py:535
  157.0 5.1 %collective-permute-start.7 = (f32[48,128]{1,0:T(8,128)S(1)}, f32[48,128]{1,0:T(8,128)S(1)}, u32[]{:S(2)}, u32[]{:S(2)}) collective-permute-start(f32[48,128]{1,0:T(8,128)S(1)} %shard_map.88.refs_0_), channel_id=1, source_target_pairs={{0,2},{1,3},{2,0},{3,1},{4,6},{5,7},{6,4},{7,5},{8,14},{9,15},{10,... | collective-permute-start | bytes 73736 | tf_op jit(solution)/shard_map/ppermute | solution.py:535
  158.1 4.0 %collective-permute-start.6 = (f32[48,128]{1,0:T(8,128)S(1)}, f32[48,128]{1,0:T(8,128)S(1)}, u32[]{:S(2)}, u32[]{:S(2)}) collective-permute-start(f32[48,128]{1,0:T(8,128)S(1)} %shard_map.88.refs_0_), channel_id=1, source_target_pairs={{0,3},{1,0},{2,1},{3,2},{4,7},{5,4},{6,5},{7,6},{8,15},{9,12},{10,... | collective-permute-start | bytes 73736 | tf_op jit(solution)/shard_map/ppermute | solution.py:535
  160.7 4.9 %collective-permute-start.5 = (f32[48,128]{1,0:T(8,128)S(1)}, f32[48,128]{1,0:T(8,128)S(1)}, u32[]{:S(2)}, u32[]{:S(2)}) collective-permute-start(f32[48,128]{1,0:T(8,128)S(1)} %shard_map.88.refs_0_), channel_id=1, source_target_pairs={{0,1},{1,2},{2,3},{3,0},{4,5},{5,6},{6,7},{7,4},{8,13},{9,14},{10,... | collective-permute-start | bytes 73736 | tf_op jit(solution)/shard_map/ppermute | solution.py:535
  165.6 1.6 collective-permute-start.9
  167.2 1.0 collective-permute-start.11
  167.9 4.5 %collective-permute-start.10 = (f32[48,128]{1,0:T(8,128)S(1)}, f32[48,128]{1,0:T(8,128)S(1)}, u32[]{:S(2)}, u32[]{:S(2)}) collective-permute-start(f32[48,128]{1,0:T(8,128)S(1)} %shard_map.90.refs_0_), channel_id=1, source_target_pairs={{0,16},{1,17},{2,18},{3,19},{4,20},{5,21},{6,22},{7,23},{8,40},{9,... | collective-permute-start | bytes 73736 | tf_op jit(solution)/shard_map/ppermute | solution.py:535
  172.3 4.0 %collective-permute-start.12 = (f32[48,128]{1,0:T(8,128)S(1)}, f32[48,128]{1,0:T(8,128)S(1)}, u32[]{:S(2)}, u32[]{:S(2)}) collective-permute-start(f32[48,128]{1,0:T(8,128)S(1)} %shard_map.91.refs_0_), channel_id=1, source_target_pairs={{0,8},{1,9},{2,10},{3,11},{4,12},{5,13},{6,14},{7,15},{8,0},{9,1},... | collective-permute-start | bytes 73736 | tf_op jit(solution)/shard_map/ppermute | solution.py:535
  176.3 1.2 collective-permute-start.14
  177.0 7.0 %collective-permute-start.13 = (f32[48,128]{1,0:T(8,128)S(1)}, f32[48,128]{1,0:T(8,128)S(1)}, u32[]{:S(2)}, u32[]{:S(2)}) collective-permute-start(f32[48,128]{1,0:T(8,128)S(1)} %shard_map.92.refs_0_), channel_id=1, source_target_pairs={{0,64},{1,65},{2,66},{3,67},{4,68},{5,69},{6,70},{7,71},{8,136},{9... | collective-permute-start | bytes 73736 | tf_op jit(solution)/shard_map/ppermute | solution.py:535
  183.9 2.2 %collective-permute-start.15 = (f32[48,128]{1,0:T(8,128)S(1)}, f32[48,128]{1,0:T(8,128)S(1)}, u32[]{:S(2)}, u32[]{:S(2)}) collective-permute-start(f32[48,128]{1,0:T(8,128)S(1)} %shard_map.93.refs_0_), channel_id=1, source_target_pairs={{0,8},{1,9},{2,10},{3,11},{4,12},{5,13},{6,14},{7,15},{8,0},{9,1},... | collective-permute-start | bytes 73736 | tf_op jit(solution)/shard_map/ppermute | solution.py:535

commit v5 on v4

--- a/solution.py
+++ b/solution.py
@@ -282,13 +282,11 @@
 
 
 def publish(sums_ref, out_ref):
-    ones = jnp.ones((8, 128), jnp.bfloat16)
-    row = None
-    for part in split_three(sums_ref[...]):
-        term = lax.dot_general(
-            ones, part, (((1,), (1,)), ((), ())), preferred_element_type=jnp.float32
-        )
-        row = term if row is None else row + term
+    shape = sums_ref.shape
+    total = jnp.broadcast_to(jnp.sum(sums_ref[...], axis=1, keepdims=True), shape)
+    index = lax.broadcasted_iota(jnp.int32, shape, 0)
+    picked = jnp.where(index == lax.broadcasted_iota(jnp.int32, shape, 1), total, 0.0)
+    row = jnp.broadcast_to(jnp.sum(picked, axis=0, keepdims=True), (8, 128))
     for j in range(0, out_ref.shape[0], 8):
         out_ref[j : j + 8, :] = row
 
@@ -386,7 +384,6 @@
 def first_kernel(before_ref, fields_ref, after_ref, cots_ref, area_ref, s_ref, v_ref, cot_ref, out_ref, sums):
     stream(Joined(before_ref, fields_ref, after_ref), s_ref)
     speeds(s_ref, v_ref)
-    sums[...] = jnp.zeros_like(sums)
     turbine_sums(area_ref, v_ref, sums, 0)
     publish(sums, out_ref)
     half = OWN_SPAN // 2
@@ -416,7 +413,6 @@
     chunks(one)
     stream(field, next_ref)
     speeds(next_ref, vn_ref)
-    sums[...] = jnp.zeros_like(sums)
     turbine_sums(area_ref, vn_ref, sums, 0)
     if last:
 
@@ -459,17 +455,21 @@
 
     chunks(other)
     if sends:
-        sums[...] = jnp.zeros_like(sums)
         turbine_sums(area_ref, drag_ref, sums, 0)
         publish(sums, rest[3])
 
 
 def last_kernel(s_ref, a_ref, area_ref, rotor_ref, point_ref, size_ref, inv_ref, out_ref, grad_ref, field, result, bar):
-    known, swing, slope = (
-        point_ref[NTURB * j : NTURB * (j + 1), :PTS] for j in range(3)
-    )
-    total = jnp.sum(size_ref[...] * swing, axis=1, keepdims=True)
-    grad_ref[...] = known + total * slope
+    known, swing, slope = (point_ref[NTURB * j : NTURB * (j + 1), :] for j in range(3))
+    total = jnp.sum(size_ref[...] * swing[:, :PTS], axis=1, keepdims=True)
+    grad = known + total * slope
+    turned = [grad] + [pltpu.roll(grad, 128 - PTS // 3 * j, 1) for j in (1, 2, 3)]
+    lane = lax.broadcasted_iota(jnp.int32, (1, 128), 1)
+    for m in range(NTURB // 4):
+        for j in range(3):
+            row = 4 * m + j
+            first, second = turned[j][row : row + 1], turned[j + 1][row + 1 : row + 2]
+            grad_ref[3 * m + j : 3 * m + j + 1, :] = jnp.where(lane < 128 - 32 * (j + 1), first, second)
     bar[...] = jnp.broadcast_to(total, (NTURB, 128)) * inv_ref[...]
     adjoint_field(s_ref, a_ref, area_ref, rotor_ref, bar, field)
     stream_adjoint(field, result)
@@ -636,15 +636,14 @@
     spots, cell_x, own_yz, area, inverse = ready
 
     s, v, rotor = [None] * 5, [None] * 5, [None] * 5
-    table = (128, 128)
     every = (count_x * count_y, 128)
-    s[1], v[1], cot, sums = call(first_kernel, [full, flat, full, every], [table], *parts, spots)
+    s[1], v[1], cot, sums = call(first_kernel, [full, flat, full, every], [row], *parts, spots)
     for k in (1, 2, 3):
         last = k == 3
         s[k + 1], v[k + 1], rotor[k], sums = call(
             functools.partial(forward_kernel, last),
             [full, flat, row, every],
-            [full, table] + ([flat] if last else []),
+            [full, (2 * NTURB, 128) if last else row] + ([flat] if last else []),
             *([s[k], v[k], spots, inverse, exchange(sums)] + ([cot] if last else [])),
         )
     adjoint = cot
@@ -655,7 +654,7 @@
         outs = call(
             functools.partial(backward_kernel, first, sends),
             [full, flat, row] + ([every] if sends else []) + ([row] if first else []),
-            [full, table],
+            [full, row],
             *(args + ([] if first else [rotor[k]])),
         )
         adjoint, drag[k - 1], bar[k] = outs[:3]
@@ -670,7 +669,7 @@
     )
     grad, grad_area = call(
         last_kernel,
-        [(19, CX, CY * NZ), (NTURB, PTS)],
+        [(19, CX, CY * NZ), (NTURB * PTS // 128, 128)],
         [full, full, row],
         *(s[1], adjoint, spots, rotor[1], spread(points), area, inverse),
     )

time: 189 us -> 188 us (level)
  no operation moved by 1% of the time
where the time goes in v5:
time: 188 us; the launch traced here: 187 us
  blocking collectives  122 us (65%)
  waiting for transfers between devices  27.4 us (15%)
  starting transfers between devices  20.6 us (11%)
  Pallas kernels  12.3 us (7%)
  local copies, waits for them, and re-layouts  3.61 us (2%)
    all_to_all x6, blocking collectives, exchange(): return lax.all_to_all(rows, ('gx', 'gy'), 0, 0, tiled=True)  122 us
    ppermute x12, waiting for transfers between devices, route(): return lax.ppermute(value, ('gx', 'gy'), pairs)  18.9 us
    ppermute x12, starting transfers between devices, route(): return lax.ppermute(value, ('gx', 'gy'), pairs)  13.1 us
    pallas_call x18, Pallas kernels, call(): pl.pallas_call(kernel, out_shape=[jax.ShapeDtypeStruct(shape, jnp.float32...  11.9 us
    ppermute x4, waiting for transfers between devices, shift(): lax.ppermute(value, axis, [(i, (i + step) % size) for i in range(size)])  8.56 us
    ppermute x4, starting transfers between devices, shift(): lax.ppermute(value, axis, [(i, (i + step) % size) for i in range(size)])  7.46 us
  transfers between devices with their start and end apart: 16, of which 9 were waited for; matrix products, arithmetic and copies ran while one was open for 0% of the time, Pallas kernels for 2%

profile of v5, /device:TPU:1, one launch (start us, length us, event | category | flops | bytes accessed | tf_op | source)
XLA Modules:
  0.0 187.4 jit_solution(16495964086813604122)
XLA Ops:
  2.9 2.7 %collective-permute-start = (f32[19,8,384]{2,1,0:T(8,128)S(1)}, f32[19,8,384]{2,1,0:T(8,128)S(1)}, u32[]{:S(2)}, u32[]{:S(2)}) collective-permute-start(f32[19,8,384]{2,1,0:T(8,128)S(1)} %get-tuple-element.45), channel_id=1, source_target_pairs={{0,8},{8,16},{16,24},{24,32},{32,40},{40,48},{48,56},{56,64},{64,7... | collective-permute-start | bytes 700424 | tf_op jit(solution)/shard_map/ppermute | solution.py:591
  8.3 2.9 %shard_map.78.area_ref = f32[16,24,512]{2,1,0:T(8,128)S(1)} custom-call(s32[16,96]{1,0:T(8,128)S(1)} %fusion.19.x_ref, s32[16,96]{1,0:T(8,128)S(1)} %get-tuple-element.89.yz_ref, f32[16,96]{1,0:T(8,128)S(1)} %reshape.65.area_ref.size_ref), custom_call_target="tpu_custom_call" | custom-call | tf_op jit(solution)/shard_map/pallas_call | solution.py:517
  11.5 1.2 collective-permute-start.2
  12.7 2.9 %collective-permute-start.3 = (f32[19,32,128]{2,1,0:T(8,128)S(1)}, f32[19,32,128]{2,1,0:T(8,128)S(1)}, u32[]{:S(2)}, u32[]{:S(2)}) collective-permute-start(f32[19,32,128]{2,1,0:T(8,128)S(1)} %get-tuple-element.51), channel_id=1, source_target_pairs={{0,7},{1,0},{2,1},{3,2},{4,3},{5,4},{6,5},{7,6},{8,15},{9,8},{10,9... | collective-permute-start | bytes 933896 | tf_op jit(solution)/shard_map/ppermute | solution.py:591
  15.6 8.6 %collective-permute-done.2.before_ref = f32[19,32,128]{2,1,0:T(8,128)S(1)} collective-permute-done((f32[19,32,128]{2,1,0:T(8,128)S(1)}, f32[19,32,128]{2,1,0:T(8,128)S(1)}, u32[]{:S(2)}, u32[]{:S(2)}) %collective-permute-start.2) | collective-permute-done | bytes 311328 | tf_op jit(solution)/shard_map/ppermute | solution.py:591
  24.6 29.3 %all_to_all.66 = f32[256,1,128]{2,1,0:T(1,128)S(1)} all-to-all(f32[256,1,128]{2,1,0:T(1,128)S(1)} %bitcast.31), channel_id=1, replica_groups=mesh['gx'=32,'gy'=8] {'gx','gy'}, dimensions={0} | all-to-all | bytes 262144 | tf_op jit(solution)/shard_map/all_to_all | solution.py:543
  54.7 18.6 %all_to_all.67 = f32[256,1,128]{2,1,0:T(1,128)S(1)} all-to-all(f32[256,1,128]{2,1,0:T(1,128)S(1)} %bitcast.34), channel_id=1, replica_groups=mesh['gx'=32,'gy'=8] {'gx','gy'}, dimensions={0} | all-to-all | bytes 262144 | tf_op jit(solution)/shard_map/all_to_all | solution.py:543
  74.2 18.6 %all_to_all.68 = f32[256,1,128]{2,1,0:T(1,128)S(1)} all-to-all(f32[256,1,128]{2,1,0:T(1,128)S(1)} %bitcast.35), channel_id=1, replica_groups=mesh['gx'=32,'gy'=8] {'gx','gy'}, dimensions={0} | all-to-all | bytes 262144 | tf_op jit(solution)/shard_map/all_to_all | solution.py:543
  93.7 18.8 %all_to_all.69 = f32[256,1,128]{2,1,0:T(1,128)S(1)} all-to-all(f32[256,1,128]{2,1,0:T(1,128)S(1)} %bitcast.36), channel_id=1, replica_groups=mesh['gx'=32,'gy'=8] {'gx','gy'}, dimensions={0} | all-to-all | bytes 262144 | tf_op jit(solution)/shard_map/all_to_all | solution.py:543
  112.5 1.2 shard_map.84
  113.7 18.6 %all_to_all.70 = f32[256,1,128]{2,1,0:T(1,128)S(1)} all-to-all(f32[256,1,128]{2,1,0:T(1,128)S(1)} %bitcast.32), channel_id=1, replica_groups=mesh['gx'=32,'gy'=8] {'gx','gy'}, dimensions={0} | all-to-all | bytes 262144 | tf_op jit(solution)/shard_map/all_to_all | solution.py:543
  132.3 1.2 shard_map.85
  133.5 18.6 %all_to_all.71 = f32[256,1,128]{2,1,0:T(1,128)S(1)} all-to-all(f32[256,1,128]{2,1,0:T(1,128)S(1)} %bitcast.33), channel_id=1, replica_groups=mesh['gx'=32,'gy'=8] {'gx','gy'}, dimensions={0} | all-to-all | bytes 262144 | tf_op jit(solution)/shard_map/all_to_all | solution.py:543
  152.1 1.2 shard_map.86
  153.8 1.2 collective-permute-start.4
  156.7 1.1 collective-permute-start.7
  157.8 2.6 %collective-permute-start.6 = (f32[48,128]{1,0:T(8,128)S(1)}, f32[48,128]{1,0:T(8,128)S(1)}, u32[]{:S(2)}, u32[]{:S(2)}) collective-permute-start(f32[48,128]{1,0:T(8,128)S(1)} %shard_map.88.refs_0_), channel_id=1, source_target_pairs={{0,3},{1,0},{2,1},{3,2},{4,7},{5,4},{6,5},{7,6},{8,15},{9,12},{10,... | collective-permute-start | bytes 73736 | tf_op jit(solution)/shard_map/ppermute | solution.py:535
  160.4 1.4 collective-permute-done.7.refs_3_
  161.8 3.5 %collective-permute-done.5.refs_1_ = f32[48,128]{1,0:T(8,128)S(1)} collective-permute-done((f32[48,128]{1,0:T(8,128)S(1)}, f32[48,128]{1,0:T(8,128)S(1)}, u32[]{:S(2)}, u32[]{:S(2)}) %collective-permute-start.5) | collective-permute-done | bytes 24608 | tf_op jit(solution)/shard_map/ppermute | solution.py:535
  167.9 4.2 %collective-permute-done.10.refs_1_ = f32[48,128]{1,0:T(8,128)S(1)} collective-permute-done((f32[48,128]{1,0:T(8,128)S(1)}, f32[48,128]{1,0:T(8,128)S(1)}, u32[]{:S(2)}, u32[]{:S(2)}) %collective-permute-start.10) | collective-permute-done | bytes 24608 | tf_op jit(solution)/shard_map/ppermute | solution.py:535
  172.1 3.1 %collective-permute-start.12 = (f32[48,128]{1,0:T(8,128)S(1)}, f32[48,128]{1,0:T(8,128)S(1)}, u32[]{:S(2)}, u32[]{:S(2)}) collective-permute-start(f32[48,128]{1,0:T(8,128)S(1)} %shard_map.91.refs_0_), channel_id=1, source_target_pairs={{0,8},{1,9},{2,10},{3,11},{4,12},{5,13},{6,14},{7,15},{8,0},{9,1},... | collective-permute-start | bytes 73736 | tf_op jit(solution)/shard_map/ppermute | solution.py:535
  177.3 6.4 %collective-permute-done.13.refs_1_ = f32[48,128]{1,0:T(8,128)S(1)} collective-permute-done((f32[48,128]{1,0:T(8,128)S(1)}, f32[48,128]{1,0:T(8,128)S(1)}, u32[]{:S(2)}, u32[]{:S(2)}) %collective-permute-start.13) | collective-permute-done | bytes 24608 | tf_op jit(solution)/shard_map/ppermute | solution.py:535
  183.7 1.3 collective-permute-start.15
  185.9 1.6 shard_map.95
  (62 shorter events, 16.0 us)
Async XLA Ops:
  0.6 0.9 copy-start
  1.5 0.9 copy-start.2
  2.5 3.8 %copy-start.4 = (s32[1536]{0:T(1024)S(1)}, s32[1536]{0:T(1024)}, u32[]{:S(2)}) copy-start(s32[1536]{0:T(1024)} %param.10) | copy-start | bytes 18436
  2.9 8.4 %collective-permute-start = (f32[19,8,384]{2,1,0:T(8,128)S(1)}, f32[19,8,384]{2,1,0:T(8,128)S(1)}, u32[]{:S(2)}, u32[]{:S(2)}) collective-permute-start(f32[19,8,384]{2,1,0:T(8,128)S(1)} %get-tuple-element.45), channel_id=1, source_target_pairs={{0,8},{8,16},{16,24},{24,32},{32,40},{40,48},{48,56},{56,64},{64,7... | collective-permute-start | bytes 700424 | tf_op jit(solution)/shard_map/ppermute | solution.py:591
  5.6 5.7 %collective-permute-start.1 = (f32[19,8,384]{2,1,0:T(8,128)S(1)}, f32[19,8,384]{2,1,0:T(8,128)S(1)}, u32[]{:S(2)}, u32[]{:S(2)}) collective-permute-start(f32[19,8,384]{2,1,0:T(8,128)S(1)} %get-tuple-element.46), channel_id=1, source_target_pairs={{0,248},{8,0},{16,8},{24,16},{32,24},{40,32},{48,40},{56,48},{64,5... | collective-permute-start | bytes 700424 | tf_op jit(solution)/shard_map/ppermute | solution.py:591
  6.3 0.8 copy-start.5
  6.3 0.7 copy-start.7
  7.4 0.7 copy-start.6
  8.3 3.0 %copy-start.1 = (f32[19,8,256]{2,1,0:T(8,128)S(1)}, f32[19,8,256]{2,1,0:T(8,128)}, u32[]{:S(2)}) copy-start(f32[19,8,256]{2,1,0:T(8,128)} %field_ref.1) | copy-start | bytes 466948
  8.3 3.0 %copy-start.3 = (f32[19,8,256]{2,1,0:T(8,128)S(1)}, f32[19,8,256]{2,1,0:T(8,128)}, u32[]{:S(2)}) copy-start(f32[19,8,256]{2,1,0:T(8,128)} %cot_ref.1) | copy-start | bytes 466948
  11.5 12.6 %collective-permute-start.2 = (f32[19,32,128]{2,1,0:T(8,128)S(1)}, f32[19,32,128]{2,1,0:T(8,128)S(1)}, u32[]{:S(2)}, u32[]{:S(2)}) collective-permute-start(f32[19,32,128]{2,1,0:T(8,128)S(1)} %get-tuple-element.49), channel_id=1, source_target_pairs={{0,1},{1,2},{2,3},{3,4},{4,5},{5,6},{6,7},{7,0},{8,9},{9,10},{10,1... | collective-permute-start | bytes 933896 | tf_op jit(solution)/shard_map/ppermute | solution.py:591
  12.7 11.4 %collective-permute-start.3 = (f32[19,32,128]{2,1,0:T(8,128)S(1)}, f32[19,32,128]{2,1,0:T(8,128)S(1)}, u32[]{:S(2)}, u32[]{:S(2)}) collective-permute-start(f32[19,32,128]{2,1,0:T(8,128)S(1)} %get-tuple-element.51), channel_id=1, source_target_pairs={{0,7},{1,0},{2,1},{3,2},{4,3},{5,4},{6,5},{7,6},{8,15},{9,8},{10,9... | collective-permute-start | bytes 933896 | tf_op jit(solution)/shard_map/ppermute | solution.py:591
  153.8 2.1 %collective-permute-start.4 = (f32[48,128]{1,0:T(8,128)S(1)}, f32[48,128]{1,0:T(8,128)S(1)}, u32[]{:S(2)}, u32[]{:S(2)}) collective-permute-start(f32[48,128]{1,0:T(8,128)S(1)} %shard_map.87.refs_0_), channel_id=1, source_target_pairs={{0,8},{1,9},{2,10},{3,11},{4,12},{5,13},{6,14},{7,15},{8,0},{9,1},... | collective-permute-start | bytes 73736 | tf_op jit(solution)/shard_map/ppermute | solution.py:535
  155.9 4.5 %collective-permute-start.8 = (f32[48,128]{1,0:T(8,128)S(1)}, f32[48,128]{1,0:T(8,128)S(1)}, u32[]{:S(2)}, u32[]{:S(2)}) collective-permute-start(f32[48,128]{1,0:T(8,128)S(1)} %shard_map.88.refs_0_), channel_id=1, source_target_pairs={{0,4},{1,5},{2,6},{3,7},{4,0},{5,1},{6,2},{7,3},{8,12},{9,13},{10,... | collective-permute-start | bytes 73736 | tf_op jit(solution)/shard_map/ppermute | solution.py:535
  156.7 5.1 %collective-permute-start.7 = (f32[48,128]{1,0:T(8,128)S(1)}, f32[48,128]{1,0:T(8,128)S(1)}, u32[]{:S(2)}, u32[]{:S(2)}) collective-permute-start(f32[48,128]{1,0:T(8,128)S(1)} %shard_map.88.refs_0_), channel_id=1, source_target_pairs={{0,2},{1,3},{2,0},{3,1},{4,6},{5,7},{6,4},{7,5},{8,14},{9,15},{10,... | collective-permute-start | bytes 73736 | tf_op jit(solution)/shard_map/ppermute | solution.py:535
  157.8 4.0 %collective-permute-start.6 = (f32[48,128]{1,0:T(8,128)S(1)}, f32[48,128]{1,0:T(8,128)S(1)}, u32[]{:S(2)}, u32[]{:S(2)}) collective-permute-start(f32[48,128]{1,0:T(8,128)S(1)} %shard_map.88.refs_0_), channel_id=1, source_target_pairs={{0,3},{1,0},{2,1},{3,2},{4,7},{5,4},{6,5},{7,6},{8,15},{9,12},{10,... | collective-permute-start | bytes 73736 | tf_op jit(solution)/shard_map/ppermute | solution.py:535
  160.4 4.9 %collective-permute-start.5 = (f32[48,128]{1,0:T(8,128)S(1)}, f32[48,128]{1,0:T(8,128)S(1)}, u32[]{:S(2)}, u32[]{:S(2)}) collective-permute-start(f32[48,128]{1,0:T(8,128)S(1)} %shard_map.88.refs_0_), channel_id=1, source_target_pairs={{0,1},{1,2},{2,3},{3,0},{4,5},{5,6},{6,7},{7,4},{8,13},{9,14},{10,... | collective-permute-start | bytes 73736 | tf_op jit(solution)/shard_map/ppermute | solution.py:535
  165.3 1.6 collective-permute-start.9
  166.9 1.0 collective-permute-start.11
  167.6 4.5 %collective-permute-start.10 = (f32[48,128]{1,0:T(8,128)S(1)}, f32[48,128]{1,0:T(8,128)S(1)}, u32[]{:S(2)}, u32[]{:S(2)}) collective-permute-start(f32[48,128]{1,0:T(8,128)S(1)} %shard_map.90.refs_0_), channel_id=1, source_target_pairs={{0,16},{1,17},{2,18},{3,19},{4,20},{5,21},{6,22},{7,23},{8,40},{9,... | collective-permute-start | bytes 73736 | tf_op jit(solution)/shard_map/ppermute | solution.py:535
  172.1 4.0 %collective-permute-start.12 = (f32[48,128]{1,0:T(8,128)S(1)}, f32[48,128]{1,0:T(8,128)S(1)}, u32[]{:S(2)}, u32[]{:S(2)}) collective-permute-start(f32[48,128]{1,0:T(8,128)S(1)} %shard_map.91.refs_0_), channel_id=1, source_target_pairs={{0,8},{1,9},{2,10},{3,11},{4,12},{5,13},{6,14},{7,15},{8,0},{9,1},... | collective-permute-start | bytes 73736 | tf_op jit(solution)/shard_map/ppermute | solution.py:535
  176.1 1.2 collective-permute-start.14
  176.7 7.0 %collective-permute-start.13 = (f32[48,128]{1,0:T(8,128)S(1)}, f32[48,128]{1,0:T(8,128)S(1)}, u32[]{:S(2)}, u32[]{:S(2)}) collective-permute-start(f32[48,128]{1,0:T(8,128)S(1)} %shard_map.92.refs_0_), channel_id=1, source_target_pairs={{0,64},{1,65},{2,66},{3,67},{4,68},{5,69},{6,70},{7,71},{8,136},{9... | collective-permute-start | bytes 73736 | tf_op jit(solution)/shard_map/ppermute | solution.py:535
  183.7 2.2 %collective-permute-start.15 = (f32[48,128]{1,0:T(8,128)S(1)}, f32[48,128]{1,0:T(8,128)S(1)}, u32[]{:S(2)}, u32[]{:S(2)}) collective-permute-start(f32[48,128]{1,0:T(8,128)S(1)} %shard_map.93.refs_0_), channel_id=1, source_target_pairs={{0,8},{1,9},{2,10},{3,11},{4,12},{5,13},{6,14},{7,15},{8,0},{9,1},... | collective-permute-start | bytes 73736 | tf_op jit(solution)/shard_map/ppermute | solution.py:535

commit v6 on v5

--- a/solution.py
+++ b/solution.py
@@ -599,7 +599,7 @@
         in_specs=[pl.BlockSpec(memory_space=pltpu.HBM)] * 2,
         out_specs=[pl.BlockSpec(memory_space=pltpu.VMEM)] * 2,
         scratch_shapes=[pltpu.VMEM(checkpoint.shape, jnp.float32)] * 2 + [pltpu.SemaphoreType.DMA((2,))],
-        compiler_params=pltpu.CompilerParams(vmem_limit_bytes=VMEM_LIMIT),
+        compiler_params=pltpu.CompilerParams(vmem_limit_bytes=60 * 1024 * 1024),
     )(checkpoint, cotangent)
     before, after = shift(right, "gx", 1), shift(left, "gx", -1)
     before, after, *ready = lax.optimization_barrier((before, after) + ready)

time: 188 us -> 187 us (level)
  no operation moved by 1% of the time
where the time goes in v6:
time: 187 us
  blocking collectives  122 us (65%)
  waiting for transfers between devices  27.4 us (15%)
  starting transfers between devices  20.6 us (11%)
  Pallas kernels  13.7 us (7%)
    all_to_all x6, blocking collectives, exchange(): return lax.all_to_all(rows, ('gx', 'gy'), 0, 0, tiled=True)  122 us
    ppermute x12, waiting for transfers between devices, route(): return lax.ppermute(value, ('gx', 'gy'), pairs)  18.9 us
    ppermute x12, starting transfers between devices, route(): return lax.ppermute(value, ('gx', 'gy'), pairs)  12.9 us
    pallas_call x18, Pallas kernels, call(): pl.pallas_call(kernel, out_shape=[jax.ShapeDtypeStruct(shape, jnp.float32...  11.8 us
    ppermute x4, waiting for transfers between devices, shift(): lax.ppermute(value, axis, [(i, (i + step) % size) for i in range(size)])  8.58 us
    ppermute x4, starting transfers between devices, shift(): lax.ppermute(value, axis, [(i, (i + step) % size) for i in range(size)])  7.66 us
  transfers between devices with their start and end apart: 16, of which 9 were waited for; matrix products, arithmetic and copies ran while one was open for 0% of the time, Pallas kernels for 2%

profile of v6, /device:TPU:1, one launch (start us, length us, event | category | flops | bytes accessed | tf_op | source)
XLA Modules:
  0.0 187.0 jit_solution(7423019519200870630)
XLA Ops:
  0.6 1.8 shard_map.77
  2.5 2.7 %collective-permute-start = (f32[19,8,384]{2,1,0:T(8,128)}, f32[19,8,384]{2,1,0:T(8,128)S(1)}, u32[]{:S(2)}, u32[]{:S(2)}) collective-permute-start(f32[19,8,384]{2,1,0:T(8,128)} %get-tuple-element.45), channel_id=1, source_target_pairs={{0,8},{8,16},{16,24},{24,32},{32,40},{40,48},{48,56},{56,64},{64,7... | collective-permute-start | bytes 700424 | tf_op jit(solution)/shard_map/ppermute | solution.py:591
  7.9 2.9 %shard_map.78.area_ref = f32[16,24,512]{2,1,0:T(8,128)S(1)} custom-call(s32[16,96]{1,0:T(8,128)S(1)} %fusion.19.x_ref, s32[16,96]{1,0:T(8,128)S(1)} %get-tuple-element.89.yz_ref, f32[16,96]{1,0:T(8,128)S(1)} %reshape.65.area_ref.size_ref), custom_call_target="tpu_custom_call" | custom-call | tf_op jit(solution)/shard_map/pallas_call | solution.py:517
  11.1 1.4 collective-permute-start.2
  12.5 2.9 %collective-permute-start.3 = (f32[19,32,128]{2,1,0:T(8,128)S(1)}, f32[19,32,128]{2,1,0:T(8,128)S(1)}, u32[]{:S(2)}, u32[]{:S(2)}) collective-permute-start(f32[19,32,128]{2,1,0:T(8,128)S(1)} %get-tuple-element.51), channel_id=1, source_target_pairs={{0,7},{1,0},{2,1},{3,2},{4,3},{5,4},{6,5},{7,6},{8,15},{9,8},{10,9... | collective-permute-start | bytes 933896 | tf_op jit(solution)/shard_map/ppermute | solution.py:591
  15.4 8.6 %collective-permute-done.2.before_ref = f32[19,32,128]{2,1,0:T(8,128)S(1)} collective-permute-done((f32[19,32,128]{2,1,0:T(8,128)S(1)}, f32[19,32,128]{2,1,0:T(8,128)S(1)}, u32[]{:S(2)}, u32[]{:S(2)}) %collective-permute-start.2) | collective-permute-done | bytes 311328 | tf_op jit(solution)/shard_map/ppermute | solution.py:591
  24.3 29.3 %all_to_all.66 = f32[256,1,128]{2,1,0:T(1,128)S(1)} all-to-all(f32[256,1,128]{2,1,0:T(1,128)S(1)} %bitcast.31), channel_id=1, replica_groups=mesh['gx'=32,'gy'=8] {'gx','gy'}, dimensions={0} | all-to-all | bytes 262144 | tf_op jit(solution)/shard_map/all_to_all | solution.py:543
  54.5 18.6 %all_to_all.67 = f32[256,1,128]{2,1,0:T(1,128)S(1)} all-to-all(f32[256,1,128]{2,1,0:T(1,128)S(1)} %bitcast.34), channel_id=1, replica_groups=mesh['gx'=32,'gy'=8] {'gx','gy'}, dimensions={0} | all-to-all | bytes 262144 | tf_op jit(solution)/shard_map/all_to_all | solution.py:543
  74.0 18.6 %all_to_all.68 = f32[256,1,128]{2,1,0:T(1,128)S(1)} all-to-all(f32[256,1,128]{2,1,0:T(1,128)S(1)} %bitcast.35), channel_id=1, replica_groups=mesh['gx'=32,'gy'=8] {'gx','gy'}, dimensions={0} | all-to-all | bytes 262144 | tf_op jit(solution)/shard_map/all_to_all | solution.py:543
  93.5 18.8 %all_to_all.69 = f32[256,1,128]{2,1,0:T(1,128)S(1)} all-to-all(f32[256,1,128]{2,1,0:T(1,128)S(1)} %bitcast.36), channel_id=1, replica_groups=mesh['gx'=32,'gy'=8] {'gx','gy'}, dimensions={0} | all-to-all | bytes 262144 | tf_op jit(solution)/shard_map/all_to_all | solution.py:543
  112.3 1.2 shard_map.84
  113.5 18.6 %all_to_all.70 = f32[256,1,128]{2,1,0:T(1,128)S(1)} all-to-all(f32[256,1,128]{2,1,0:T(1,128)S(1)} %bitcast.32), channel_id=1, replica_groups=mesh['gx'=32,'gy'=8] {'gx','gy'}, dimensions={0} | all-to-all | bytes 262144 | tf_op jit(solution)/shard_map/all_to_all | solution.py:543
  132.1 1.2 shard_map.85
  133.3 18.6 %all_to_all.71 = f32[256,1,128]{2,1,0:T(1,128)S(1)} all-to-all(f32[256,1,128]{2,1,0:T(1,128)S(1)} %bitcast.33), channel_id=1, replica_groups=mesh['gx'=32,'gy'=8] {'gx','gy'}, dimensions={0} | all-to-all | bytes 262144 | tf_op jit(solution)/shard_map/all_to_all | solution.py:543
  151.9 1.2 shard_map.86
  153.6 1.2 collective-permute-start.4
  157.6 2.6 %collective-permute-start.6 = (f32[48,128]{1,0:T(8,128)S(1)}, f32[48,128]{1,0:T(8,128)S(1)}, u32[]{:S(2)}, u32[]{:S(2)}) collective-permute-start(f32[48,128]{1,0:T(8,128)S(1)} %shard_map.88.refs_0_), channel_id=1, source_target_pairs={{0,3},{1,0},{2,1},{3,2},{4,7},{5,4},{6,5},{7,6},{8,15},{9,12},{10,... | collective-permute-start | bytes 73736 | tf_op jit(solution)/shard_map/ppermute | solution.py:535
  160.2 1.4 collective-permute-done.7.refs_3_
  161.6 3.5 %collective-permute-done.5.refs_1_ = f32[48,128]{1,0:T(8,128)S(1)} collective-permute-done((f32[48,128]{1,0:T(8,128)S(1)}, f32[48,128]{1,0:T(8,128)S(1)}, u32[]{:S(2)}, u32[]{:S(2)}) %collective-permute-start.5) | collective-permute-done | bytes 24608 | tf_op jit(solution)/shard_map/ppermute | solution.py:535
  167.5 4.2 %collective-permute-done.10.refs_1_ = f32[48,128]{1,0:T(8,128)S(1)} collective-permute-done((f32[48,128]{1,0:T(8,128)S(1)}, f32[48,128]{1,0:T(8,128)S(1)}, u32[]{:S(2)}, u32[]{:S(2)}) %collective-permute-start.10) | collective-permute-done | bytes 24608 | tf_op jit(solution)/shard_map/ppermute | solution.py:535
  171.6 3.1 %collective-permute-start.12 = (f32[48,128]{1,0:T(8,128)S(1)}, f32[48,128]{1,0:T(8,128)S(1)}, u32[]{:S(2)}, u32[]{:S(2)}) collective-permute-start(f32[48,128]{1,0:T(8,128)S(1)} %shard_map.91.refs_0_), channel_id=1, source_target_pairs={{0,8},{1,9},{2,10},{3,11},{4,12},{5,13},{6,14},{7,15},{8,0},{9,1},... | collective-permute-start | bytes 73736 | tf_op jit(solution)/shard_map/ppermute | solution.py:535
  176.8 6.4 %collective-permute-done.13.refs_1_ = f32[48,128]{1,0:T(8,128)S(1)} collective-permute-done((f32[48,128]{1,0:T(8,128)S(1)}, f32[48,128]{1,0:T(8,128)S(1)}, u32[]{:S(2)}, u32[]{:S(2)}) %collective-permute-start.13) | collective-permute-done | bytes 24608 | tf_op jit(solution)/shard_map/ppermute | solution.py:535
  183.3 1.3 collective-permute-start.15
  185.4 1.6 shard_map.95
  (58 shorter events, 14.7 us)
Async XLA Ops:
  0.6 5.2 %copy-start.2 = (s32[1536]{0:T(1024)S(1)}, s32[1536]{0:T(1024)}, u32[]{:S(2)}) copy-start(s32[1536]{0:T(1024)} %param.10) | copy-start | bytes 18436
  2.5 8.4 %collective-permute-start = (f32[19,8,384]{2,1,0:T(8,128)}, f32[19,8,384]{2,1,0:T(8,128)S(1)}, u32[]{:S(2)}, u32[]{:S(2)}) collective-permute-start(f32[19,8,384]{2,1,0:T(8,128)} %get-tuple-element.45), channel_id=1, source_target_pairs={{0,8},{8,16},{16,24},{24,32},{32,40},{40,48},{48,56},{56,64},{64,7... | collective-permute-start | bytes 700424 | tf_op jit(solution)/shard_map/ppermute | solution.py:591
  5.1 5.7 %collective-permute-start.1 = (f32[19,8,384]{2,1,0:T(8,128)}, f32[19,8,384]{2,1,0:T(8,128)S(1)}, u32[]{:S(2)}, u32[]{:S(2)}) collective-permute-start(f32[19,8,384]{2,1,0:T(8,128)} %get-tuple-element.46), channel_id=1, source_target_pairs={{0,248},{8,0},{16,8},{24,16},{32,24},{40,32},{48,40},{56,48},{64,5... | collective-permute-start | bytes 700424 | tf_op jit(solution)/shard_map/ppermute | solution.py:591
  5.9 0.8 copy-start.3
  5.9 0.7 copy-start.5
  7.0 0.7 copy-start.4
  7.9 3.0 %copy-start = (f32[19,8,256]{2,1,0:T(8,128)S(1)}, f32[19,8,256]{2,1,0:T(8,128)}, u32[]{:S(2)}) copy-start(f32[19,8,256]{2,1,0:T(8,128)} %field_ref.1) | copy-start | bytes 466948
  7.9 3.0 %copy-start.1 = (f32[19,8,256]{2,1,0:T(8,128)S(1)}, f32[19,8,256]{2,1,0:T(8,128)}, u32[]{:S(2)}) copy-start(f32[19,8,256]{2,1,0:T(8,128)} %cot_ref.1) | copy-start | bytes 466948
  11.1 12.8 %collective-permute-start.2 = (f32[19,32,128]{2,1,0:T(8,128)S(1)}, f32[19,32,128]{2,1,0:T(8,128)S(1)}, u32[]{:S(2)}, u32[]{:S(2)}) collective-permute-start(f32[19,32,128]{2,1,0:T(8,128)S(1)} %get-tuple-element.49), channel_id=1, source_target_pairs={{0,1},{1,2},{2,3},{3,4},{4,5},{5,6},{6,7},{7,0},{8,9},{9,10},{10,1... | collective-permute-start | bytes 933896 | tf_op jit(solution)/shard_map/ppermute | solution.py:591
  12.5 11.4 %collective-permute-start.3 = (f32[19,32,128]{2,1,0:T(8,128)S(1)}, f32[19,32,128]{2,1,0:T(8,128)S(1)}, u32[]{:S(2)}, u32[]{:S(2)}) collective-permute-start(f32[19,32,128]{2,1,0:T(8,128)S(1)} %get-tuple-element.51), channel_id=1, source_target_pairs={{0,7},{1,0},{2,1},{3,2},{4,3},{5,4},{6,5},{7,6},{8,15},{9,8},{10,9... | collective-permute-start | bytes 933896 | tf_op jit(solution)/shard_map/ppermute | solution.py:591
  153.6 2.1 %collective-permute-start.4 = (f32[48,128]{1,0:T(8,128)S(1)}, f32[48,128]{1,0:T(8,128)S(1)}, u32[]{:S(2)}, u32[]{:S(2)}) collective-permute-start(f32[48,128]{1,0:T(8,128)S(1)} %shard_map.87.refs_0_), channel_id=1, source_target_pairs={{0,8},{1,9},{2,10},{3,11},{4,12},{5,13},{6,14},{7,15},{8,0},{9,1},... | collective-permute-start | bytes 73736 | tf_op jit(solution)/shard_map/ppermute | solution.py:535
  155.7 4.5 %collective-permute-start.8 = (f32[48,128]{1,0:T(8,128)S(1)}, f32[48,128]{1,0:T(8,128)S(1)}, u32[]{:S(2)}, u32[]{:S(2)}) collective-permute-start(f32[48,128]{1,0:T(8,128)S(1)} %shard_map.88.refs_0_), channel_id=1, source_target_pairs={{0,4},{1,5},{2,6},{3,7},{4,0},{5,1},{6,2},{7,3},{8,12},{9,13},{10,... | collective-permute-start | bytes 73736 | tf_op jit(solution)/shard_map/ppermute | solution.py:535
  156.5 5.1 %collective-permute-start.7 = (f32[48,128]{1,0:T(8,128)S(1)}, f32[48,128]{1,0:T(8,128)S(1)}, u32[]{:S(2)}, u32[]{:S(2)}) collective-permute-start(f32[48,128]{1,0:T(8,128)S(1)} %shard_map.88.refs_0_), channel_id=1, source_target_pairs={{0,2},{1,3},{2,0},{3,1},{4,6},{5,7},{6,4},{7,5},{8,14},{9,15},{10,... | collective-permute-start | bytes 73736 | tf_op jit(solution)/shard_map/ppermute | solution.py:535
  157.6 4.0 %collective-permute-start.6 = (f32[48,128]{1,0:T(8,128)S(1)}, f32[48,128]{1,0:T(8,128)S(1)}, u32[]{:S(2)}, u32[]{:S(2)}) collective-permute-start(f32[48,128]{1,0:T(8,128)S(1)} %shard_map.88.refs_0_), channel_id=1, source_target_pairs={{0,3},{1,0},{2,1},{3,2},{4,7},{5,4},{6,5},{7,6},{8,15},{9,12},{10,... | collective-permute-start | bytes 73736 | tf_op jit(solution)/shard_map/ppermute | solution.py:535
  160.2 4.9 %collective-permute-start.5 = (f32[48,128]{1,0:T(8,128)S(1)}, f32[48,128]{1,0:T(8,128)S(1)}, u32[]{:S(2)}, u32[]{:S(2)}) collective-permute-start(f32[48,128]{1,0:T(8,128)S(1)} %shard_map.88.refs_0_), channel_id=1, source_target_pairs={{0,1},{1,2},{2,3},{3,0},{4,5},{5,6},{6,7},{7,4},{8,13},{9,14},{10,... | collective-permute-start | bytes 73736 | tf_op jit(solution)/shard_map/ppermute | solution.py:535
  165.1 1.6 collective-permute-start.9
  166.7 0.8 collective-permute-start.11
  167.4 4.3 %collective-permute-start.10 = (f32[48,128]{1,0:T(8,128)S(1)}, f32[48,128]{1,0:T(8,128)S(1)}, u32[]{:S(2)}, u32[]{:S(2)}) collective-permute-start(f32[48,128]{1,0:T(8,128)S(1)} %shard_map.90.refs_0_), channel_id=1, source_target_pairs={{0,16},{1,17},{2,18},{3,19},{4,20},{5,21},{6,22},{7,23},{8,40},{9,... | collective-permute-start | bytes 73736 | tf_op jit(solution)/shard_map/ppermute | solution.py:535
  171.6 4.0 %collective-permute-start.12 = (f32[48,128]{1,0:T(8,128)S(1)}, f32[48,128]{1,0:T(8,128)S(1)}, u32[]{:S(2)}, u32[]{:S(2)}) collective-permute-start(f32[48,128]{1,0:T(8,128)S(1)} %shard_map.91.refs_0_), channel_id=1, source_target_pairs={{0,8},{1,9},{2,10},{3,11},{4,12},{5,13},{6,14},{7,15},{8,0},{9,1},... | collective-permute-start | bytes 73736 | tf_op jit(solution)/shard_map/ppermute | solution.py:535
  175.6 1.2 collective-permute-start.14
  176.3 7.0 %collective-permute-start.13 = (f32[48,128]{1,0:T(8,128)S(1)}, f32[48,128]{1,0:T(8,128)S(1)}, u32[]{:S(2)}, u32[]{:S(2)}) collective-permute-start(f32[48,128]{1,0:T(8,128)S(1)} %shard_map.92.refs_0_), channel_id=1, source_target_pairs={{0,64},{1,65},{2,66},{3,67},{4,68},{5,69},{6,70},{7,71},{8,136},{9... | collective-permute-start | bytes 73736 | tf_op jit(solution)/shard_map/ppermute | solution.py:535
  183.3 2.2 %collective-permute-start.15 = (f32[48,128]{1,0:T(8,128)S(1)}, f32[48,128]{1,0:T(8,128)S(1)}, u32[]{:S(2)}, u32[]{:S(2)}) collective-permute-start(f32[48,128]{1,0:T(8,128)S(1)} %shard_map.93.refs_0_), channel_id=1, source_target_pairs={{0,8},{1,9},{2,10},{3,11},{4,12},{5,13},{6,14},{7,15},{8,0},{9,1},... | collective-permute-start | bytes 73736 | tf_op jit(solution)/shard_map/ppermute | solution.py:535
